TPU v7x, 32 devices: a whole 2x2x4 slice. The times are simulated.
32 devices in a mesh: lat: 4 (over y, core), lon: 8 (over z, x).
Axes of the slice: x: 2, y: 2, z: 4, core: 2. Of those that a mesh axis runs over, the one named last changes fastest.
Arguments:
- background: bfloat16 [256, 512, 128], P('lat', 'lon'), may hold values from -6 to 6
- diffusivity: float32 [256, 512, 128], P('lat', 'lon'), may hold values from 0.12 to 0.245
- tile_index: int32 [16384, 1], P(('lat', 'lon')), may hold values from 0 to 31; in each aligned block of 512 rows (0 to 511, 512 to 1023, ...) at most 32 rows name the same one
- anchor: int32 [16384], P(('lat', 'lon')), may hold values from 0 to 3968
- weights: float32 [16384, 4], P(('lat', 'lon')), may hold values from 0.2 to 1
- observed: float32 [16384, 128], P(('lat', 'lon')), may hold values from -6 to 6
- accept: int32 [16384, 128], P(('lat', 'lon')), may hold values 0 or 1
- absorb: float32 [128, 128], replicated, may hold values from 0.001 to 0.1
- sensitivity: float32 [128], replicated, may hold values from -0.5 to 0.5
- inverse_variance: float32 [128], replicated, may hold values from 0.25 to 4
Outputs:
- departure: float32 [16384, 128], P(('lat', 'lon'))
- increment: float32 [256, 512, 128], P('lat', 'lon')
Inputs may be any that keep to these rules, and one draw needn't show every extreme that they name: `tile_index`: among the 512 footprints of one device no tile is named more than 32 times, a bound that some block reaches.
All inputs are finite; a program needn't handle non-finite values. No bound on the sum of `accept` on one device may be relied on, other than what follows from the above.
Results may differ from a plain program's by a relative error of at most 0.0003.
Values may be sent and summed in bfloat16 or wider, within the bound.
No kernel may reach another device: no remote copies, remote signals or barrier semaphores. Data moves between devices by JAX's collectives and lax.ppermute only.
A program may use at most 64 MiB of HBM per device.

v0:
```python
import functools
import math

import jax
import jax.numpy as jnp
from jax import lax
from jax.experimental import pallas as pl
from jax.experimental.pallas import tpu as pltpu
from jax.sharding import PartitionSpec as P


STEPS = 8
REJECTED = 64.0
META = 8
LOG2E = math.log2(math.e)
LN2 = math.log(2.0)
MIB = 1024 * 1024
UNROLL = 16


def thirds(x):
    high = x.astype(jnp.bfloat16)
    rest = x - high.astype(jnp.float32)
    mid = rest.astype(jnp.bfloat16)
    low = (rest - mid.astype(jnp.float32)).astype(jnp.bfloat16)
    return high, mid, low


def dot_f32(a, b, contract):
    return lax.dot_general(a, b, (contract, ((), ())), preferred_element_type=jnp.float32)


def iota(shape, dim):
    return lax.broadcasted_iota(jnp.int32, shape, dim)


def pack_kernel(
    dev_count, capacity, tile_cols, lane_ref, tile_ref, anchor_ref, weights_ref, observed_ref,
    accept_ref, send_ref, slot_ref, vals_ref
):
    foot_count, channels = observed_ref.shape
    bf16 = jnp.bfloat16
    tile = tile_ref[...]
    onehot = jnp.where(iota((dev_count, foot_count), 0) == tile, 1.0, 0.0)
    earlier = jnp.where(
        iota((foot_count, foot_count), 0) < iota((foot_count, foot_count), 1), 1.0, 0.0
    ).astype(bf16)
    before = dot_f32(onehot.astype(bf16), earlier, ((1,), (0,)))
    rank = jnp.sum(before * onehot, axis=0, keepdims=True).astype(jnp.int32)
    slot = tile * capacity + rank
    slot_ref[...] = slot

    chosen = jnp.where(accept_ref[...] != 0, observed_ref[...], REJECTED)
    parts = thirds(chosen)
    per_chunk = max(1, 128 // capacity)
    chunk = per_chunk * capacity
    for start in range(0, dev_count, per_chunk):
        place = jnp.where(
            iota((chunk, foot_count), 0) + start * capacity == slot, 1.0, 0.0
        ).astype(bf16)
        rows = [dot_f32(place, part, ((1,), (0,))) for part in parts]
        rows = (rows[0] + rows[1]) + rows[2]
        send_ref[start : start + per_chunk, :capacity, :] = rows.reshape(
            per_chunk, capacity, channels
        )

    anchor = anchor_ref[...]
    line = jnp.floor((anchor.astype(jnp.float32) + 0.5) * (1.0 / (tile_cols - 1)))
    base = anchor.astype(jnp.float32) + line
    weights = weights_ref[...]
    shares = weights / jnp.sum(weights, axis=0, keepdims=True)
    meta = jnp.concatenate(
        [base, shares, jnp.zeros((META - 5, foot_count), jnp.float32)], axis=0
    )
    for dev in range(dev_count):
        vals_ref[dev * META : (dev + 1) * META, :] = jnp.where(tile == dev, meta, 0.0)
    lanes = jnp.where(
        iota((channels, foot_count), 0) == rank + lane_ref[0], 1.0, 0.0
    ).astype(bf16)
    rows = [dot_f32(part, lanes, ((1,), (1,))) for part in thirds(vals_ref[...])]
    rows = (rows[0] + rows[1]) + rows[2]
    send_ref[:, capacity:, :] = rows.reshape(dev_count, META, channels)


def spread_kernel(absorb_ref, out_ref, turned_ref):
    levels, channels, lanes = out_ref.shape
    turned_ref[...] = (absorb_ref[...] * LOG2E).T

    def some_levels(i, carry):
        turned = turned_ref[...]
        for u in range(8):
            out_ref[i * 8 + u] = jnp.broadcast_to(turned[:, u : u + 1], (channels, lanes))
        turned_ref[...] = pltpu.roll(turned, levels - 8, 1)
        return carry

    lax.fori_loop(0, levels // 8, some_levels, 0)


def column_kernel(
    capacity, halo, recv_ref, background_ref, absorb_any, sensitivity_ref, inverse_ref,
    ready_west, ready_east, evolved_ref, field_ref, top_ref, bottom_ref, left_ref, right_ref,
    base_ref, sem, absorb_sem, cells_ref, absorb_b, slope_b, inverse_b, taken_ref, terms_ref, profile_ref,
    rise_ref, obs_ref, evo_ref, main_ref, side_ref, push_ref, sums_ref
):
    dev_count = recv_ref.shape[0]
    tile_rows, tile_cols, levels = background_ref.shape
    cells = tile_rows * tile_cols
    levels, channels, lanes = absorb_b.shape
    group = lanes // capacity
    blocks = dev_count // group
    wide = main_ref.shape[1]
    per_loop = UNROLL * wide * lanes // (levels * channels)
    corners = (0, 1, tile_cols, tile_cols + 1)

    copy = pltpu.make_async_copy(recv_ref.at[:, capacity, :], base_ref, sem)
    copy.start()
    absorb_copy = pltpu.make_async_copy(absorb_any, absorb_b, absorb_sem)
    absorb_copy.start()

    cells_ref[...] = background_ref[...].reshape(cells, levels).astype(jnp.float32)
    slope_b[...] = jnp.broadcast_to(sensitivity_ref[...] * LOG2E, (lanes, channels)).T
    inverse_b[...] = jnp.broadcast_to(inverse_ref[...], (lanes, channels)).T

    sums_ref[...] = jnp.zeros_like(sums_ref)
    terms_ref[...] = jnp.zeros_like(terms_ref)
    copy.wait()

    def base_of(f, at):
        return base_ref[f * group + lax.div(at, capacity), at].astype(jnp.int32)

    def gather(f, at):
        base = base_of(f, at)
        for k, step in enumerate(corners):
            taken_ref[k, pl.ds(at, 1), :] = cells_ref[pl.ds(base + step, 1), :]

    def scatter(f, at):
        base = base_of(f, at)
        for k, step in enumerate(corners):
            sums_ref[k, pl.ds(base + step, 1), :] += terms_ref[k, pl.ds(at, 1), :]

    def gather_first(i, carry):
        for u in range(8):
            gather(0, i * 8 + u)
        return carry

    lax.fori_loop(0, lanes // 8, gather_first, 0)
    absorb_copy.wait()

    def block(f, carry):
        before = jnp.maximum(f - 1, 0)
        after = jnp.minimum(f + 1, blocks - 1)
        mine = recv_ref[pl.ds(f * group, group)]
        shares = jnp.sum(mine[:, capacity:, :], axis=0)
        obs_ref[...] = mine[:, :capacity, :].reshape(lanes, channels).T
        profile = shares[1:2] * taken_ref[0].T
        for k in range(1, 4):
            profile = profile + shares[k + 1 : k + 2] * taken_ref[k].T
        profile_ref[...] = profile
        rise_ref[0 : levels - 1, :] = profile[1:] - profile[:-1]
        rise_ref[levels - 1 : levels, :] = jnp.zeros((1, lanes), jnp.float32)
        push_ref[...] = jnp.zeros_like(push_ref)

        def some_channels(c, carry):
            at = pl.multiple_of(c * wide, wide)
            slope = slope_b[pl.ds(at, wide), :]
            scale = slope * (LN2 * LN2)

            def down(i, state):
                path, total, above = state
                for u in range(UNROLL):
                    level = i * UNROLL + u
                    depth = absorb_b[level, pl.ds(at, wide), :] * jnp.exp2(
                        slope * profile_ref[pl.ds(level, 1), :]
                    )
                    path = path - depth
                    trans = jnp.exp2(path)
                    side = depth * scale
                    side_ref[level] = side
                    main_ref[level] = (above - trans) + side * total
                    total = total + trans * rise_ref[pl.ds(level, 1), :]
                    above = trans
                for u in range(per_loop):
                    scatter(before, (c * (levels // UNROLL) + i) * per_loop + u)
                return path, total, above

            zero = jnp.zeros((wide, lanes), jnp.float32)
            _, total, last = lax.fori_loop(0, levels // UNROLL, down, (zero, zero, zero + 1.0))
            main_ref[levels - 1] += last
            evolved = total + profile_ref[0:1, :]
            evo_ref[pl.ds(at, wide), :] = evolved
            obs = obs_ref[pl.ds(at, wide), :]
            force = jnp.where(
                obs < 0.5 * REJECTED, inverse_b[pl.ds(at, wide), :] * (obs - evolved), 0.0
            )

            def up(i, carry):
                for u in range(UNROLL):
                    level = i * UNROLL + u
                    push = force * (main_ref[level] - total * side_ref[level])
                    push_ref[pl.ds(pl.multiple_of(level * 8, 8), 8), :] += jnp.sum(
                        push.reshape(wide // 8, 8, lanes), axis=0
                    )
                for u in range(per_loop):
                    gather(after, (c * (levels // UNROLL) + i) * per_loop + u)
                return carry

            lax.fori_loop(0, levels // UNROLL, up, 0)
            return carry

        lax.fori_loop(0, channels // wide, some_channels, 0)
        evolved_ref[pl.ds(f * group, group)] = evo_ref[...].T.reshape(group, capacity, channels)
        push = push_ref[pl.ds(0, levels, stride=8), :]
        for u in range(1, 8):
            push = push + push_ref[pl.ds(u, levels, stride=8), :]
        for k in range(4):
            terms_ref[k] = (shares[k + 1 : k + 2] * push).T
        return carry

    lax.fori_loop(0, blocks, block, 0)

    def scatter_last(i, carry):
        for u in range(8):
            scatter(blocks - 1, i * 8 + u)
        return carry

    lax.fori_loop(0, lanes // 8, scatter_last, 0)

    field = (sums_ref[0] + sums_ref[1]) + (sums_ref[2] + sums_ref[3])
    field = field.reshape(tile_rows, tile_cols, levels)
    field_ref[...] = field

    borders = (
        (top_ref, field[:halo]),
        (bottom_ref, field[tile_rows - halo :]),
        (left_ref, field[:, :halo]),
        (right_ref, field[:, tile_cols - halo :]),
    )
    peak = jnp.full((1, levels), 1e-30, jnp.float32)
    for _, strip in borders:
        peak = jnp.maximum(
            peak, jnp.max(jnp.max(jnp.abs(strip), axis=0), axis=0, keepdims=True)
        )
    power = jnp.ceil(jnp.log2(peak))
    scale = jnp.exp2(15.0 - power)
    for ref, strip in borders:
        count = strip.shape[0]
        whole = jnp.floor(strip * scale + 0.5)
        whole = jnp.clip(whole, -32767.0, 32767.0)
        ref[:count] = whole.astype(jnp.int32).astype(jnp.int16)
        ref[count] = jnp.broadcast_to(power, strip.shape[1:]).astype(jnp.int32).astype(jnp.int16)


def decode_field(coded, power):
    scale = jnp.exp2(power.astype(jnp.int32).astype(jnp.float32) - 15.0)
    return coded.astype(jnp.int32).astype(jnp.float32) * scale


def lay(halo, target, centre, north, south, west, east):
    tile_rows, tile_cols, _ = centre.shape
    breadth = tile_cols + 2 * halo
    mid_r, mid_c = slice(halo, halo + tile_rows), slice(halo, halo + tile_cols)
    target[mid_r, mid_c] = centre[...]
    target[:halo, mid_c] = decode_field(north[:halo], north[halo])
    target[halo + tile_rows :, mid_c] = decode_field(south[:halo], south[halo])
    for side, cols in ((west, slice(0, halo)), (east, slice(halo + tile_cols, breadth))):
        read, put = 0, 0
        for count in (halo, tile_rows, halo):
            target[put : put + count, cols] = decode_field(
                side[read : read + count], side[read + count]
            )
            read, put = read + count + 1, put + count


KAPPA_LOW = 0.12
KAPPA_STEP = 0.125 / 65535


def encode_kappa(x):
    whole = jnp.round((x - KAPPA_LOW) * (1.0 / KAPPA_STEP))
    return (jnp.clip(whole, 0.0, 65535.0) - 32768.0).astype(jnp.int16)


def decode_kappa(x):
    whole = x.astype(jnp.int32).astype(jnp.float32) + 32768.0
    return whole * KAPPA_STEP + KAPPA_LOW


def interleave(plain_ref, target_ref):
    stretch = target_ref.shape[1]

    def row(i, carry):
        for t in range(stretch):
            target_ref[i, t] = plain_ref[i, pl.ds(t, 8, stride=stretch), :]
        return carry

    lax.fori_loop(0, plain_ref.shape[0], row, 0)


def eastward(x):
    return jnp.concatenate([x[1:], pltpu.roll(x[0], 7, 0)[None]], axis=0)


def westward(x):
    return jnp.concatenate([pltpu.roll(x[-1], 1, 0)[None], x[:-1]], axis=0)


def edges_kernel(
    halo, inside_ref, centre_ref, north_ref, south_ref, west_ref, east_side_ref, east_ref,
    south_edge_ref, plain_ref, kappa_ref
):
    tile_rows, tile_cols, _ = centre_ref.shape
    height, _ = plain_ref.shape[:2]
    mid_r, mid_c = slice(halo, halo + tile_rows), slice(halo, halo + tile_cols)
    low, end = slice(0, halo), slice(halo + tile_rows, height)
    plain_ref[mid_r, mid_c] = centre_ref[...]
    plain_ref[:, :halo] = decode_kappa(west_ref[...])
    plain_ref[:, halo + tile_cols :] = decode_kappa(east_side_ref[...])
    plain_ref[low, mid_c] = decode_kappa(north_ref[...])
    plain_ref[end, mid_c] = decode_kappa(south_ref[...])
    plain_ref[low] = plain_ref[low] * inside_ref[0]
    plain_ref[end] = plain_ref[end] * inside_ref[1]
    interleave(plain_ref, kappa_ref)

    def edges(i, carry):
        here = kappa_ref[i]
        east_ref[i] = 0.5 * (here + eastward(here))
        south_edge_ref[i] = 0.5 * (here + kappa_ref[jnp.minimum(i + 1, height - 1)])
        return carry

    lax.fori_loop(0, height, edges, 0)


def relax_kernel(
    halo, inside_ref, centre_ref, north_ref, south_ref, west_ref, east_side_ref, east_ref,
    south_edge_ref, out_ref, plain_ref, first_ref, second_ref
):
    tile_rows, tile_cols, _ = out_ref.shape
    height = tile_rows + 2 * halo
    stretch = first_ref.shape[1]
    lay(halo, plain_ref, centre_ref, north_ref, south_ref, west_ref, east_side_ref)
    interleave(plain_ref, first_ref)

    source, target = first_ref, second_ref
    for step in range(1, halo + 1):
        last = step == halo

        def row(i, carry, scale=None, source=source, target=target, last=last):
            here, from_north = carry
            below = source[i + 1]
            to_east = east_ref[i] * (eastward(here) - here)
            from_south = south_edge_ref[i] * (below - here)
            value = here + (to_east - westward(to_east)) + (from_south - from_north)
            if scale is not None:
                value = value * scale
            if last:
                for t in range(stretch):
                    plain_ref[i, pl.ds(t, 8, stride=stretch), :] = value[t]
            else:
                target[i] = value
            return below, from_south

        here = source[step]
        carry = (here, south_edge_ref[step - 1] * (here - source[step - 1]))
        carry = lax.fori_loop(
            step, halo, functools.partial(row, scale=inside_ref[0]), carry, unroll=True
        )
        carry = lax.fori_loop(halo, halo + tile_rows, row, carry, unroll=4)
        lax.fori_loop(
            halo + tile_rows, height - step, functools.partial(row, scale=inside_ref[1]), carry,
            unroll=True,
        )
        source, target = target, source
    out_ref[...] = plain_ref[halo : halo + tile_rows, halo : halo + tile_cols, :]


def depart_kernel(slot_ref, evolved_ref, observed_ref, out_ref):
    foot_count, _ = observed_ref.shape
    slots = evolved_ref.shape[0]
    slot = slot_ref[...]
    parts = thirds(evolved_ref[...])
    chosen = jnp.where(iota((slots, foot_count), 0) == slot, 1.0, 0.0).astype(jnp.bfloat16)
    rows = [dot_f32(chosen, part, ((0,), (0,))) for part in parts]
    out_ref[...] = observed_ref[...] - ((rows[0] + rows[1]) + rows[2])


def vmem():
    return pl.BlockSpec(memory_space=pltpu.VMEM)


def smem():
    return pl.BlockSpec(memory_space=pltpu.SMEM)


def anywhere():
    return pl.BlockSpec(memory_space=pl.ANY)


def params(mib):
    return pltpu.CompilerParams(vmem_limit_bytes=mib * MIB)


def cost(flops, transcendentals, moved):
    return pl.CostEstimate(flops=flops, transcendentals=transcendentals, bytes_accessed=moved)


def neighbours(axis, periodic):
    count = lax.axis_size(axis)
    forward = [(i, i + 1) for i in range(count - 1)]
    if periodic:
        forward.append((count - 1, 0))
    return forward, [(target, source) for source, target in forward]


def halos(top, bottom, left, right):
    lat_up, lat_down = neighbours("lat", False)
    lon_up, lon_down = neighbours("lon", True)
    halo = left.shape[1]
    north = lax.ppermute(bottom, "lat", lat_up)
    south = lax.ppermute(top, "lat", lat_down)
    rights = jnp.concatenate([north[:, -halo:], right, south[:, -halo:]], axis=0)
    lefts = jnp.concatenate([north[:, :halo], left, south[:, :halo]], axis=0)
    west = lax.ppermute(rights, "lon", lon_up)
    east = lax.ppermute(lefts, "lon", lon_down)
    return north, south, west, east


def local(
    background, diffusivity, tile_index, anchor, weights, observed, accept, absorb, sensitivity,
    inverse_variance
):
    f32 = jnp.float32
    lat_count = lax.axis_size("lat")
    lon_count = lax.axis_size("lon")
    dev_count = lat_count * lon_count
    foot_count, channels = observed.shape
    capacity = max(2, 2 * foot_count // dev_count)
    tile_rows, tile_cols, levels = background.shape
    slots = dev_count * capacity
    lanes = 128
    group = lanes // capacity
    cells = tile_rows * tile_cols
    halo = STEPS

    me = lax.axis_index("lat") * lon_count + lax.axis_index("lon")
    lane = (lax.rem(me, group) * capacity).astype(jnp.int32).reshape(1)
    send, slot = pl.pallas_call(
        functools.partial(pack_kernel, dev_count, capacity, tile_cols),
        out_shape=(
            jax.ShapeDtypeStruct((dev_count, capacity + META, channels), f32),
            jax.ShapeDtypeStruct((1, foot_count), jnp.int32),
        ),
        in_specs=[smem()] + [vmem()] * 5,
        out_specs=(vmem(), vmem()),
        scratch_shapes=[pltpu.VMEM((dev_count * META, foot_count), f32)],
        compiler_params=params(60),
        cost_estimate=cost(2 * slots * foot_count * channels * 3, 0, 4 * slots * channels * 3),
        name="pack",
    )(
        lane, tile_index.reshape(1, foot_count), anchor.reshape(1, foot_count), weights.T,
        observed, accept
    )
    recv = lax.all_to_all(send, ("lat", "lon"), split_axis=0, concat_axis=0, tiled=True)

    kappa_halos = halos(
        encode_kappa(diffusivity[:halo]), encode_kappa(diffusivity[-halo:]),
        encode_kappa(diffusivity[:, :halo]), encode_kappa(diffusivity[:, -halo:])
    )
    absorb_wide = pl.pallas_call(
        spread_kernel,
        out_shape=jax.ShapeDtypeStruct((levels, channels, lanes), f32),
        in_specs=[vmem()],
        out_specs=vmem(),
        scratch_shapes=[pltpu.VMEM((channels, levels), f32)],
        compiler_params=params(60),
        cost_estimate=cost(levels * channels * lanes, 0, 4 * levels * channels * lanes),
        name="spread",
    )(absorb)

    wide = 32
    evolved, field, top, bottom, left, right = pl.pallas_call(
        functools.partial(column_kernel, capacity, halo),
        out_shape=(
            jax.ShapeDtypeStruct((dev_count, capacity, channels), f32),
            jax.ShapeDtypeStruct((tile_rows, tile_cols, levels), f32),
            jax.ShapeDtypeStruct((halo + 1, tile_cols, levels), jnp.int16),
            jax.ShapeDtypeStruct((halo + 1, tile_cols, levels), jnp.int16),
            jax.ShapeDtypeStruct((tile_rows + 1, halo, levels), jnp.int16),
            jax.ShapeDtypeStruct((tile_rows + 1, halo, levels), jnp.int16),
        ),
        in_specs=[vmem()] * 2 + [anywhere()] + [vmem()] * 2 + [anywhere()] * 2,
        out_specs=(vmem(),) * 6,
        scratch_shapes=[
            pltpu.SMEM((dev_count, channels), f32),
            pltpu.SemaphoreType.DMA,
            pltpu.SemaphoreType.DMA,
            pltpu.VMEM((cells, levels), f32),
            pltpu.VMEM((levels, channels, lanes), f32),
            pltpu.VMEM((channels, lanes), f32),
            pltpu.VMEM((channels, lanes), f32),
            pltpu.VMEM((4, lanes, levels), f32),
            pltpu.VMEM((4, lanes, levels), f32),
            pltpu.VMEM((levels, lanes), f32),
            pltpu.VMEM((levels, lanes), f32),
            pltpu.VMEM((channels, lanes), f32),
            pltpu.VMEM((channels, lanes), f32),
            pltpu.VMEM((levels, wide, lanes), f32),
            pltpu.VMEM((levels, wide, lanes), f32),
            pltpu.VMEM((levels * 8, lanes), f32),
            pltpu.VMEM((4, cells, levels), f32),
        ],
        compiler_params=params(60),
        cost_estimate=cost(
            14 * slots * levels * channels, 2 * slots * levels * channels, 12 * cells * levels
        ),
        name="column",
    )(
        recv, background, absorb_wide, sensitivity.reshape(1, channels),
        inverse_variance.reshape(1, channels), *kappa_halos[2:]
    )

    field_halos = halos(top, bottom, left, right)
    lat_at = lax.axis_index("lat")
    inside = jnp.stack([lat_at > 0, lat_at < lat_count - 1]).astype(f32)
    height, breadth = tile_rows + 2 * halo, tile_cols + 2 * halo

    plain = pltpu.VMEM((height, breadth, levels), f32)
    mixed = (height, breadth // 8, 8, levels)

    east, south = pl.pallas_call(
        functools.partial(edges_kernel, halo),
        out_shape=(jax.ShapeDtypeStruct(mixed, f32),) * 2,
        in_specs=[smem()] + [vmem()] * 5,
        out_specs=(vmem(),) * 2,
        scratch_shapes=[plain, pltpu.VMEM(mixed, f32)],
        compiler_params=params(22),
        cost_estimate=cost(4 * height * breadth * levels, 0, 12 * cells * levels),
        name="edges",
    )(inside, diffusivity, *kappa_halos)


    returned = lax.all_to_all(
        evolved, ("lat", "lon"), split_axis=0, concat_axis=0, tiled=True
    )

    departure = pl.pallas_call(
        depart_kernel,
        out_shape=jax.ShapeDtypeStruct((foot_count, channels), f32),
        in_specs=[vmem()] * 3,
        out_specs=vmem(),
        compiler_params=params(16),
        cost_estimate=cost(2 * slots * foot_count * channels * 3, 0, 4 * slots * channels * 2),
        name="depart",
    )(slot, returned.reshape(slots, channels), observed)

    increment = pl.pallas_call(
        functools.partial(relax_kernel, halo),
        out_shape=jax.ShapeDtypeStruct((tile_rows, tile_cols, levels), f32),
        in_specs=[smem()] + [vmem()] * 7,
        out_specs=vmem(),
        scratch_shapes=[plain, pltpu.VMEM(mixed, f32), pltpu.VMEM(mixed, f32)],
        compiler_params=params(26),
        cost_estimate=cost(10 * STEPS * height * breadth * levels, 0, 16 * cells * levels),
        name="relax",
    )(inside, field, *field_halos, east, south)
    return (departure, increment)


def solution(mesh):
    in_specs = (
        P("lat", "lon", None),
        P("lat", "lon", None),
        P(("lat", "lon"), None),
        P(("lat", "lon")),
        P(("lat", "lon"), None),
        P(("lat", "lon"), None),
        P(("lat", "lon"), None),
        P(),
        P(),
        P(),
    )
    out_specs = (P(("lat", "lon"), None), P("lat", "lon", None))

    return jax.shard_map(local, mesh=mesh, in_specs=in_specs, out_specs=out_specs, check_vma=False)
```

profile of v0, /device:TPU:1, one launch (start us, length us, event | category | flops | bytes accessed | tf_op | source)
XLA Modules:
  0.0 122.4 jit_solution(12385890958236815221)
XLA Ops:
  0.6 3.5 %pack.1 = (f32[32,40,128]{2,1,0:T(8,128)}, s32[1,512]{1,0:T(1,128)}) custom-call(s32[1]{0:T(128)} %bitcast.lane_ref, s32[1,512]{1,0:T(1,128)} %bitcast.11, s32[1,512]{1,0:T(1,128)} %bitcast.12, f32[4,512]{1,0:T(4,128)} %bitcast.10, f32[512,128]{1,0:T(8,128)} %observed_ref.3, s32[512,128]{1,0:T(8,128)} %accept_ref.1), custom_call_target="tpu_custom_call" | custom-call | flops 402653184 | bytes 1572864 | tf_op jit(solution)/shard_map/pack/pallas_call | solution.py:446
  4.2 7.1 %all-to-all-start = ((f32[32,40,128]{2,1,0:T(8,128)}), f32[32,40,128]{2,1,0:T(8,128)}, u32[]{:S(2)}, u32[]{:S(2)}) async-start(f32[32,40,128]{2,1,0:T(8,128)} %get-tuple-element.13), calls=%async_computation | async-start | bytes 1310720 | tf_op jit(solution)/shard_map/all_to_all | solution.py:462
  11.3 0.2 add_convert_fusion.3
  11.5 2.2 %collective-permute-start.1 = (s16[8,64,128]{2,1,0:T(8,128)(2,1)S(1)}, s16[8,64,128]{2,1,0:T(8,128)(2,1)S(1)}, u32[]{:S(2)}, u32[]{:S(2)}) collective-permute-start(s16[8,64,128]{2,1,0:T(8,128)(2,1)S(1)} %get-tuple-element.25), channel_id=1, source_target_pairs={{8,0},{16,8},{24,16},{9,1},{17,9},{25,17},{10,2},{18,10},{26,18},{... | collective-permute-start | bytes 393224 | tf_op jit(solution)/shard_map/ppermute | solution.py:419
  13.8 3.3 %collective-permute-start = (s16[8,64,128]{2,1,0:T(8,128)(2,1)S(1)}, s16[8,64,128]{2,1,0:T(8,128)(2,1)S(1)}, u32[]{:S(2)}, u32[]{:S(2)}) collective-permute-start(s16[8,64,128]{2,1,0:T(8,128)(2,1)S(1)} %get-tuple-element.24), channel_id=1, source_target_pairs={{0,8},{8,16},{16,24},{1,9},{9,17},{17,25},{2,10},{10,18},{18,26},{... | collective-permute-start | bytes 393224 | tf_op jit(solution)/shard_map/ppermute | solution.py:418
  17.1 0.2 add_convert_fusion
  17.3 2.7 %collective-permute-done.1.south_ref = s16[8,64,128]{2,1,0:T(8,128)(2,1)S(1)} collective-permute-done((s16[8,64,128]{2,1,0:T(8,128)(2,1)S(1)}, s16[8,64,128]{2,1,0:T(8,128)(2,1)S(1)}, u32[]{:S(2)}, u32[]{:S(2)}) %collective-permute-start.1) | collective-permute-done | bytes 131104 | tf_op jit(solution)/shard_map/ppermute | solution.py:419
  20.0 0.6 collective-permute-done.north_ref
  20.6 0.4 collective-permute-start.2
  21.1 3.9 %collective-permute-start.3 = (s16[80,8,128]{2,1,0:T(8,128)(2,1)S(1)}, s16[80,8,128]{2,1,0:T(8,128)(2,1)S(1)}, u32[]{:S(2)}, u32[]{:S(2)}) collective-permute-start(s16[80,8,128]{2,1,0:T(8,128)(2,1)S(1)} %pad_add_fusion.3), channel_id=1, source_target_pairs={{1,0},{2,1},{3,2},{4,3},{5,4},{6,5},{7,6},{0,7},{9,8},{10,9},{11,1... | collective-permute-start | bytes 491528 | tf_op jit(solution)/shard_map/ppermute | solution.py:423
  24.9 7.9 %spread.1.absorb_any = f32[128,128,128]{2,1,0:T(8,128)} custom-call(f32[128,128]{1,0:T(8,128)} %absorb_ref.1), custom_call_target="tpu_custom_call" | custom-call | flops 2097152 | bytes 8388608 | tf_op jit(solution)/shard_map/spread/pallas_call | solution.py:468
  32.8 0.0 collective-permute-done.2.ready_west.west_ref
  32.8 0.6 all-to-all-done.recv_ref
  33.4 0.0 copy-done.2
  33.5 0.1 copy-done.4
  33.6 50.9 %column.1 = (f32[32,32,128]{2,1,0:T(8,128)}, f32[64,64,128]{2,1,0:T(8,128)}, s16[9,64,128]{2,1,0:T(8,128)(2,1)}, s16[9,64,128]{2,1,0:T(8,128)(2,1)}, s16[65,8,12...) custom-call(f32[32,40,128]{2,1,0:T(8,128)} %all-to-all-done.recv_ref, bf16[64,64,128]{2,1,0:T(8,128)(2,1)} %background_ref.1, ...), custom_call_target="tpu_custom_call" | custom-call | flops 234881024 | bytes 6291456 | tf_op jit(solution)/shard_map/column/pallas_call | solution.py:480
  84.4 4.2 %all-to-all-start.1 = ((f32[32,32,128]{2,1,0:T(8,128)}), f32[32,32,128]{2,1,0:T(8,128)S(1)}, u32[]{:S(2)}, u32[]{:S(2)}) async-start(f32[32,32,128]{2,1,0:T(8,128)} %get-tuple-element.14), calls=%async_computation.1 | async-start | bytes 1048576 | tf_op jit(solution)/shard_map/all_to_all | solution.py:541
  88.6 2.2 %collective-permute-start.5 = (s16[9,64,128]{2,1,0:T(8,128)(2,1)}, s16[9,64,128]{2,1,0:T(8,128)(2,1)S(1)}, u32[]{:S(2)}, u32[]{:S(2)}) collective-permute-start(s16[9,64,128]{2,1,0:T(8,128)(2,1)} %get-tuple-element.17), channel_id=1, source_target_pairs={{8,0},{16,8},{24,16},{9,1},{17,9},{25,17},{10,2},{18,10},{26,18},{... | collective-permute-start | bytes 442376 | tf_op jit(solution)/shard_map/ppermute | solution.py:419
  90.8 3.4 %collective-permute-start.4 = (s16[9,64,128]{2,1,0:T(8,128)(2,1)}, s16[9,64,128]{2,1,0:T(8,128)(2,1)S(1)}, u32[]{:S(2)}, u32[]{:S(2)}) collective-permute-start(s16[9,64,128]{2,1,0:T(8,128)(2,1)} %get-tuple-element.16), channel_id=1, source_target_pairs={{0,8},{8,16},{16,24},{1,9},{9,17},{17,25},{2,10},{10,18},{18,26},{... | collective-permute-start | bytes 442376 | tf_op jit(solution)/shard_map/ppermute | solution.py:418
  94.2 3.4 %collective-permute-done.5.south_ref = s16[9,64,128]{2,1,0:T(8,128)(2,1)S(1)} collective-permute-done((s16[9,64,128]{2,1,0:T(8,128)(2,1)}, s16[9,64,128]{2,1,0:T(8,128)(2,1)S(1)}, u32[]{:S(2)}, u32[]{:S(2)}) %collective-permute-start.5) | collective-permute-done | bytes 147488 | tf_op jit(solution)/shard_map/ppermute | solution.py:419
  97.6 0.2 collective-permute-done.4.north_ref
  97.8 1.6 %pad_add_fusion = s16[83,8,128]{2,1,0:T(8,128)(2,1)} fusion(s16[9,8,128]{2,1,0:T(8,128)(2,1)S(1)} %get-tuple-element.29, s16[65,8,128]{2,1,0:T(8,128)(2,1)} %get-tuple-element.18, s16[9,8,128]{2,1,0:T(8,128)(2,1)S(1)} %get-tuple-element.27), kind=kLoop, calls=%fused_computation.4 | loop fusion | flops 169984 | bytes 339968 | tf_op jit(solution)/shard_map/concatenate | solution.py:420
  99.4 0.4 collective-permute-start.6
  99.8 1.6 %pad_add_fusion.1 = s16[83,8,128]{2,1,0:T(8,128)(2,1)} fusion(s16[9,8,128]{2,1,0:T(8,128)(2,1)S(1)} %get-tuple-element.28, s16[65,8,128]{2,1,0:T(8,128)(2,1)} %get-tuple-element.19, s16[9,8,128]{2,1,0:T(8,128)(2,1)S(1)} %get-tuple-element.26), kind=kLoop, calls=%fused_computation.5 | loop fusion | flops 169984 | bytes 339968 | tf_op jit(solution)/shard_map/concatenate | solution.py:421
  101.4 3.8 %collective-permute-start.7 = (s16[83,8,128]{2,1,0:T(8,128)(2,1)}, s16[83,8,128]{2,1,0:T(8,128)(2,1)S(1)}, u32[]{:S(2)}, u32[]{:S(2)}) collective-permute-start(s16[83,8,128]{2,1,0:T(8,128)(2,1)} %pad_add_fusion.1), channel_id=1, source_target_pairs={{1,0},{2,1},{3,2},{4,3},{5,4},{6,5},{7,6},{0,7},{9,8},{10,9},{11,1... | collective-permute-start | bytes 509960 | tf_op jit(solution)/shard_map/ppermute | solution.py:423
  105.2 0.1 add_convert_fusion.4.inside_ref
  105.2 1.0 copy-done.3
  106.3 0.9 copy-done.5
  107.2 2.3 %edges.1 = (f32[80,10,8,128]{3,2,1,0:T(8,128)S(1)}, f32[80,10,8,128]{3,2,1,0:T(8,128)S(1)}) custom-call(f32[2]{0:T(128)S(1)} %add_convert_fusion.4.inside_ref, f32[64,64,128]{2,1,0:T(8,128)S(1)} %copy-done, s16[8,64,128]{2,1,0:T(8,128)(2,1)S(1)} %collective-permute-done.north_ref, s16[8,64,128]{2,1,0:T(8,128)(2,1)S(1)} %collective-permute-done.1.south_ref, ...), custom_call_target="tpu_custom_call" | custom-call | flops 3276800 | bytes 6291456 | tf_op jit(solution)/shard_map/edges/pallas_call | solution.py:529
  109.6 0.3 collective-permute-done.7.east_side_ref
  109.8 10.7 %relax.1 = f32[64,64,128]{2,1,0:T(8,128)} custom-call(f32[2]{0:T(128)S(1)} %add_convert_fusion.4.inside_ref, f32[64,64,128]{2,1,0:T(8,128)S(1)} %copy-done.1, s16[9,64,128]{2,1,0:T(8,128)(2,1)S(1)} %collective-permute-done.4.north_ref, s16[9,64,128]{2,1,0:T(8,128)(2,1)S(1)} %collective-permute-done.5.south_ref, ...), custom_call_target="tpu_custom_call" | custom-call | flops 65536000 | bytes 8388608 | tf_op jit(solution)/shard_map/relax/pallas_call | solution.py:555
  120.6 1.8 %depart.1 = f32[512,128]{1,0:T(8,128)} custom-call(s32[1,512]{1,0:T(1,128)S(1)} %copy-done.7, f32[1024,128]{1,0:T(8,128)S(1)} %bitcast.9, f32[512,128]{1,0:T(8,128)S(1)} %copy-done.6), custom_call_target="tpu_custom_call" | custom-call | flops 402653184 | bytes 1048576 | tf_op jit(solution)/shard_map/depart/pallas_call | solution.py:545
  (21 shorter events, 0.1 us)
Async XLA Ops:
  0.6 10.7 %copy-start = (f32[64,64,128]{2,1,0:T(8,128)S(1)}, f32[64,64,128]{2,1,0:T(8,128)}, u32[]{:S(2)}) copy-start(f32[64,64,128]{2,1,0:T(8,128)} %centre_ref.1) | copy-start | bytes 6291460
  4.2 29.3 %all-to-all-start = ((f32[32,40,128]{2,1,0:T(8,128)}), f32[32,40,128]{2,1,0:T(8,128)}, u32[]{:S(2)}, u32[]{:S(2)}) async-start(f32[32,40,128]{2,1,0:T(8,128)} %get-tuple-element.13), calls=%async_computation | async-start | bytes 1310720 | tf_op jit(solution)/shard_map/all_to_all | solution.py:462
  11.5 8.5 %collective-permute-start.1 = (s16[8,64,128]{2,1,0:T(8,128)(2,1)S(1)}, s16[8,64,128]{2,1,0:T(8,128)(2,1)S(1)}, u32[]{:S(2)}, u32[]{:S(2)}) collective-permute-start(s16[8,64,128]{2,1,0:T(8,128)(2,1)S(1)} %get-tuple-element.25), channel_id=1, source_target_pairs={{8,0},{16,8},{24,16},{9,1},{17,9},{25,17},{10,2},{18,10},{26,18},{... | collective-permute-start | bytes 393224 | tf_op jit(solution)/shard_map/ppermute | solution.py:419
  13.8 6.9 %collective-permute-start = (s16[8,64,128]{2,1,0:T(8,128)(2,1)S(1)}, s16[8,64,128]{2,1,0:T(8,128)(2,1)S(1)}, u32[]{:S(2)}, u32[]{:S(2)}) collective-permute-start(s16[8,64,128]{2,1,0:T(8,128)(2,1)S(1)} %get-tuple-element.24), channel_id=1, source_target_pairs={{0,8},{8,16},{16,24},{1,9},{9,17},{17,25},{2,10},{10,18},{18,26},{... | collective-permute-start | bytes 393224 | tf_op jit(solution)/shard_map/ppermute | solution.py:418
  20.6 12.2 %collective-permute-start.2 = (s16[80,8,128]{2,1,0:T(8,128)(2,1)S(1)}, s16[80,8,128]{2,1,0:T(8,128)(2,1)S(1)}, u32[]{:S(2)}, u32[]{:S(2)}) collective-permute-start(s16[80,8,128]{2,1,0:T(8,128)(2,1)S(1)} %pad_add_fusion.2), channel_id=1, source_target_pairs={{0,1},{1,2},{2,3},{3,4},{4,5},{5,6},{6,7},{7,0},{8,9},{9,10},{10,1... | collective-permute-start | bytes 491528 | tf_op jit(solution)/shard_map/ppermute | solution.py:422
  21.1 11.8 %collective-permute-start.3 = (s16[80,8,128]{2,1,0:T(8,128)(2,1)S(1)}, s16[80,8,128]{2,1,0:T(8,128)(2,1)S(1)}, u32[]{:S(2)}, u32[]{:S(2)}) collective-permute-start(s16[80,8,128]{2,1,0:T(8,128)(2,1)S(1)} %pad_add_fusion.3), channel_id=1, source_target_pairs={{1,0},{2,1},{3,2},{4,3},{5,4},{6,5},{7,6},{0,7},{9,8},{10,9},{11,1... | collective-permute-start | bytes 491528 | tf_op jit(solution)/shard_map/ppermute | solution.py:423
  32.8 0.7 copy-start.2
  32.8 0.7 copy-start.4
  84.4 36.1 %all-to-all-start.1 = ((f32[32,32,128]{2,1,0:T(8,128)}), f32[32,32,128]{2,1,0:T(8,128)S(1)}, u32[]{:S(2)}, u32[]{:S(2)}) async-start(f32[32,32,128]{2,1,0:T(8,128)} %get-tuple-element.14), calls=%async_computation.1 | async-start | bytes 1048576 | tf_op jit(solution)/shard_map/all_to_all | solution.py:541
  88.6 9.0 %collective-permute-start.5 = (s16[9,64,128]{2,1,0:T(8,128)(2,1)}, s16[9,64,128]{2,1,0:T(8,128)(2,1)S(1)}, u32[]{:S(2)}, u32[]{:S(2)}) collective-permute-start(s16[9,64,128]{2,1,0:T(8,128)(2,1)} %get-tuple-element.17), channel_id=1, source_target_pairs={{8,0},{16,8},{24,16},{9,1},{17,9},{25,17},{10,2},{18,10},{26,18},{... | collective-permute-start | bytes 442376 | tf_op jit(solution)/shard_map/ppermute | solution.py:419
  90.8 7.0 %collective-permute-start.4 = (s16[9,64,128]{2,1,0:T(8,128)(2,1)}, s16[9,64,128]{2,1,0:T(8,128)(2,1)S(1)}, u32[]{:S(2)}, u32[]{:S(2)}) collective-permute-start(s16[9,64,128]{2,1,0:T(8,128)(2,1)} %get-tuple-element.16), channel_id=1, source_target_pairs={{0,8},{8,16},{16,24},{1,9},{9,17},{17,25},{2,10},{10,18},{18,26},{... | collective-permute-start | bytes 442376 | tf_op jit(solution)/shard_map/ppermute | solution.py:418
  99.4 10.1 %collective-permute-start.6 = (s16[83,8,128]{2,1,0:T(8,128)(2,1)}, s16[83,8,128]{2,1,0:T(8,128)(2,1)S(1)}, u32[]{:S(2)}, u32[]{:S(2)}) collective-permute-start(s16[83,8,128]{2,1,0:T(8,128)(2,1)} %pad_add_fusion), channel_id=1, source_target_pairs={{0,1},{1,2},{2,3},{3,4},{4,5},{5,6},{6,7},{7,0},{8,9},{9,10},{10,1... | collective-permute-start | bytes 509960 | tf_op jit(solution)/shard_map/ppermute | solution.py:422
  101.4 8.5 %collective-permute-start.7 = (s16[83,8,128]{2,1,0:T(8,128)(2,1)}, s16[83,8,128]{2,1,0:T(8,128)(2,1)S(1)}, u32[]{:S(2)}, u32[]{:S(2)}) collective-permute-start(s16[83,8,128]{2,1,0:T(8,128)(2,1)} %pad_add_fusion.1), channel_id=1, source_target_pairs={{1,0},{2,1},{3,2},{4,3},{5,4},{6,5},{7,6},{0,7},{9,8},{10,9},{11,1... | collective-permute-start | bytes 509960 | tf_op jit(solution)/shard_map/ppermute | solution.py:423
  105.2 4.7 %copy-start.1 = (f32[64,64,128]{2,1,0:T(8,128)S(1)}, f32[64,64,128]{2,1,0:T(8,128)}, u32[]{:S(2)}) copy-start(f32[64,64,128]{2,1,0:T(8,128)} %get-tuple-element.15.centre_ref) | copy-start | bytes 6291460
  105.2 1.1 copy-start.3
  106.3 0.9 copy-start.5
  109.8 10.7 %copy-start.6 = (f32[512,128]{1,0:T(8,128)S(1)}, f32[512,128]{1,0:T(8,128)}, u32[]{:S(2)}) copy-start(f32[512,128]{1,0:T(8,128)} %observed_ref.3) | copy-start | bytes 786436
  109.8 10.7 %copy-start.7 = (s32[1,512]{1,0:T(1,128)S(1)}, s32[1,512]{1,0:T(1,128)}, u32[]{:S(2)}) copy-start(s32[1,512]{1,0:T(1,128)} %get-tuple-element.12.slot_ref) | copy-start | bytes 6148
where the time goes:
time: 123 us; the launch traced here: 122 us
  Pallas kernels  77.1 us (63%)
  starting transfers between devices  30.9 us (25%)
  waiting for transfers between devices  7.83 us (6%)
  other arithmetic  3.65 us (3%)
  local copies, waits for them, and re-layouts  2.12 us (2%)
    pallas_call x1, Pallas kernels, local(): pl.pallas_call(functools.partial(column_kernel, capacity, halo), out_shap...  50.9 us
    pallas_call x1, Pallas kernels, local(): pl.pallas_call(functools.partial(relax_kernel, halo), out_shape=jax.Shape...  10.7 us
    pallas_call x1, Pallas kernels, local(): pl.pallas_call(spread_kernel, out_shape=jax.ShapeDtypeStruct((levels, cha...  7.89 us
    ppermute x2, starting transfers between devices, halos(): east = lax.ppermute(lefts, 'lon', lon_down)  7.63 us
    all_to_all x1, starting transfers between devices, local(): lax.all_to_all(send, ('lat', 'lon'), split_axis=0, concat_axis=0, tiled=T...  7.13 us
    ppermute x2, starting transfers between devices, halos(): north = lax.ppermute(bottom, 'lat', lat_up)  6.72 us
    ppermute x2, waiting for transfers between devices, halos(): south = lax.ppermute(top, 'lat', lat_down)  6.09 us
    ppermute x2, starting transfers between devices, halos(): south = lax.ppermute(top, 'lat', lat_down)  4.4 us
  transfers between devices with their start and end apart: 10, of which 6 were waited for; matrix products, arithmetic and copies ran while one was open for 3% of the time, Pallas kernels for 17%

commit v1 on v0

--- a/solution.py
+++ b/solution.py
@@ -15,7 +15,7 @@
 LOG2E = math.log2(math.e)
 LN2 = math.log(2.0)
 MIB = 1024 * 1024
-UNROLL = 16
+UNROLL = 32
 
 
 def thirds(x):
@@ -83,17 +83,17 @@
 
 
 def spread_kernel(absorb_ref, out_ref, turned_ref):
-    levels, channels, lanes = out_ref.shape
-    turned_ref[...] = (absorb_ref[...] * LOG2E).T
-
-    def some_levels(i, carry):
-        turned = turned_ref[...]
-        for u in range(8):
-            out_ref[i * 8 + u] = jnp.broadcast_to(turned[:, u : u + 1], (channels, lanes))
-        turned_ref[...] = pltpu.roll(turned, levels - 8, 1)
-        return carry
-
-    lax.fori_loop(0, levels // 8, some_levels, 0)
+    some, channels, lanes = out_ref.shape
+    levels = absorb_ref.shape[0]
+
+    @pl.when(pl.program_id(0) == 0)
+    def _():
+        turned_ref[...] = (absorb_ref[...] * LOG2E).T
+
+    turned = turned_ref[...]
+    for u in range(some):
+        out_ref[u] = jnp.broadcast_to(turned[:, u : u + 1], (channels, lanes))
+    turned_ref[...] = pltpu.roll(turned, levels - some, 1)
 
 
 def column_kernel(
@@ -230,24 +230,24 @@
     field_ref[...] = field
 
     borders = (
-        (top_ref, field[:halo]),
-        (bottom_ref, field[tile_rows - halo :]),
-        (left_ref, field[:, :halo]),
-        (right_ref, field[:, tile_cols - halo :]),
+        (top_ref, 0, field[:halo]),
+        (bottom_ref, 0, field[tile_rows - halo :]),
+        (left_ref, halo + 1, field[:, :halo]),
+        (right_ref, halo + 1, field[:, tile_cols - halo :]),
     )
     peak = jnp.full((1, levels), 1e-30, jnp.float32)
-    for _, strip in borders:
+    for _, _, strip in borders:
         peak = jnp.maximum(
             peak, jnp.max(jnp.max(jnp.abs(strip), axis=0), axis=0, keepdims=True)
         )
     power = jnp.ceil(jnp.log2(peak))
     scale = jnp.exp2(15.0 - power)
-    for ref, strip in borders:
-        count = strip.shape[0]
+    for ref, first, strip in borders:
+        last = first + strip.shape[0]
         whole = jnp.floor(strip * scale + 0.5)
         whole = jnp.clip(whole, -32767.0, 32767.0)
-        ref[:count] = whole.astype(jnp.int32).astype(jnp.int16)
-        ref[count] = jnp.broadcast_to(power, strip.shape[1:]).astype(jnp.int32).astype(jnp.int16)
+        ref[first:last] = whole.astype(jnp.int32).astype(jnp.int16)
+        ref[last] = jnp.broadcast_to(power, strip.shape[1:]).astype(jnp.int32).astype(jnp.int16)
 
 
 def decode_field(coded, power):
@@ -305,18 +305,26 @@
 
 
 def edges_kernel(
-    halo, inside_ref, centre_ref, north_ref, south_ref, west_ref, east_side_ref, east_ref,
-    south_edge_ref, plain_ref, kappa_ref
+    halo, inside_ref, centre_ref, north_ref, south_ref, west_hbm, east_hbm, east_ref,
+    south_edge_ref, plain_ref, kappa_ref, west_ref, east_side_ref, sems
 ):
+    copies = [
+        pltpu.make_async_copy(west_hbm, west_ref, sems.at[0]),
+        pltpu.make_async_copy(east_hbm, east_side_ref, sems.at[1]),
+    ]
+    for copy in copies:
+        copy.start()
     tile_rows, tile_cols, _ = centre_ref.shape
     height, _ = plain_ref.shape[:2]
     mid_r, mid_c = slice(halo, halo + tile_rows), slice(halo, halo + tile_cols)
     low, end = slice(0, halo), slice(halo + tile_rows, height)
     plain_ref[mid_r, mid_c] = centre_ref[...]
+    plain_ref[low, mid_c] = decode_kappa(north_ref[...])
+    plain_ref[end, mid_c] = decode_kappa(south_ref[...])
+    for copy in copies:
+        copy.wait()
     plain_ref[:, :halo] = decode_kappa(west_ref[...])
     plain_ref[:, halo + tile_cols :] = decode_kappa(east_side_ref[...])
-    plain_ref[low, mid_c] = decode_kappa(north_ref[...])
-    plain_ref[end, mid_c] = decode_kappa(south_ref[...])
     plain_ref[low] = plain_ref[low] * inside_ref[0]
     plain_ref[end] = plain_ref[end] * inside_ref[1]
     interleave(plain_ref, kappa_ref)
@@ -391,8 +399,8 @@
     return pl.BlockSpec(memory_space=pltpu.SMEM)
 
 
-def anywhere():
-    return pl.BlockSpec(memory_space=pl.ANY)
+def hbm():
+    return pl.BlockSpec(memory_space=pltpu.HBM)
 
 
 def params(mib):
@@ -411,14 +419,50 @@
     return forward, [(target, source) for source, target in forward]
 
 
-def halos(top, bottom, left, right):
+def join(north, south, left, right):
+    halo = left.shape[1]
+    right = jnp.concatenate([north[:, -halo:], right, south[:, -halo:]], axis=0)
+    left = jnp.concatenate([north[:, :halo], left, south[:, :halo]], axis=0)
+    return left, right
+
+
+def join_kernel(north_ref, south_ref, _, __, left_ref, right_ref, sems):
+    count, tile_cols, _ = north_ref.shape
+    total, halo, _ = left_ref.shape
+    copies = []
+    for target, cols in ((left_ref, 0), (right_ref, tile_cols - halo)):
+        for source, row in ((north_ref, 0), (south_ref, total - count)):
+            copies.append(
+                pltpu.make_async_copy(
+                    source.at[:, pl.ds(cols, halo)], target.at[pl.ds(row, count)],
+                    sems.at[len(copies)],
+                )
+            )
+    for copy in copies:
+        copy.start()
+    for copy in copies:
+        copy.wait()
+
+
+def join_in_place(north, south, left, right):
+    return pl.pallas_call(
+        join_kernel,
+        out_shape=tuple(jax.ShapeDtypeStruct(x.shape, x.dtype) for x in (left, right)),
+        in_specs=[vmem()] * 2 + [hbm()] * 2,
+        out_specs=(hbm(), hbm()),
+        input_output_aliases={2: 0, 3: 1},
+        scratch_shapes=[pltpu.SemaphoreType.DMA((4,))],
+        compiler_params=params(2),
+        name="join",
+    )(north, south, left, right)
+
+
+def halos(top, bottom, left, right, join):
     lat_up, lat_down = neighbours("lat", False)
     lon_up, lon_down = neighbours("lon", True)
-    halo = left.shape[1]
     north = lax.ppermute(bottom, "lat", lat_up)
     south = lax.ppermute(top, "lat", lat_down)
-    rights = jnp.concatenate([north[:, -halo:], right, south[:, -halo:]], axis=0)
-    lefts = jnp.concatenate([north[:, :halo], left, south[:, :halo]], axis=0)
+    lefts, rights = join(north, south, left, right)
     west = lax.ppermute(rights, "lon", lon_up)
     east = lax.ppermute(lefts, "lon", lon_down)
     return north, south, west, east
@@ -463,13 +507,14 @@
 
     kappa_halos = halos(
         encode_kappa(diffusivity[:halo]), encode_kappa(diffusivity[-halo:]),
-        encode_kappa(diffusivity[:, :halo]), encode_kappa(diffusivity[:, -halo:])
+        encode_kappa(diffusivity[:, :halo]), encode_kappa(diffusivity[:, -halo:]), join
     )
     absorb_wide = pl.pallas_call(
         spread_kernel,
         out_shape=jax.ShapeDtypeStruct((levels, channels, lanes), f32),
-        in_specs=[vmem()],
-        out_specs=vmem(),
+        grid=(levels // 16,),
+        in_specs=[pl.BlockSpec((levels, channels), lambda i: (0, 0))],
+        out_specs=pl.BlockSpec((16, channels, lanes), lambda i: (i, 0, 0)),
         scratch_shapes=[pltpu.VMEM((channels, levels), f32)],
         compiler_params=params(60),
         cost_estimate=cost(levels * channels * lanes, 0, 4 * levels * channels * lanes),
@@ -484,10 +529,10 @@
             jax.ShapeDtypeStruct((tile_rows, tile_cols, levels), f32),
             jax.ShapeDtypeStruct((halo + 1, tile_cols, levels), jnp.int16),
             jax.ShapeDtypeStruct((halo + 1, tile_cols, levels), jnp.int16),
-            jax.ShapeDtypeStruct((tile_rows + 1, halo, levels), jnp.int16),
-            jax.ShapeDtypeStruct((tile_rows + 1, halo, levels), jnp.int16),
+            jax.ShapeDtypeStruct((tile_rows + 2 * halo + 3, halo, levels), jnp.int16),
+            jax.ShapeDtypeStruct((tile_rows + 2 * halo + 3, halo, levels), jnp.int16),
         ),
-        in_specs=[vmem()] * 2 + [anywhere()] + [vmem()] * 2 + [anywhere()] * 2,
+        in_specs=[vmem()] * 2 + [hbm()] + [vmem()] * 2 + [hbm()] * 2,
         out_specs=(vmem(),) * 6,
         scratch_shapes=[
             pltpu.SMEM((dev_count, channels), f32),
@@ -518,7 +563,7 @@
         inverse_variance.reshape(1, channels), *kappa_halos[2:]
     )
 
-    field_halos = halos(top, bottom, left, right)
+    field_halos = halos(top, bottom, left, right, join_in_place)
     lat_at = lax.axis_index("lat")
     inside = jnp.stack([lat_at > 0, lat_at < lat_count - 1]).astype(f32)
     height, breadth = tile_rows + 2 * halo, tile_cols + 2 * halo
@@ -529,9 +574,11 @@
     east, south = pl.pallas_call(
         functools.partial(edges_kernel, halo),
         out_shape=(jax.ShapeDtypeStruct(mixed, f32),) * 2,
-        in_specs=[smem()] + [vmem()] * 5,
+        in_specs=[smem()] + [vmem()] * 3 + [hbm()] * 2,
         out_specs=(vmem(),) * 2,
-        scratch_shapes=[plain, pltpu.VMEM(mixed, f32)],
+        scratch_shapes=[plain, pltpu.VMEM(mixed, f32)]
+        + [pltpu.VMEM((height, halo, levels), jnp.int16)] * 2
+        + [pltpu.SemaphoreType.DMA((2,))],
         compiler_params=params(22),
         cost_estimate=cost(4 * height * breadth * levels, 0, 12 * cells * levels),
         name="edges",

time: 123 us -> 120 us (0.976)
  other arithmetic: 3.65 us -> 0.47 us
  waiting for transfers between devices: 7.83 us -> 11 us
  Pallas kernels: 77.1 us -> 74.9 us
    concatenate x4 -> x2, other arithmetic: 3.21 us -> 0.03 us  [the longest x1 0.02 us: join(): right = jnp.concatenate([north[:, -halo:], right, south[:, -halo:]], axis=0)]
    pallas_call x1, Pallas kernels: 50.9 us -> 48.6 us  [local(): pl.pallas_call(functools.partial(column_kernel, capacity, halo), out_shap...]
    ppermute x2, waiting for transfers between devices: 0.85 us -> 2.62 us  [halos(): north = lax.ppermute(bottom, 'lat', lat_up)]
  transfers between devices with their start and end apart: 10 -> 10, of which waited for: 6 -> 5; matrix products, arithmetic and copies ran while one was open for 3% -> 0% of each run, Pallas kernels for 17% -> 18%
where the time goes in v1:
time: 120 us; the launch traced here: 119 us
  Pallas kernels  74.9 us (62%)
  starting transfers between devices  29.9 us (25%)
  waiting for transfers between devices  11 us (9%)
  local copies, waits for them, and re-layouts  2 us (2%)
    pallas_call x1, Pallas kernels, local(): pl.pallas_call(functools.partial(column_kernel, capacity, halo), out_shap...  48.6 us
    pallas_call x1, Pallas kernels, local(): pl.pallas_call(functools.partial(relax_kernel, halo), out_shape=jax.Shape...  10.7 us
    ppermute x2, starting transfers between devices, halos(): east = lax.ppermute(lefts, 'lon', lon_down)  7.53 us
    all_to_all x1, starting transfers between devices, local(): lax.all_to_all(send, ('lat', 'lon'), split_axis=0, concat_axis=0, tiled=T...  7.13 us
    ppermute x2, starting transfers between devices, halos(): north = lax.ppermute(bottom, 'lat', lat_up)  6.87 us
    pallas_call x1, Pallas kernels, local(): pl.pallas_call(spread_kernel, out_shape=jax.ShapeDtypeStruct((levels, cha...  6.84 us
    ppermute x2, waiting for transfers between devices, halos(): south = lax.ppermute(top, 'lat', lat_down)  6.68 us
    ppermute x2, starting transfers between devices, halos(): south = lax.ppermute(top, 'lat', lat_down)  4.15 us
  transfers between devices with their start and end apart: 10, of which 5 were waited for; matrix products, arithmetic and copies ran while one was open for 0% of the time, Pallas kernels for 18%

profile of v1, /device:TPU:1, one launch (start us, length us, event | category | flops | bytes accessed | tf_op | source)
XLA Modules:
  0.0 119.0 jit_solution(13992295453078521521)
XLA Ops:
  0.6 3.5 %pack.1 = (f32[32,40,128]{2,1,0:T(8,128)}, s32[1,512]{1,0:T(1,128)}) custom-call(s32[1]{0:T(128)} %bitcast.lane_ref, s32[1,512]{1,0:T(1,128)} %bitcast.11, s32[1,512]{1,0:T(1,128)} %bitcast.12, f32[4,512]{1,0:T(4,128)} %bitcast.10, f32[512,128]{1,0:T(8,128)} %observed_ref.3, s32[512,128]{1,0:T(8,128)} %accept_ref.1), custom_call_target="tpu_custom_call" | custom-call | flops 402653184 | bytes 1572864 | tf_op jit(solution)/shard_map/pack/pallas_call | solution.py:490
  4.2 7.1 %all-to-all-start = ((f32[32,40,128]{2,1,0:T(8,128)}), f32[32,40,128]{2,1,0:T(8,128)}, u32[]{:S(2)}, u32[]{:S(2)}) async-start(f32[32,40,128]{2,1,0:T(8,128)} %get-tuple-element.15), calls=%async_computation | async-start | bytes 1310720 | tf_op jit(solution)/shard_map/all_to_all | solution.py:506
  11.3 0.2 add_convert_fusion.3
  11.5 2.2 %collective-permute-start.1 = (s16[8,64,128]{2,1,0:T(8,128)(2,1)S(1)}, s16[8,64,128]{2,1,0:T(8,128)(2,1)S(1)}, u32[]{:S(2)}, u32[]{:S(2)}) collective-permute-start(s16[8,64,128]{2,1,0:T(8,128)(2,1)S(1)} %get-tuple-element.29), channel_id=1, source_target_pairs={{8,0},{16,8},{24,16},{9,1},{17,9},{25,17},{10,2},{18,10},{26,18},{... | collective-permute-start | bytes 393224 | tf_op jit(solution)/shard_map/ppermute | solution.py:464
  13.8 3.3 %collective-permute-start = (s16[8,64,128]{2,1,0:T(8,128)(2,1)S(1)}, s16[8,64,128]{2,1,0:T(8,128)(2,1)S(1)}, u32[]{:S(2)}, u32[]{:S(2)}) collective-permute-start(s16[8,64,128]{2,1,0:T(8,128)(2,1)S(1)} %get-tuple-element.28), channel_id=1, source_target_pairs={{0,8},{8,16},{16,24},{1,9},{9,17},{17,25},{2,10},{10,18},{18,26},{... | collective-permute-start | bytes 393224 | tf_op jit(solution)/shard_map/ppermute | solution.py:463
  17.1 0.2 add_convert_fusion
  17.3 2.7 %collective-permute-done.1.south_ref = s16[8,64,128]{2,1,0:T(8,128)(2,1)S(1)} collective-permute-done((s16[8,64,128]{2,1,0:T(8,128)(2,1)S(1)}, s16[8,64,128]{2,1,0:T(8,128)(2,1)S(1)}, u32[]{:S(2)}, u32[]{:S(2)}) %collective-permute-start.1) | collective-permute-done | bytes 131104 | tf_op jit(solution)/shard_map/ppermute | solution.py:464
  20.0 0.6 collective-permute-done.north_ref
  20.6 0.4 collective-permute-start.2
  21.1 3.9 %collective-permute-start.3 = (s16[80,8,128]{2,1,0:T(8,128)(2,1)S(1)}, s16[80,8,128]{2,1,0:T(8,128)(2,1)S(1)}, u32[]{:S(2)}, u32[]{:S(2)}) collective-permute-start(s16[80,8,128]{2,1,0:T(8,128)(2,1)S(1)} %pad_add_fusion.1), channel_id=1, source_target_pairs={{1,0},{2,1},{3,2},{4,3},{5,4},{6,5},{7,6},{0,7},{9,8},{10,9},{11,1... | collective-permute-start | bytes 491528 | tf_op jit(solution)/shard_map/ppermute | solution.py:467
  24.9 6.8 %spread.1.absorb_any = f32[128,128,128]{2,1,0:T(8,128)} custom-call(f32[128,128]{1,0:T(8,128)} %absorb_ref.1), custom_call_target="tpu_custom_call" | custom-call | flops 2097152 | bytes 8388608 | tf_op jit(solution)/shard_map/spread/pallas_call | solution.py:512
  31.8 0.0 collective-permute-done.2.ready_west.west_hbm
  31.8 0.0 collective-permute-done.3.ready_east.east_hbm
  31.8 1.7 %all-to-all-done.recv_ref = f32[32,40,128]{2,1,0:T(8,128)} async-done(((f32[32,40,128]{2,1,0:T(8,128)}), f32[32,40,128]{2,1,0:T(8,128)}, u32[]{:S(2)}, u32[]{:S(2)}) %all-to-all-start) | async-done | bytes 655392 | tf_op jit(solution)/shard_map/all_to_all | solution.py:506
  33.5 48.6 %column.1 = (f32[32,32,128]{2,1,0:T(8,128)}, f32[64,64,128]{2,1,0:T(8,128)}, s16[9,64,128]{2,1,0:T(8,128)(2,1)}, s16[9,64,128]{2,1,0:T(8,128)(2,1)}, s16[83,8,12...) custom-call(f32[32,40,128]{2,1,0:T(8,128)} %all-to-all-done.recv_ref, bf16[64,64,128]{2,1,0:T(8,128)(2,1)} %background_ref.1, ...), custom_call_target="tpu_custom_call" | custom-call | flops 234881024 | bytes 6291456 | tf_op jit(solution)/shard_map/column/pallas_call | solution.py:525
  82.0 3.3 %all-to-all-start.1 = ((f32[32,32,128]{2,1,0:T(8,128)}), f32[32,32,128]{2,1,0:T(8,128)S(1)}, u32[]{:S(2)}, u32[]{:S(2)}) async-start(f32[32,32,128]{2,1,0:T(8,128)} %get-tuple-element.16), calls=%async_computation.1 | async-start | bytes 1048576 | tf_op jit(solution)/shard_map/all_to_all | solution.py:588
  85.3 3.5 %collective-permute-start.4 = (s16[9,64,128]{2,1,0:T(8,128)(2,1)}, s16[9,64,128]{2,1,0:T(8,128)(2,1)S(1)}, u32[]{:S(2)}, u32[]{:S(2)}) collective-permute-start(s16[9,64,128]{2,1,0:T(8,128)(2,1)} %get-tuple-element.18), channel_id=1, source_target_pairs={{0,8},{8,16},{16,24},{1,9},{9,17},{17,25},{2,10},{10,18},{18,26},{... | collective-permute-start | bytes 442376 | tf_op jit(solution)/shard_map/ppermute | solution.py:463
  88.9 1.9 %collective-permute-start.5 = (s16[9,64,128]{2,1,0:T(8,128)(2,1)}, s16[9,64,128]{2,1,0:T(8,128)(2,1)S(1)}, u32[]{:S(2)}, u32[]{:S(2)}) collective-permute-start(s16[9,64,128]{2,1,0:T(8,128)(2,1)} %get-tuple-element.19), channel_id=1, source_target_pairs={{8,0},{16,8},{24,16},{9,1},{17,9},{25,17},{10,2},{18,10},{26,18},{... | collective-permute-start | bytes 442376 | tf_op jit(solution)/shard_map/ppermute | solution.py:464
  90.8 2.0 %collective-permute-done.4.north_ref = s16[9,64,128]{2,1,0:T(8,128)(2,1)S(1)} collective-permute-done((s16[9,64,128]{2,1,0:T(8,128)(2,1)}, s16[9,64,128]{2,1,0:T(8,128)(2,1)S(1)}, u32[]{:S(2)}, u32[]{:S(2)}) %collective-permute-start.4) | collective-permute-done | bytes 147488 | tf_op jit(solution)/shard_map/ppermute | solution.py:463
  92.8 4.0 %collective-permute-done.5.south_ref = s16[9,64,128]{2,1,0:T(8,128)(2,1)S(1)} collective-permute-done((s16[9,64,128]{2,1,0:T(8,128)(2,1)}, s16[9,64,128]{2,1,0:T(8,128)(2,1)S(1)}, u32[]{:S(2)}, u32[]{:S(2)}) %collective-permute-start.5) | collective-permute-done | bytes 147488 | tf_op jit(solution)/shard_map/ppermute | solution.py:464
  96.8 0.6 join.1
  97.4 0.5 collective-permute-start.6
  98.0 3.7 %collective-permute-start.7 = (s16[83,8,128]{2,1,0:T(8,128)(2,1)}, s16[83,8,128]{2,1,0:T(8,128)(2,1)S(1)}, u32[]{:S(2)}, u32[]{:S(2)}) collective-permute-start(s16[83,8,128]{2,1,0:T(8,128)(2,1)} %get-tuple-element.23), channel_id=1, source_target_pairs={{1,0},{2,1},{3,2},{4,3},{5,4},{6,5},{7,6},{0,7},{9,8},{10,9},{11,1... | collective-permute-start | bytes 509960 | tf_op jit(solution)/shard_map/ppermute | solution.py:467
  101.6 0.1 add_convert_fusion.4.inside_ref
  101.7 1.0 copy-done.3
  102.8 0.9 copy-done.5
  103.7 2.7 %edges.1 = (f32[80,10,8,128]{3,2,1,0:T(8,128)S(1)}, f32[80,10,8,128]{3,2,1,0:T(8,128)S(1)}) custom-call(f32[2]{0:T(128)S(1)} %add_convert_fusion.4.inside_ref, f32[64,64,128]{2,1,0:T(8,128)S(1)} %copy-done, s16[8,64,128]{2,1,0:T(8,128)(2,1)S(1)} %collective-permute-done.north_ref, s16[8,64,128]{2,1,0:T(8,128)(2,1)S(1)} %collective-permute-done.1.south_ref, ...), custom_call_target="tpu_custom_call" | custom-call | flops 3276800 | bytes 6291456 | tf_op jit(solution)/shard_map/edges/pallas_call | solution.py:574
  106.4 0.0 collective-permute-done.6.west_ref
  106.4 0.0 collective-permute-done.7.east_side_ref
  106.5 0.0 copy-start.6
  106.5 10.7 %relax.1 = f32[64,64,128]{2,1,0:T(8,128)} custom-call(f32[2]{0:T(128)S(1)} %add_convert_fusion.4.inside_ref, f32[64,64,128]{2,1,0:T(8,128)S(1)} %copy-done.1, s16[9,64,128]{2,1,0:T(8,128)(2,1)S(1)} %collective-permute-done.4.north_ref, s16[9,64,128]{2,1,0:T(8,128)(2,1)S(1)} %collective-permute-done.5.south_ref, ...), custom_call_target="tpu_custom_call" | custom-call | flops 65536000 | bytes 8388608 | tf_op jit(solution)/shard_map/relax/pallas_call | solution.py:602
  117.2 1.8 %depart.1 = f32[512,128]{1,0:T(8,128)} custom-call(s32[1,512]{1,0:T(1,128)S(1)} %copy-done.7, f32[1024,128]{1,0:T(8,128)S(1)} %bitcast.9, f32[512,128]{1,0:T(8,128)S(1)} %copy-done.6), custom_call_target="tpu_custom_call" | custom-call | flops 402653184 | bytes 1048576 | tf_op jit(solution)/shard_map/depart/pallas_call | solution.py:592
  (18 shorter events, 0.1 us)
Async XLA Ops:
  0.6 10.7 %copy-start = (f32[64,64,128]{2,1,0:T(8,128)S(1)}, f32[64,64,128]{2,1,0:T(8,128)}, u32[]{:S(2)}) copy-start(f32[64,64,128]{2,1,0:T(8,128)} %centre_ref.1) | copy-start | bytes 6291460
  4.2 29.3 %all-to-all-start = ((f32[32,40,128]{2,1,0:T(8,128)}), f32[32,40,128]{2,1,0:T(8,128)}, u32[]{:S(2)}, u32[]{:S(2)}) async-start(f32[32,40,128]{2,1,0:T(8,128)} %get-tuple-element.15), calls=%async_computation | async-start | bytes 1310720 | tf_op jit(solution)/shard_map/all_to_all | solution.py:506
  11.5 8.5 %collective-permute-start.1 = (s16[8,64,128]{2,1,0:T(8,128)(2,1)S(1)}, s16[8,64,128]{2,1,0:T(8,128)(2,1)S(1)}, u32[]{:S(2)}, u32[]{:S(2)}) collective-permute-start(s16[8,64,128]{2,1,0:T(8,128)(2,1)S(1)} %get-tuple-element.29), channel_id=1, source_target_pairs={{8,0},{16,8},{24,16},{9,1},{17,9},{25,17},{10,2},{18,10},{26,18},{... | collective-permute-start | bytes 393224 | tf_op jit(solution)/shard_map/ppermute | solution.py:464
  13.8 6.9 %collective-permute-start = (s16[8,64,128]{2,1,0:T(8,128)(2,1)S(1)}, s16[8,64,128]{2,1,0:T(8,128)(2,1)S(1)}, u32[]{:S(2)}, u32[]{:S(2)}) collective-permute-start(s16[8,64,128]{2,1,0:T(8,128)(2,1)S(1)} %get-tuple-element.28), channel_id=1, source_target_pairs={{0,8},{8,16},{16,24},{1,9},{9,17},{17,25},{2,10},{10,18},{18,26},{... | collective-permute-start | bytes 393224 | tf_op jit(solution)/shard_map/ppermute | solution.py:463
  20.6 11.1 %collective-permute-start.2 = (s16[80,8,128]{2,1,0:T(8,128)(2,1)S(1)}, s16[80,8,128]{2,1,0:T(8,128)(2,1)S(1)}, u32[]{:S(2)}, u32[]{:S(2)}) collective-permute-start(s16[80,8,128]{2,1,0:T(8,128)(2,1)S(1)} %pad_add_fusion), channel_id=1, source_target_pairs={{0,1},{1,2},{2,3},{3,4},{4,5},{5,6},{6,7},{7,0},{8,9},{9,10},{10,1... | collective-permute-start | bytes 491528 | tf_op jit(solution)/shard_map/ppermute | solution.py:466
  21.1 10.7 %collective-permute-start.3 = (s16[80,8,128]{2,1,0:T(8,128)(2,1)S(1)}, s16[80,8,128]{2,1,0:T(8,128)(2,1)S(1)}, u32[]{:S(2)}, u32[]{:S(2)}) collective-permute-start(s16[80,8,128]{2,1,0:T(8,128)(2,1)S(1)} %pad_add_fusion.1), channel_id=1, source_target_pairs={{1,0},{2,1},{3,2},{4,3},{5,4},{6,5},{7,6},{0,7},{9,8},{10,9},{11,1... | collective-permute-start | bytes 491528 | tf_op jit(solution)/shard_map/ppermute | solution.py:467
  31.8 1.7 %copy-start.2 = (s16[80,8,128]{2,1,0:T(8,128)(2,1)}, s16[80,8,128]{2,1,0:T(8,128)(2,1)S(1)}, u32[]{:S(2)}) copy-start(s16[80,8,128]{2,1,0:T(8,128)(2,1)S(1)} %collective-permute-done.2.ready_west.west_hbm) | copy-start | bytes 491524
  31.8 1.7 %copy-start.4 = (s16[80,8,128]{2,1,0:T(8,128)(2,1)}, s16[80,8,128]{2,1,0:T(8,128)(2,1)S(1)}, u32[]{:S(2)}) copy-start(s16[80,8,128]{2,1,0:T(8,128)(2,1)S(1)} %collective-permute-done.3.ready_east.east_hbm) | copy-start | bytes 491524
  82.0 35.2 %all-to-all-start.1 = ((f32[32,32,128]{2,1,0:T(8,128)}), f32[32,32,128]{2,1,0:T(8,128)S(1)}, u32[]{:S(2)}, u32[]{:S(2)}) async-start(f32[32,32,128]{2,1,0:T(8,128)} %get-tuple-element.16), calls=%async_computation.1 | async-start | bytes 1048576 | tf_op jit(solution)/shard_map/all_to_all | solution.py:588
  85.3 7.5 %collective-permute-start.4 = (s16[9,64,128]{2,1,0:T(8,128)(2,1)}, s16[9,64,128]{2,1,0:T(8,128)(2,1)S(1)}, u32[]{:S(2)}, u32[]{:S(2)}) collective-permute-start(s16[9,64,128]{2,1,0:T(8,128)(2,1)} %get-tuple-element.18), channel_id=1, source_target_pairs={{0,8},{8,16},{16,24},{1,9},{9,17},{17,25},{2,10},{10,18},{18,26},{... | collective-permute-start | bytes 442376 | tf_op jit(solution)/shard_map/ppermute | solution.py:463
  88.9 7.9 %collective-permute-start.5 = (s16[9,64,128]{2,1,0:T(8,128)(2,1)}, s16[9,64,128]{2,1,0:T(8,128)(2,1)S(1)}, u32[]{:S(2)}, u32[]{:S(2)}) collective-permute-start(s16[9,64,128]{2,1,0:T(8,128)(2,1)} %get-tuple-element.19), channel_id=1, source_target_pairs={{8,0},{16,8},{24,16},{9,1},{17,9},{25,17},{10,2},{18,10},{26,18},{... | collective-permute-start | bytes 442376 | tf_op jit(solution)/shard_map/ppermute | solution.py:464
  97.4 9.0 %collective-permute-start.6 = (s16[83,8,128]{2,1,0:T(8,128)(2,1)}, s16[83,8,128]{2,1,0:T(8,128)(2,1)S(1)}, u32[]{:S(2)}, u32[]{:S(2)}) collective-permute-start(s16[83,8,128]{2,1,0:T(8,128)(2,1)} %get-tuple-element.22), channel_id=1, source_target_pairs={{0,1},{1,2},{2,3},{3,4},{4,5},{5,6},{6,7},{7,0},{8,9},{9,10},{10,1... | collective-permute-start | bytes 509960 | tf_op jit(solution)/shard_map/ppermute | solution.py:466
  98.0 8.5 %collective-permute-start.7 = (s16[83,8,128]{2,1,0:T(8,128)(2,1)}, s16[83,8,128]{2,1,0:T(8,128)(2,1)S(1)}, u32[]{:S(2)}, u32[]{:S(2)}) collective-permute-start(s16[83,8,128]{2,1,0:T(8,128)(2,1)} %get-tuple-element.23), channel_id=1, source_target_pairs={{1,0},{2,1},{3,2},{4,3},{5,4},{6,5},{7,6},{0,7},{9,8},{10,9},{11,1... | collective-permute-start | bytes 509960 | tf_op jit(solution)/shard_map/ppermute | solution.py:467
  101.6 4.8 %copy-start.1 = (f32[64,64,128]{2,1,0:T(8,128)S(1)}, f32[64,64,128]{2,1,0:T(8,128)}, u32[]{:S(2)}) copy-start(f32[64,64,128]{2,1,0:T(8,128)} %get-tuple-element.17.centre_ref) | copy-start | bytes 6291460
  101.7 1.1 copy-start.3
  102.8 0.9 copy-start.5
  106.5 10.7 %copy-start.6 = (f32[512,128]{1,0:T(8,128)S(1)}, f32[512,128]{1,0:T(8,128)}, u32[]{:S(2)}) copy-start(f32[512,128]{1,0:T(8,128)} %observed_ref.3) | copy-start | bytes 786436
  106.5 10.7 %copy-start.7 = (s32[1,512]{1,0:T(1,128)S(1)}, s32[1,512]{1,0:T(1,128)}, u32[]{:S(2)}) copy-start(s32[1,512]{1,0:T(1,128)} %get-tuple-element.14.slot_ref) | copy-start | bytes 6148

commit v2 on v1

--- a/solution.py
+++ b/solution.py
@@ -114,8 +114,15 @@
 
     copy = pltpu.make_async_copy(recv_ref.at[:, capacity, :], base_ref, sem)
     copy.start()
-    absorb_copy = pltpu.make_async_copy(absorb_any, absorb_b, absorb_sem)
-    absorb_copy.start()
+
+    def absorb_copy(c):
+        some = pl.ds(pl.multiple_of(c * wide, wide), wide)
+        return pltpu.make_async_copy(
+            absorb_any.at[:, some, :], absorb_b.at[:, some, :], absorb_sem.at[c]
+        )
+
+    for c in range(channels // wide):
+        absorb_copy(c).start()
 
     cells_ref[...] = background_ref[...].reshape(cells, levels).astype(jnp.float32)
     slope_b[...] = jnp.broadcast_to(sensitivity_ref[...] * LOG2E, (lanes, channels)).T
@@ -144,7 +151,6 @@
         return carry
 
     lax.fori_loop(0, lanes // 8, gather_first, 0)
-    absorb_copy.wait()
 
     def block(f, carry):
         before = jnp.maximum(f - 1, 0)
@@ -161,6 +167,10 @@
         push_ref[...] = jnp.zeros_like(push_ref)
 
         def some_channels(c, carry):
+            @pl.when(f == 0)
+            def _():
+                absorb_copy(c).wait()
+
             at = pl.multiple_of(c * wide, wide)
             slope = slope_b[pl.ds(at, wide), :]
             scale = slope * (LN2 * LN2)
@@ -285,15 +295,8 @@
     return whole * KAPPA_STEP + KAPPA_LOW
 
 
-def interleave(plain_ref, target_ref):
-    stretch = target_ref.shape[1]
-
-    def row(i, carry):
-        for t in range(stretch):
-            target_ref[i, t] = plain_ref[i, pl.ds(t, 8, stride=stretch), :]
-        return carry
-
-    lax.fori_loop(0, plain_ref.shape[0], row, 0)
+def mixed_row(plain_ref, i, stretch):
+    return jnp.stack([plain_ref[i, pl.ds(t, 8, stride=stretch), :] for t in range(stretch)])
 
 
 def eastward(x):
@@ -306,7 +309,7 @@
 
 def edges_kernel(
     halo, inside_ref, centre_ref, north_ref, south_ref, west_hbm, east_hbm, east_ref,
-    south_edge_ref, plain_ref, kappa_ref, west_ref, east_side_ref, sems
+    south_edge_ref, plain_ref, west_ref, east_side_ref, sems
 ):
     copies = [
         pltpu.make_async_copy(west_hbm, west_ref, sems.at[0]),
@@ -327,15 +330,15 @@
     plain_ref[:, halo + tile_cols :] = decode_kappa(east_side_ref[...])
     plain_ref[low] = plain_ref[low] * inside_ref[0]
     plain_ref[end] = plain_ref[end] * inside_ref[1]
-    interleave(plain_ref, kappa_ref)
-
-    def edges(i, carry):
-        here = kappa_ref[i]
+    stretch = east_ref.shape[1]
+
+    def edges(i, here):
+        below = mixed_row(plain_ref, i + 1, stretch)
         east_ref[i] = 0.5 * (here + eastward(here))
-        south_edge_ref[i] = 0.5 * (here + kappa_ref[jnp.minimum(i + 1, height - 1)])
-        return carry
-
-    lax.fori_loop(0, height, edges, 0)
+        south_edge_ref[i] = 0.5 * (here + below)
+        return below
+
+    lax.fori_loop(0, height - 1, edges, mixed_row(plain_ref, 0, stretch), unroll=2)
 
 
 def relax_kernel(
@@ -346,15 +349,17 @@
     height = tile_rows + 2 * halo
     stretch = first_ref.shape[1]
     lay(halo, plain_ref, centre_ref, north_ref, south_ref, west_ref, east_side_ref)
-    interleave(plain_ref, first_ref)
-
-    source, target = first_ref, second_ref
+
+    source, target = None, second_ref
     for step in range(1, halo + 1):
         last = step == halo
 
-        def row(i, carry, scale=None, source=source, target=target, last=last):
+        def read(i, source=source):
+            return mixed_row(plain_ref, i, stretch) if source is None else source[i]
+
+        def row(i, carry, scale=None, read=read, target=target, last=last):
             here, from_north = carry
-            below = source[i + 1]
+            below = read(i + 1)
             to_east = east_ref[i] * (eastward(here) - here)
             from_south = south_edge_ref[i] * (below - here)
             value = here + (to_east - westward(to_east)) + (from_south - from_north)
@@ -367,8 +372,8 @@
                 target[i] = value
             return below, from_south
 
-        here = source[step]
-        carry = (here, south_edge_ref[step - 1] * (here - source[step - 1]))
+        here = read(step)
+        carry = (here, south_edge_ref[step - 1] * (here - read(step - 1)))
         carry = lax.fori_loop(
             step, halo, functools.partial(row, scale=inside_ref[0]), carry, unroll=True
         )
@@ -377,7 +382,7 @@
             halo + tile_rows, height - step, functools.partial(row, scale=inside_ref[1]), carry,
             unroll=True,
         )
-        source, target = target, source
+        source, target = target, first_ref if target is second_ref else second_ref
     out_ref[...] = plain_ref[halo : halo + tile_rows, halo : halo + tile_cols, :]
 
 
@@ -460,8 +465,8 @@
 def halos(top, bottom, left, right, join):
     lat_up, lat_down = neighbours("lat", False)
     lon_up, lon_down = neighbours("lon", True)
+    south = lax.ppermute(top, "lat", lat_down)
     north = lax.ppermute(bottom, "lat", lat_up)
-    south = lax.ppermute(top, "lat", lat_down)
     lefts, rights = join(north, south, left, right)
     west = lax.ppermute(rights, "lon", lon_up)
     east = lax.ppermute(lefts, "lon", lon_down)
@@ -537,7 +542,7 @@
         scratch_shapes=[
             pltpu.SMEM((dev_count, channels), f32),
             pltpu.SemaphoreType.DMA,
-            pltpu.SemaphoreType.DMA,
+            pltpu.SemaphoreType.DMA((channels // wide,)),
             pltpu.VMEM((cells, levels), f32),
             pltpu.VMEM((levels, channels, lanes), f32),
             pltpu.VMEM((channels, lanes), f32),
@@ -576,7 +581,7 @@
         out_shape=(jax.ShapeDtypeStruct(mixed, f32),) * 2,
         in_specs=[smem()] + [vmem()] * 3 + [hbm()] * 2,
         out_specs=(vmem(),) * 2,
-        scratch_shapes=[plain, pltpu.VMEM(mixed, f32)]
+        scratch_shapes=[plain]
         + [pltpu.VMEM((height, halo, levels), jnp.int16)] * 2
         + [pltpu.SemaphoreType.DMA((2,))],
         compiler_params=params(22),

time: 120 us -> 116 us (0.967)
  Pallas kernels: 74.9 us -> 71.8 us
    pallas_call x1, Pallas kernels: 48.6 us -> 46.8 us  [local(): pl.pallas_call(functools.partial(column_kernel, capacity, halo), out_shap...]
  transfers between devices with their start and end apart: 10 -> 10, of which waited for: 5 -> 5; matrix products, arithmetic and copies ran while one was open for 0% -> 0% of each run, Pallas kernels for 18% -> 17%
where the time goes in v2:
time: 116 us
  Pallas kernels  71.8 us (62%)
  starting transfers between devices  29.9 us (26%)
  waiting for transfers between devices  11 us (9%)
  local copies, waits for them, and re-layouts  2 us (2%)
    pallas_call x1, Pallas kernels, local(): pl.pallas_call(functools.partial(column_kernel, capacity, halo), out_shap...  46.8 us
    pallas_call x1, Pallas kernels, local(): pl.pallas_call(functools.partial(relax_kernel, halo), out_shape=jax.Shape...  10.1 us
    ppermute x2, starting transfers between devices, halos(): east = lax.ppermute(lefts, 'lon', lon_down)  7.53 us
    all_to_all x1, starting transfers between devices, local(): lax.all_to_all(send, ('lat', 'lon'), split_axis=0, concat_axis=0, tiled=T...  7.13 us
    ppermute x2, starting transfers between devices, halos(): north = lax.ppermute(bottom, 'lat', lat_up)  6.87 us
    pallas_call x1, Pallas kernels, local(): pl.pallas_call(spread_kernel, out_shape=jax.ShapeDtypeStruct((levels, cha...  6.84 us
    ppermute x2, waiting for transfers between devices, halos(): south = lax.ppermute(top, 'lat', lat_down)  6.68 us
    ppermute x2, starting transfers between devices, halos(): south = lax.ppermute(top, 'lat', lat_down)  4.15 us
  transfers between devices with their start and end apart: 10, of which 5 were waited for; matrix products, arithmetic and copies ran while one was open for 0% of the time, Pallas kernels for 17%

profile of v2, /device:TPU:1, one launch (start us, length us, event | category | flops | bytes accessed | tf_op | source)
XLA Modules:
  0.0 115.9 jit_solution(7265781313239580129)
XLA Ops:
  0.6 3.5 %pack.1 = (f32[32,40,128]{2,1,0:T(8,128)}, s32[1,512]{1,0:T(1,128)}) custom-call(s32[1]{0:T(128)} %bitcast.lane_ref, s32[1,512]{1,0:T(1,128)} %bitcast.11, s32[1,512]{1,0:T(1,128)} %bitcast.12, f32[4,512]{1,0:T(4,128)} %bitcast.10, f32[512,128]{1,0:T(8,128)} %observed_ref.3, s32[512,128]{1,0:T(8,128)} %accept_ref.1), custom_call_target="tpu_custom_call" | custom-call | flops 402653184 | bytes 1572864 | tf_op jit(solution)/shard_map/pack/pallas_call | solution.py:495
  4.2 7.1 %all-to-all-start = ((f32[32,40,128]{2,1,0:T(8,128)}), f32[32,40,128]{2,1,0:T(8,128)}, u32[]{:S(2)}, u32[]{:S(2)}) async-start(f32[32,40,128]{2,1,0:T(8,128)} %get-tuple-element.15), calls=%async_computation | async-start | bytes 1310720 | tf_op jit(solution)/shard_map/all_to_all | solution.py:511
  11.3 0.2 add_convert_fusion.3
  11.5 2.2 %collective-permute-start.1 = (s16[8,64,128]{2,1,0:T(8,128)(2,1)S(1)}, s16[8,64,128]{2,1,0:T(8,128)(2,1)S(1)}, u32[]{:S(2)}, u32[]{:S(2)}) collective-permute-start(s16[8,64,128]{2,1,0:T(8,128)(2,1)S(1)} %get-tuple-element.29), channel_id=1, source_target_pairs={{8,0},{16,8},{24,16},{9,1},{17,9},{25,17},{10,2},{18,10},{26,18},{... | collective-permute-start | bytes 393224 | tf_op jit(solution)/shard_map/ppermute | solution.py:468
  13.8 3.3 %collective-permute-start = (s16[8,64,128]{2,1,0:T(8,128)(2,1)S(1)}, s16[8,64,128]{2,1,0:T(8,128)(2,1)S(1)}, u32[]{:S(2)}, u32[]{:S(2)}) collective-permute-start(s16[8,64,128]{2,1,0:T(8,128)(2,1)S(1)} %get-tuple-element.28), channel_id=1, source_target_pairs={{0,8},{8,16},{16,24},{1,9},{9,17},{17,25},{2,10},{10,18},{18,26},{... | collective-permute-start | bytes 393224 | tf_op jit(solution)/shard_map/ppermute | solution.py:469
  17.1 0.2 add_convert_fusion
  17.3 2.7 %collective-permute-done.1.south_ref = s16[8,64,128]{2,1,0:T(8,128)(2,1)S(1)} collective-permute-done((s16[8,64,128]{2,1,0:T(8,128)(2,1)S(1)}, s16[8,64,128]{2,1,0:T(8,128)(2,1)S(1)}, u32[]{:S(2)}, u32[]{:S(2)}) %collective-permute-start.1) | collective-permute-done | bytes 131104 | tf_op jit(solution)/shard_map/ppermute | solution.py:468
  20.0 0.6 collective-permute-done.north_ref
  20.6 0.4 collective-permute-start.2
  21.1 3.9 %collective-permute-start.3 = (s16[80,8,128]{2,1,0:T(8,128)(2,1)S(1)}, s16[80,8,128]{2,1,0:T(8,128)(2,1)S(1)}, u32[]{:S(2)}, u32[]{:S(2)}) collective-permute-start(s16[80,8,128]{2,1,0:T(8,128)(2,1)S(1)} %pad_add_fusion.1), channel_id=1, source_target_pairs={{1,0},{2,1},{3,2},{4,3},{5,4},{6,5},{7,6},{0,7},{9,8},{10,9},{11,1... | collective-permute-start | bytes 491528 | tf_op jit(solution)/shard_map/ppermute | solution.py:472
  24.9 6.8 %spread.1.absorb_any = f32[128,128,128]{2,1,0:T(8,128)} custom-call(f32[128,128]{1,0:T(8,128)} %absorb_ref.1), custom_call_target="tpu_custom_call" | custom-call | flops 2097152 | bytes 8388608 | tf_op jit(solution)/shard_map/spread/pallas_call | solution.py:517
  31.8 0.0 collective-permute-done.2.ready_west.west_hbm
  31.8 0.0 collective-permute-done.3.ready_east.east_hbm
  31.8 1.7 %all-to-all-done.recv_ref = f32[32,40,128]{2,1,0:T(8,128)} async-done(((f32[32,40,128]{2,1,0:T(8,128)}), f32[32,40,128]{2,1,0:T(8,128)}, u32[]{:S(2)}, u32[]{:S(2)}) %all-to-all-start) | async-done | bytes 655392 | tf_op jit(solution)/shard_map/all_to_all | solution.py:511
  33.5 46.8 %column.1 = (f32[32,32,128]{2,1,0:T(8,128)}, f32[64,64,128]{2,1,0:T(8,128)}, s16[9,64,128]{2,1,0:T(8,128)(2,1)}, s16[9,64,128]{2,1,0:T(8,128)(2,1)}, s16[83,8,12...) custom-call(f32[32,40,128]{2,1,0:T(8,128)} %all-to-all-done.recv_ref, bf16[64,64,128]{2,1,0:T(8,128)(2,1)} %background_ref.1, ...), custom_call_target="tpu_custom_call" | custom-call | flops 234881024 | bytes 6291456 | tf_op jit(solution)/shard_map/column/pallas_call | solution.py:530
  80.3 3.3 %all-to-all-start.1 = ((f32[32,32,128]{2,1,0:T(8,128)}), f32[32,32,128]{2,1,0:T(8,128)S(1)}, u32[]{:S(2)}, u32[]{:S(2)}) async-start(f32[32,32,128]{2,1,0:T(8,128)} %get-tuple-element.16), calls=%async_computation.1 | async-start | bytes 1048576 | tf_op jit(solution)/shard_map/all_to_all | solution.py:593
  83.6 3.5 %collective-permute-start.4 = (s16[9,64,128]{2,1,0:T(8,128)(2,1)}, s16[9,64,128]{2,1,0:T(8,128)(2,1)S(1)}, u32[]{:S(2)}, u32[]{:S(2)}) collective-permute-start(s16[9,64,128]{2,1,0:T(8,128)(2,1)} %get-tuple-element.18), channel_id=1, source_target_pairs={{0,8},{8,16},{16,24},{1,9},{9,17},{17,25},{2,10},{10,18},{18,26},{... | collective-permute-start | bytes 442376 | tf_op jit(solution)/shard_map/ppermute | solution.py:469
  87.1 1.9 %collective-permute-start.5 = (s16[9,64,128]{2,1,0:T(8,128)(2,1)}, s16[9,64,128]{2,1,0:T(8,128)(2,1)S(1)}, u32[]{:S(2)}, u32[]{:S(2)}) collective-permute-start(s16[9,64,128]{2,1,0:T(8,128)(2,1)} %get-tuple-element.19), channel_id=1, source_target_pairs={{8,0},{16,8},{24,16},{9,1},{17,9},{25,17},{10,2},{18,10},{26,18},{... | collective-permute-start | bytes 442376 | tf_op jit(solution)/shard_map/ppermute | solution.py:468
  89.0 2.0 %collective-permute-done.4.north_ref = s16[9,64,128]{2,1,0:T(8,128)(2,1)S(1)} collective-permute-done((s16[9,64,128]{2,1,0:T(8,128)(2,1)}, s16[9,64,128]{2,1,0:T(8,128)(2,1)S(1)}, u32[]{:S(2)}, u32[]{:S(2)}) %collective-permute-start.4) | collective-permute-done | bytes 147488 | tf_op jit(solution)/shard_map/ppermute | solution.py:469
  91.0 4.0 %collective-permute-done.5.south_ref = s16[9,64,128]{2,1,0:T(8,128)(2,1)S(1)} collective-permute-done((s16[9,64,128]{2,1,0:T(8,128)(2,1)}, s16[9,64,128]{2,1,0:T(8,128)(2,1)S(1)}, u32[]{:S(2)}, u32[]{:S(2)}) %collective-permute-start.5) | collective-permute-done | bytes 147488 | tf_op jit(solution)/shard_map/ppermute | solution.py:468
  95.0 0.6 join.1
  95.7 0.5 collective-permute-start.6
  96.2 3.7 %collective-permute-start.7 = (s16[83,8,128]{2,1,0:T(8,128)(2,1)}, s16[83,8,128]{2,1,0:T(8,128)(2,1)S(1)}, u32[]{:S(2)}, u32[]{:S(2)}) collective-permute-start(s16[83,8,128]{2,1,0:T(8,128)(2,1)} %get-tuple-element.23), channel_id=1, source_target_pairs={{1,0},{2,1},{3,2},{4,3},{5,4},{6,5},{7,6},{0,7},{9,8},{10,9},{11,1... | collective-permute-start | bytes 509960 | tf_op jit(solution)/shard_map/ppermute | solution.py:472
  99.9 0.1 add_convert_fusion.4.inside_ref
  100.0 1.0 copy-done.3
  101.0 0.9 copy-done.5
  101.9 2.0 %edges.1 = (f32[80,10,8,128]{3,2,1,0:T(8,128)S(1)}, f32[80,10,8,128]{3,2,1,0:T(8,128)S(1)}) custom-call(f32[2]{0:T(128)S(1)} %add_convert_fusion.4.inside_ref, f32[64,64,128]{2,1,0:T(8,128)S(1)} %copy-done, s16[8,64,128]{2,1,0:T(8,128)(2,1)S(1)} %collective-permute-done.north_ref, s16[8,64,128]{2,1,0:T(8,128)(2,1)S(1)} %collective-permute-done.1.south_ref, ...), custom_call_target="tpu_custom_call" | custom-call | flops 3276800 | bytes 6291456 | tf_op jit(solution)/shard_map/edges/pallas_call | solution.py:579
  103.9 0.0 collective-permute-done.6.west_ref
  104.0 0.0 copy-start.6
  104.0 10.1 %relax.1 = f32[64,64,128]{2,1,0:T(8,128)} custom-call(f32[2]{0:T(128)S(1)} %add_convert_fusion.4.inside_ref, f32[64,64,128]{2,1,0:T(8,128)S(1)} %copy-done.1, s16[9,64,128]{2,1,0:T(8,128)(2,1)S(1)} %collective-permute-done.4.north_ref, s16[9,64,128]{2,1,0:T(8,128)(2,1)S(1)} %collective-permute-done.5.south_ref, ...), custom_call_target="tpu_custom_call" | custom-call | flops 65536000 | bytes 8388608 | tf_op jit(solution)/shard_map/relax/pallas_call | solution.py:607
  114.1 0.0 all-to-all-done.1
  114.1 1.8 %depart.1 = f32[512,128]{1,0:T(8,128)} custom-call(s32[1,512]{1,0:T(1,128)S(1)} %copy-done.7, f32[1024,128]{1,0:T(8,128)S(1)} %bitcast.9, f32[512,128]{1,0:T(8,128)S(1)} %copy-done.6), custom_call_target="tpu_custom_call" | custom-call | flops 402653184 | bytes 1048576 | tf_op jit(solution)/shard_map/depart/pallas_call | solution.py:597
  (18 shorter events, 0.1 us)
Async XLA Ops:
  0.6 10.7 %copy-start = (f32[64,64,128]{2,1,0:T(8,128)S(1)}, f32[64,64,128]{2,1,0:T(8,128)}, u32[]{:S(2)}) copy-start(f32[64,64,128]{2,1,0:T(8,128)} %centre_ref.1) | copy-start | bytes 6291460
  4.2 29.3 %all-to-all-start = ((f32[32,40,128]{2,1,0:T(8,128)}), f32[32,40,128]{2,1,0:T(8,128)}, u32[]{:S(2)}, u32[]{:S(2)}) async-start(f32[32,40,128]{2,1,0:T(8,128)} %get-tuple-element.15), calls=%async_computation | async-start | bytes 1310720 | tf_op jit(solution)/shard_map/all_to_all | solution.py:511
  11.5 8.5 %collective-permute-start.1 = (s16[8,64,128]{2,1,0:T(8,128)(2,1)S(1)}, s16[8,64,128]{2,1,0:T(8,128)(2,1)S(1)}, u32[]{:S(2)}, u32[]{:S(2)}) collective-permute-start(s16[8,64,128]{2,1,0:T(8,128)(2,1)S(1)} %get-tuple-element.29), channel_id=1, source_target_pairs={{8,0},{16,8},{24,16},{9,1},{17,9},{25,17},{10,2},{18,10},{26,18},{... | collective-permute-start | bytes 393224 | tf_op jit(solution)/shard_map/ppermute | solution.py:468
  13.8 6.9 %collective-permute-start = (s16[8,64,128]{2,1,0:T(8,128)(2,1)S(1)}, s16[8,64,128]{2,1,0:T(8,128)(2,1)S(1)}, u32[]{:S(2)}, u32[]{:S(2)}) collective-permute-start(s16[8,64,128]{2,1,0:T(8,128)(2,1)S(1)} %get-tuple-element.28), channel_id=1, source_target_pairs={{0,8},{8,16},{16,24},{1,9},{9,17},{17,25},{2,10},{10,18},{18,26},{... | collective-permute-start | bytes 393224 | tf_op jit(solution)/shard_map/ppermute | solution.py:469
  20.6 11.1 %collective-permute-start.2 = (s16[80,8,128]{2,1,0:T(8,128)(2,1)S(1)}, s16[80,8,128]{2,1,0:T(8,128)(2,1)S(1)}, u32[]{:S(2)}, u32[]{:S(2)}) collective-permute-start(s16[80,8,128]{2,1,0:T(8,128)(2,1)S(1)} %pad_add_fusion), channel_id=1, source_target_pairs={{0,1},{1,2},{2,3},{3,4},{4,5},{5,6},{6,7},{7,0},{8,9},{9,10},{10,1... | collective-permute-start | bytes 491528 | tf_op jit(solution)/shard_map/ppermute | solution.py:471
  21.1 10.7 %collective-permute-start.3 = (s16[80,8,128]{2,1,0:T(8,128)(2,1)S(1)}, s16[80,8,128]{2,1,0:T(8,128)(2,1)S(1)}, u32[]{:S(2)}, u32[]{:S(2)}) collective-permute-start(s16[80,8,128]{2,1,0:T(8,128)(2,1)S(1)} %pad_add_fusion.1), channel_id=1, source_target_pairs={{1,0},{2,1},{3,2},{4,3},{5,4},{6,5},{7,6},{0,7},{9,8},{10,9},{11,1... | collective-permute-start | bytes 491528 | tf_op jit(solution)/shard_map/ppermute | solution.py:472
  31.8 1.7 %copy-start.2 = (s16[80,8,128]{2,1,0:T(8,128)(2,1)}, s16[80,8,128]{2,1,0:T(8,128)(2,1)S(1)}, u32[]{:S(2)}) copy-start(s16[80,8,128]{2,1,0:T(8,128)(2,1)S(1)} %collective-permute-done.2.ready_west.west_hbm) | copy-start | bytes 491524
  31.8 1.7 %copy-start.4 = (s16[80,8,128]{2,1,0:T(8,128)(2,1)}, s16[80,8,128]{2,1,0:T(8,128)(2,1)S(1)}, u32[]{:S(2)}) copy-start(s16[80,8,128]{2,1,0:T(8,128)(2,1)S(1)} %collective-permute-done.3.ready_east.east_hbm) | copy-start | bytes 491524
  80.3 33.8 %all-to-all-start.1 = ((f32[32,32,128]{2,1,0:T(8,128)}), f32[32,32,128]{2,1,0:T(8,128)S(1)}, u32[]{:S(2)}, u32[]{:S(2)}) async-start(f32[32,32,128]{2,1,0:T(8,128)} %get-tuple-element.16), calls=%async_computation.1 | async-start | bytes 1048576 | tf_op jit(solution)/shard_map/all_to_all | solution.py:593
  83.6 7.5 %collective-permute-start.4 = (s16[9,64,128]{2,1,0:T(8,128)(2,1)}, s16[9,64,128]{2,1,0:T(8,128)(2,1)S(1)}, u32[]{:S(2)}, u32[]{:S(2)}) collective-permute-start(s16[9,64,128]{2,1,0:T(8,128)(2,1)} %get-tuple-element.18), channel_id=1, source_target_pairs={{0,8},{8,16},{16,24},{1,9},{9,17},{17,25},{2,10},{10,18},{18,26},{... | collective-permute-start | bytes 442376 | tf_op jit(solution)/shard_map/ppermute | solution.py:469
  87.1 7.9 %collective-permute-start.5 = (s16[9,64,128]{2,1,0:T(8,128)(2,1)}, s16[9,64,128]{2,1,0:T(8,128)(2,1)S(1)}, u32[]{:S(2)}, u32[]{:S(2)}) collective-permute-start(s16[9,64,128]{2,1,0:T(8,128)(2,1)} %get-tuple-element.19), channel_id=1, source_target_pairs={{8,0},{16,8},{24,16},{9,1},{17,9},{25,17},{10,2},{18,10},{26,18},{... | collective-permute-start | bytes 442376 | tf_op jit(solution)/shard_map/ppermute | solution.py:468
  95.7 8.3 %collective-permute-start.6 = (s16[83,8,128]{2,1,0:T(8,128)(2,1)}, s16[83,8,128]{2,1,0:T(8,128)(2,1)S(1)}, u32[]{:S(2)}, u32[]{:S(2)}) collective-permute-start(s16[83,8,128]{2,1,0:T(8,128)(2,1)} %get-tuple-element.22), channel_id=1, source_target_pairs={{0,1},{1,2},{2,3},{3,4},{4,5},{5,6},{6,7},{7,0},{8,9},{9,10},{10,1... | collective-permute-start | bytes 509960 | tf_op jit(solution)/shard_map/ppermute | solution.py:471
  96.2 7.7 %collective-permute-start.7 = (s16[83,8,128]{2,1,0:T(8,128)(2,1)}, s16[83,8,128]{2,1,0:T(8,128)(2,1)S(1)}, u32[]{:S(2)}, u32[]{:S(2)}) collective-permute-start(s16[83,8,128]{2,1,0:T(8,128)(2,1)} %get-tuple-element.23), channel_id=1, source_target_pairs={{1,0},{2,1},{3,2},{4,3},{5,4},{6,5},{7,6},{0,7},{9,8},{10,9},{11,1... | collective-permute-start | bytes 509960 | tf_op jit(solution)/shard_map/ppermute | solution.py:472
  99.9 4.1 %copy-start.1 = (f32[64,64,128]{2,1,0:T(8,128)S(1)}, f32[64,64,128]{2,1,0:T(8,128)}, u32[]{:S(2)}) copy-start(f32[64,64,128]{2,1,0:T(8,128)} %get-tuple-element.17.centre_ref) | copy-start | bytes 6291460
  100.0 1.1 copy-start.3
  101.0 0.9 copy-start.5
  104.0 10.1 %copy-start.6 = (f32[512,128]{1,0:T(8,128)S(1)}, f32[512,128]{1,0:T(8,128)}, u32[]{:S(2)}) copy-start(f32[512,128]{1,0:T(8,128)} %observed_ref.3) | copy-start | bytes 786436
  104.0 10.1 %copy-start.7 = (s32[1,512]{1,0:T(1,128)S(1)}, s32[1,512]{1,0:T(1,128)}, u32[]{:S(2)}) copy-start(s32[1,512]{1,0:T(1,128)} %get-tuple-element.14.slot_ref) | copy-start | bytes 6148

commit v3 on v2

--- a/solution.py
+++ b/solution.py
@@ -98,7 +98,7 @@
 
 def column_kernel(
     capacity, halo, recv_ref, background_ref, absorb_any, sensitivity_ref, inverse_ref,
-    ready_west, ready_east, evolved_ref, field_ref, top_ref, bottom_ref, left_ref, right_ref,
+    evolved_ref, field_ref, top_ref, bottom_ref, left_ref, right_ref,
     base_ref, sem, absorb_sem, cells_ref, absorb_b, slope_b, inverse_b, taken_ref, terms_ref, profile_ref,
     rise_ref, obs_ref, evo_ref, main_ref, side_ref, push_ref, sums_ref
 ):
@@ -537,7 +537,7 @@
             jax.ShapeDtypeStruct((tile_rows + 2 * halo + 3, halo, levels), jnp.int16),
             jax.ShapeDtypeStruct((tile_rows + 2 * halo + 3, halo, levels), jnp.int16),
         ),
-        in_specs=[vmem()] * 2 + [hbm()] + [vmem()] * 2 + [hbm()] * 2,
+        in_specs=[vmem()] * 2 + [hbm()] + [vmem()] * 2,
         out_specs=(vmem(),) * 6,
         scratch_shapes=[
             pltpu.SMEM((dev_count, channels), f32),
@@ -565,7 +565,7 @@
         name="column",
     )(
         recv, background, absorb_wide, sensitivity.reshape(1, channels),
-        inverse_variance.reshape(1, channels), *kappa_halos[2:]
+        inverse_variance.reshape(1, channels)
     )
 
     field_halos = halos(top, bottom, left, right, join_in_place)

time: 116 us -> 123 us (1.060)
  waiting for transfers between devices: 11 us -> 18.5 us
  starting transfers between devices: 29.9 us -> 27.4 us
  other arithmetic: 0.47 us -> 2.52 us
    ppermute x2, waiting for transfers between devices: 0.01 us -> 8.98 us  [halos(): east = lax.ppermute(lefts, 'lon', lon_down)]
    all_to_all x1, waiting for transfers between devices: 1.65 us -> 5.3 us  [local(): lax.all_to_all(send, ('lat', 'lon'), split_axis=0, concat_axis=0, tiled=T...]
    ppermute x2, starting transfers between devices: 7.53 us -> 4.51 us  [halos(): east = lax.ppermute(lefts, 'lon', lon_down)]
    ppermute x2, waiting for transfers between devices: 2.62 us -> 0.06 us  [halos(): north = lax.ppermute(bottom, 'lat', lat_up)]
    ppermute x2, waiting for transfers between devices: 6.68 us -> 4.12 us  [halos(): south = lax.ppermute(top, 'lat', lat_down)]
  transfers between devices with their start and end apart: 10 -> 10, of which waited for: 5 -> 4; matrix products, arithmetic and copies ran while one was open for 0% -> 2% of each run, Pallas kernels for 17% -> 55%
where the time goes in v3:
time: 123 us; the launch traced here: 122 us
  Pallas kernels  72.1 us (59%)
  starting transfers between devices  27.4 us (22%)
  waiting for transfers between devices  18.5 us (15%)
  other arithmetic  2.52 us (2%)
    pallas_call x1, Pallas kernels, local(): pl.pallas_call(functools.partial(column_kernel, capacity, halo), out_shap...  46.8 us
    pallas_call x1, Pallas kernels, local(): pl.pallas_call(functools.partial(relax_kernel, halo), out_shape=jax.Shape...  10.6 us
    ppermute x2, waiting for transfers between devices, halos(): east = lax.ppermute(lefts, 'lon', lon_down)  8.98 us
    ppermute x2, starting transfers between devices, halos(): north = lax.ppermute(bottom, 'lat', lat_up)  7.09 us
    all_to_all x1, starting transfers between devices, local(): lax.all_to_all(send, ('lat', 'lon'), split_axis=0, concat_axis=0, tiled=T...  7.08 us
    pallas_call x1, Pallas kernels, local(): pl.pallas_call(spread_kernel, out_shape=jax.ShapeDtypeStruct((levels, cha...  6.87 us
    all_to_all x1, waiting for transfers between devices, local(): lax.all_to_all(send, ('lat', 'lon'), split_axis=0, concat_axis=0, tiled=T...  5.3 us
    ppermute x2, starting transfers between devices, halos(): east = lax.ppermute(lefts, 'lon', lon_down)  4.51 us
  transfers between devices with their start and end apart: 10, of which 4 were waited for; matrix products, arithmetic and copies ran while one was open for 2% of the time, Pallas kernels for 55%

profile of v3, /device:TPU:1, one launch (start us, length us, event | category | flops | bytes accessed | tf_op | source)
XLA Modules:
  0.0 122.3 jit_solution(8967450126057547729)
XLA Ops:
  0.6 3.5 %pack.1 = (f32[32,40,128]{2,1,0:T(8,128)}, s32[1,512]{1,0:T(1,128)}) custom-call(s32[1]{0:T(128)} %bitcast.lane_ref, s32[1,512]{1,0:T(1,128)} %bitcast.11, s32[1,512]{1,0:T(1,128)} %bitcast.12, f32[4,512]{1,0:T(4,128)} %bitcast.10, f32[512,128]{1,0:T(8,128)} %observed_ref.3, s32[512,128]{1,0:T(8,128)} %accept_ref.1), custom_call_target="tpu_custom_call" | custom-call | flops 402653184 | bytes 1572864 | tf_op jit(solution)/shard_map/pack/pallas_call | solution.py:495
  4.2 7.1 %all-to-all-start = ((f32[32,40,128]{2,1,0:T(8,128)}), f32[32,40,128]{2,1,0:T(8,128)S(1)}, u32[]{:S(2)}, u32[]{:S(2)}) async-start(f32[32,40,128]{2,1,0:T(8,128)} %get-tuple-element.15), calls=%async_computation | async-start | bytes 1310720 | tf_op jit(solution)/shard_map/all_to_all | solution.py:511
  11.3 0.9 add_convert_fusion.2
  12.2 3.5 %collective-permute-start.4 = (s16[8,64,128]{2,1,0:T(8,128)(2,1)}, s16[8,64,128]{2,1,0:T(8,128)(2,1)S(1)}, u32[]{:S(2)}, u32[]{:S(2)}) collective-permute-start(s16[8,64,128]{2,1,0:T(8,128)(2,1)} %get-tuple-element.29), channel_id=1, source_target_pairs={{0,8},{8,16},{16,24},{1,9},{9,17},{17,25},{2,10},{10,18},{18,26},{... | collective-permute-start | bytes 393224 | tf_op jit(solution)/shard_map/ppermute | solution.py:469
  15.7 1.9 %collective-permute-start.5 = (s16[8,64,128]{2,1,0:T(8,128)(2,1)}, s16[8,64,128]{2,1,0:T(8,128)(2,1)S(1)}, u32[]{:S(2)}, u32[]{:S(2)}) collective-permute-start(s16[8,64,128]{2,1,0:T(8,128)(2,1)} %get-tuple-element.28), channel_id=1, source_target_pairs={{8,0},{16,8},{24,16},{9,1},{17,9},{25,17},{10,2},{18,10},{26,18},{... | collective-permute-start | bytes 393224 | tf_op jit(solution)/shard_map/ppermute | solution.py:468
  17.7 6.9 %spread.1.absorb_any = f32[128,128,128]{2,1,0:T(8,128)} custom-call(f32[128,128]{1,0:T(8,128)} %absorb_ref.1), custom_call_target="tpu_custom_call" | custom-call | flops 2097152 | bytes 8388608 | tf_op jit(solution)/shard_map/spread/pallas_call | solution.py:517
  24.5 5.3 %all-to-all-done.recv_ref = f32[32,40,128]{2,1,0:T(8,128)S(1)} async-done(((f32[32,40,128]{2,1,0:T(8,128)}), f32[32,40,128]{2,1,0:T(8,128)S(1)}, u32[]{:S(2)}, u32[]{:S(2)}) %all-to-all-start) | async-done | bytes 655392 | tf_op jit(solution)/shard_map/all_to_all | solution.py:511
  29.8 0.9 copy-done.6
  30.8 46.8 %column.1 = (f32[32,32,128]{2,1,0:T(8,128)}, f32[64,64,128]{2,1,0:T(8,128)}, s16[9,64,128]{2,1,0:T(8,128)(2,1)}, s16[9,64,128]{2,1,0:T(8,128)(2,1)}, s16[83,8,12...) custom-call(f32[32,40,128]{2,1,0:T(8,128)} %copy-done.6, bf16[64,64,128]{2,1,0:T(8,128)(2,1)} %background_ref.1, ...), custom_call_target="tpu_custom_call" | custom-call | flops 234881024 | bytes 6291456 | tf_op jit(solution)/shard_map/column/pallas_call | solution.py:530
  77.6 0.0 copy-start.2
  77.6 3.2 %all-to-all-start.1 = ((f32[32,32,128]{2,1,0:T(8,128)}), f32[32,32,128]{2,1,0:T(8,128)S(1)}, u32[]{:S(2)}, u32[]{:S(2)}) async-start(f32[32,32,128]{2,1,0:T(8,128)} %get-tuple-element.16), calls=%async_computation.1 | async-start | bytes 1048576 | tf_op jit(solution)/shard_map/all_to_all | solution.py:593
  80.8 0.2 add_convert_fusion
  81.0 0.0 collective-permute-done.5.south_ref
  81.0 3.6 %collective-permute-start = (s16[9,64,128]{2,1,0:T(8,128)(2,1)}, s16[9,64,128]{2,1,0:T(8,128)(2,1)S(1)}, u32[]{:S(2)}, u32[]{:S(2)}) collective-permute-start(s16[9,64,128]{2,1,0:T(8,128)(2,1)} %get-tuple-element.18), channel_id=1, source_target_pairs={{0,8},{8,16},{16,24},{1,9},{9,17},{17,25},{2,10},{10,18},{18,26},{... | collective-permute-start | bytes 442376 | tf_op jit(solution)/shard_map/ppermute | solution.py:469
  84.6 1.9 %collective-permute-start.1 = (s16[9,64,128]{2,1,0:T(8,128)(2,1)}, s16[9,64,128]{2,1,0:T(8,128)(2,1)S(1)}, u32[]{:S(2)}, u32[]{:S(2)}) collective-permute-start(s16[9,64,128]{2,1,0:T(8,128)(2,1)} %get-tuple-element.19), channel_id=1, source_target_pairs={{8,0},{16,8},{24,16},{9,1},{17,9},{25,17},{10,2},{18,10},{26,18},{... | collective-permute-start | bytes 442376 | tf_op jit(solution)/shard_map/ppermute | solution.py:468
  86.5 0.7 pad_add_fusion
  87.2 1.2 collective-permute-start.6
  88.4 0.1 collective-permute-done.north_ref
  88.5 4.1 %collective-permute-done.1.south_ref = s16[9,64,128]{2,1,0:T(8,128)(2,1)S(1)} collective-permute-done((s16[9,64,128]{2,1,0:T(8,128)(2,1)}, s16[9,64,128]{2,1,0:T(8,128)(2,1)S(1)}, u32[]{:S(2)}, u32[]{:S(2)}) %collective-permute-start.1) | collective-permute-done | bytes 147488 | tf_op jit(solution)/shard_map/ppermute | solution.py:468
  92.6 0.1 join.1
  92.7 0.6 collective-permute-start.2
  93.2 3.7 %collective-permute-start.3 = (s16[83,8,128]{2,1,0:T(8,128)(2,1)S(1)}, s16[83,8,128]{2,1,0:T(8,128)(2,1)}, u32[]{:S(2)}, u32[]{:S(2)}) collective-permute-start(s16[83,8,128]{2,1,0:T(8,128)(2,1)S(1)} %get-tuple-element.23), channel_id=1, source_target_pairs={{1,0},{2,1},{3,2},{4,3},{5,4},{6,5},{7,6},{0,7},{9,8},{10,9},{11,1... | collective-permute-start | bytes 509960 | tf_op jit(solution)/shard_map/ppermute | solution.py:472
  96.9 0.7 pad_add_fusion.1
  97.6 0.9 collective-permute-start.7
  98.4 0.1 add_convert_fusion.4.inside_ref
  98.5 0.0 collective-permute-done.6.west_hbm
  98.5 9.0 %collective-permute-done.7.east_hbm = s16[80,8,128]{2,1,0:T(8,128)(2,1)} collective-permute-done((s16[80,8,128]{2,1,0:T(8,128)(2,1)}, s16[80,8,128]{2,1,0:T(8,128)(2,1)}, u32[]{:S(2)}, u32[]{:S(2)}) %collective-permute-start.7) | collective-permute-done | bytes 163872 | tf_op jit(solution)/shard_map/ppermute | solution.py:472
  107.5 2.3 %edges.1 = (f32[80,10,8,128]{3,2,1,0:T(8,128)S(1)}, f32[80,10,8,128]{3,2,1,0:T(8,128)S(1)}) custom-call(f32[2]{0:T(128)S(1)} %add_convert_fusion.4.inside_ref, f32[64,64,128]{2,1,0:T(8,128)S(1)} %copy-done, s16[8,64,128]{2,1,0:T(8,128)(2,1)S(1)} %collective-permute-done.4.north_ref, s16[8,64,128]{2,1,0:T(8,128)(2,1)S(1)} %collective-permute-done.5.south_ref, ...), custom_call_target="tpu_custom_call" | custom-call | flops 3276800 | bytes 6291456 | tf_op jit(solution)/shard_map/edges/pallas_call | solution.py:579
  109.9 0.0 copy-start.4
  109.9 10.6 %relax.1 = f32[64,64,128]{2,1,0:T(8,128)} custom-call(f32[2]{0:T(128)S(1)} %add_convert_fusion.4.inside_ref, f32[64,64,128]{2,1,0:T(8,128)S(1)} %copy-done.1, s16[9,64,128]{2,1,0:T(8,128)(2,1)S(1)} %collective-permute-done.north_ref, s16[9,64,128]{2,1,0:T(8,128)(2,1)S(1)} %collective-permute-done.1.south_ref, ...), custom_call_target="tpu_custom_call" | custom-call | flops 65536000 | bytes 8388608 | tf_op jit(solution)/shard_map/relax/pallas_call | solution.py:607
  120.5 0.0 all-to-all-done.1
  120.5 1.8 %depart.1 = f32[512,128]{1,0:T(8,128)} custom-call(s32[1,512]{1,0:T(1,128)S(1)} %copy-done.5, f32[1024,128]{1,0:T(8,128)S(1)} %bitcast.9, f32[512,128]{1,0:T(8,128)S(1)} %copy-done.4), custom_call_target="tpu_custom_call" | custom-call | flops 402653184 | bytes 1048576 | tf_op jit(solution)/shard_map/depart/pallas_call | solution.py:597
  (16 shorter events, 0.0 us)
Async XLA Ops:
  0.6 10.7 %copy-start = (f32[64,64,128]{2,1,0:T(8,128)S(1)}, f32[64,64,128]{2,1,0:T(8,128)}, u32[]{:S(2)}) copy-start(f32[64,64,128]{2,1,0:T(8,128)} %centre_ref.1) | copy-start | bytes 6291460
  4.2 25.6 %all-to-all-start = ((f32[32,40,128]{2,1,0:T(8,128)}), f32[32,40,128]{2,1,0:T(8,128)S(1)}, u32[]{:S(2)}, u32[]{:S(2)}) async-start(f32[32,40,128]{2,1,0:T(8,128)} %get-tuple-element.15), calls=%async_computation | async-start | bytes 1310720 | tf_op jit(solution)/shard_map/all_to_all | solution.py:511
  12.2 74.3 %collective-permute-start.4 = (s16[8,64,128]{2,1,0:T(8,128)(2,1)}, s16[8,64,128]{2,1,0:T(8,128)(2,1)S(1)}, u32[]{:S(2)}, u32[]{:S(2)}) collective-permute-start(s16[8,64,128]{2,1,0:T(8,128)(2,1)} %get-tuple-element.29), channel_id=1, source_target_pairs={{0,8},{8,16},{16,24},{1,9},{9,17},{17,25},{2,10},{10,18},{18,26},{... | collective-permute-start | bytes 393224 | tf_op jit(solution)/shard_map/ppermute | solution.py:469
  15.7 65.3 %collective-permute-start.5 = (s16[8,64,128]{2,1,0:T(8,128)(2,1)}, s16[8,64,128]{2,1,0:T(8,128)(2,1)S(1)}, u32[]{:S(2)}, u32[]{:S(2)}) collective-permute-start(s16[8,64,128]{2,1,0:T(8,128)(2,1)} %get-tuple-element.28), channel_id=1, source_target_pairs={{8,0},{16,8},{24,16},{9,1},{17,9},{25,17},{10,2},{18,10},{26,18},{... | collective-permute-start | bytes 393224 | tf_op jit(solution)/shard_map/ppermute | solution.py:468
  29.8 0.9 copy-start.6
  77.6 15.0 %copy-start.2 = (s16[83,8,128]{2,1,0:T(8,128)(2,1)S(1)}, s16[83,8,128]{2,1,0:T(8,128)(2,1)}, u32[]{:S(2)}) copy-start(s16[83,8,128]{2,1,0:T(8,128)(2,1)} %get-tuple-element.20._) | copy-start | bytes 509956
  77.6 15.0 %copy-start.3 = (s16[83,8,128]{2,1,0:T(8,128)(2,1)S(1)}, s16[83,8,128]{2,1,0:T(8,128)(2,1)}, u32[]{:S(2)}) copy-start(s16[83,8,128]{2,1,0:T(8,128)(2,1)} %get-tuple-element.21.__) | copy-start | bytes 509956
  77.6 42.9 %all-to-all-start.1 = ((f32[32,32,128]{2,1,0:T(8,128)}), f32[32,32,128]{2,1,0:T(8,128)S(1)}, u32[]{:S(2)}, u32[]{:S(2)}) async-start(f32[32,32,128]{2,1,0:T(8,128)} %get-tuple-element.16), calls=%async_computation.1 | async-start | bytes 1048576 | tf_op jit(solution)/shard_map/all_to_all | solution.py:593
  81.0 7.5 %collective-permute-start = (s16[9,64,128]{2,1,0:T(8,128)(2,1)}, s16[9,64,128]{2,1,0:T(8,128)(2,1)S(1)}, u32[]{:S(2)}, u32[]{:S(2)}) collective-permute-start(s16[9,64,128]{2,1,0:T(8,128)(2,1)} %get-tuple-element.18), channel_id=1, source_target_pairs={{0,8},{8,16},{16,24},{1,9},{9,17},{17,25},{2,10},{10,18},{18,26},{... | collective-permute-start | bytes 442376 | tf_op jit(solution)/shard_map/ppermute | solution.py:469
  84.6 8.0 %collective-permute-start.1 = (s16[9,64,128]{2,1,0:T(8,128)(2,1)}, s16[9,64,128]{2,1,0:T(8,128)(2,1)S(1)}, u32[]{:S(2)}, u32[]{:S(2)}) collective-permute-start(s16[9,64,128]{2,1,0:T(8,128)(2,1)} %get-tuple-element.19), channel_id=1, source_target_pairs={{8,0},{16,8},{24,16},{9,1},{17,9},{25,17},{10,2},{18,10},{26,18},{... | collective-permute-start | bytes 442376 | tf_op jit(solution)/shard_map/ppermute | solution.py:468
  87.2 11.3 %collective-permute-start.6 = (s16[80,8,128]{2,1,0:T(8,128)(2,1)}, s16[80,8,128]{2,1,0:T(8,128)(2,1)}, u32[]{:S(2)}, u32[]{:S(2)}) collective-permute-start(s16[80,8,128]{2,1,0:T(8,128)(2,1)} %pad_add_fusion), channel_id=1, source_target_pairs={{0,1},{1,2},{2,3},{3,4},{4,5},{5,6},{6,7},{7,0},{8,9},{9,10},{10,1... | collective-permute-start | bytes 491528 | tf_op jit(solution)/shard_map/ppermute | solution.py:471
  92.7 17.2 %collective-permute-start.2 = (s16[83,8,128]{2,1,0:T(8,128)(2,1)S(1)}, s16[83,8,128]{2,1,0:T(8,128)(2,1)}, u32[]{:S(2)}, u32[]{:S(2)}) collective-permute-start(s16[83,8,128]{2,1,0:T(8,128)(2,1)S(1)} %get-tuple-element.22), channel_id=1, source_target_pairs={{0,1},{1,2},{2,3},{3,4},{4,5},{5,6},{6,7},{7,0},{8,9},{9,10},{10,1... | collective-permute-start | bytes 509960 | tf_op jit(solution)/shard_map/ppermute | solution.py:471
  93.2 16.6 %collective-permute-start.3 = (s16[83,8,128]{2,1,0:T(8,128)(2,1)S(1)}, s16[83,8,128]{2,1,0:T(8,128)(2,1)}, u32[]{:S(2)}, u32[]{:S(2)}) collective-permute-start(s16[83,8,128]{2,1,0:T(8,128)(2,1)S(1)} %get-tuple-element.23), channel_id=1, source_target_pairs={{1,0},{2,1},{3,2},{4,3},{5,4},{6,5},{7,6},{0,7},{9,8},{10,9},{11,1... | collective-permute-start | bytes 509960 | tf_op jit(solution)/shard_map/ppermute | solution.py:472
  97.6 9.9 %collective-permute-start.7 = (s16[80,8,128]{2,1,0:T(8,128)(2,1)}, s16[80,8,128]{2,1,0:T(8,128)(2,1)}, u32[]{:S(2)}, u32[]{:S(2)}) collective-permute-start(s16[80,8,128]{2,1,0:T(8,128)(2,1)} %pad_add_fusion.1), channel_id=1, source_target_pairs={{1,0},{2,1},{3,2},{4,3},{5,4},{6,5},{7,6},{0,7},{9,8},{10,9},{11,1... | collective-permute-start | bytes 491528 | tf_op jit(solution)/shard_map/ppermute | solution.py:472
  98.4 11.4 %copy-start.1 = (f32[64,64,128]{2,1,0:T(8,128)S(1)}, f32[64,64,128]{2,1,0:T(8,128)}, u32[]{:S(2)}) copy-start(f32[64,64,128]{2,1,0:T(8,128)} %get-tuple-element.17.centre_ref) | copy-start | bytes 6291460
  109.9 10.7 %copy-start.4 = (f32[512,128]{1,0:T(8,128)S(1)}, f32[512,128]{1,0:T(8,128)}, u32[]{:S(2)}) copy-start(f32[512,128]{1,0:T(8,128)} %observed_ref.3) | copy-start | bytes 786436
  109.9 10.6 %copy-start.5 = (s32[1,512]{1,0:T(1,128)S(1)}, s32[1,512]{1,0:T(1,128)}, u32[]{:S(2)}) copy-start(s32[1,512]{1,0:T(1,128)} %get-tuple-element.14.slot_ref) | copy-start | bytes 6148

commit v4 on v3

--- a/solution.py
+++ b/solution.py
@@ -24,6 +24,11 @@
     mid = rest.astype(jnp.bfloat16)
     low = (rest - mid.astype(jnp.float32)).astype(jnp.bfloat16)
     return high, mid, low
+
+
+def add_thirds(x):
+    width = x.shape[1] // 3
+    return (x[:, :width] + x[:, width : 2 * width]) + x[:, 2 * width :]
 
 
 def dot_f32(a, b, contract):
@@ -51,15 +56,14 @@
     slot_ref[...] = slot
 
     chosen = jnp.where(accept_ref[...] != 0, observed_ref[...], REJECTED)
-    parts = thirds(chosen)
+    parts = jnp.concatenate(thirds(chosen), axis=1)
     per_chunk = max(1, 128 // capacity)
     chunk = per_chunk * capacity
     for start in range(0, dev_count, per_chunk):
         place = jnp.where(
             iota((chunk, foot_count), 0) + start * capacity == slot, 1.0, 0.0
         ).astype(bf16)
-        rows = [dot_f32(place, part, ((1,), (0,))) for part in parts]
-        rows = (rows[0] + rows[1]) + rows[2]
+        rows = add_thirds(dot_f32(place, parts, ((1,), (0,))))
         send_ref[start : start + per_chunk, :capacity, :] = rows.reshape(
             per_chunk, capacity, channels
         )
@@ -99,7 +103,7 @@
 def column_kernel(
     capacity, halo, recv_ref, background_ref, absorb_any, sensitivity_ref, inverse_ref,
     evolved_ref, field_ref, top_ref, bottom_ref, left_ref, right_ref,
-    base_ref, sem, absorb_sem, cells_ref, absorb_b, slope_b, inverse_b, taken_ref, terms_ref, profile_ref,
+    base_ref, slot_base_ref, sem, absorb_sem, cells_ref, absorb_b, slope_b, inverse_b, taken_ref, terms_ref, profile_ref,
     rise_ref, obs_ref, evo_ref, main_ref, side_ref, push_ref, sums_ref
 ):
     dev_count = recv_ref.shape[0]
@@ -112,7 +116,9 @@
     per_loop = UNROLL * wide * lanes // (levels * channels)
     corners = (0, 1, tile_cols, tile_cols + 1)
 
-    copy = pltpu.make_async_copy(recv_ref.at[:, capacity, :], base_ref, sem)
+    rows = recv_ref[:, capacity, :].reshape(blocks, group, lanes)
+    slot_base_ref[...] = jnp.sum(rows, axis=1).astype(jnp.int32)
+    copy = pltpu.make_async_copy(slot_base_ref, base_ref, sem)
     copy.start()
 
     def absorb_copy(c):
@@ -132,16 +138,13 @@
     terms_ref[...] = jnp.zeros_like(terms_ref)
     copy.wait()
 
-    def base_of(f, at):
-        return base_ref[f * group + lax.div(at, capacity), at].astype(jnp.int32)
-
     def gather(f, at):
-        base = base_of(f, at)
+        base = base_ref[f, at]
         for k, step in enumerate(corners):
             taken_ref[k, pl.ds(at, 1), :] = cells_ref[pl.ds(base + step, 1), :]
 
     def scatter(f, at):
-        base = base_of(f, at)
+        base = base_ref[f, at]
         for k, step in enumerate(corners):
             sums_ref[k, pl.ds(base + step, 1), :] += terms_ref[k, pl.ds(at, 1), :]
 
@@ -390,10 +393,9 @@
     foot_count, _ = observed_ref.shape
     slots = evolved_ref.shape[0]
     slot = slot_ref[...]
-    parts = thirds(evolved_ref[...])
+    parts = jnp.concatenate(thirds(evolved_ref[...]), axis=1)
     chosen = jnp.where(iota((slots, foot_count), 0) == slot, 1.0, 0.0).astype(jnp.bfloat16)
-    rows = [dot_f32(chosen, part, ((0,), (0,))) for part in parts]
-    out_ref[...] = observed_ref[...] - ((rows[0] + rows[1]) + rows[2])
+    out_ref[...] = observed_ref[...] - add_thirds(dot_f32(chosen, parts, ((0,), (0,))))
 
 
 def vmem():
@@ -540,7 +542,8 @@
         in_specs=[vmem()] * 2 + [hbm()] + [vmem()] * 2,
         out_specs=(vmem(),) * 6,
         scratch_shapes=[
-            pltpu.SMEM((dev_count, channels), f32),
+            pltpu.SMEM((slots // lanes, lanes), jnp.int32),
+        pltpu.VMEM((slots // lanes, lanes), jnp.int32),
             pltpu.SemaphoreType.DMA,
             pltpu.SemaphoreType.DMA((channels // wide,)),
             pltpu.VMEM((cells, levels), f32),

time: 123 us -> 122 us (level)
  no operation moved by 1% of the time
where the time goes in v4:
time: 122 us; the launch traced here: 121 us
  Pallas kernels  71.2 us (58%)
  starting transfers between devices  27.5 us (23%)
  waiting for transfers between devices  18.5 us (15%)
  other arithmetic  2.52 us (2%)
    pallas_call x1, Pallas kernels, local(): pl.pallas_call(functools.partial(column_kernel, capacity, halo), out_shap...  46.6 us
    pallas_call x1, Pallas kernels, local(): pl.pallas_call(functools.partial(relax_kernel, halo), out_shape=jax.Shape...  10.6 us
    ppermute x2, waiting for transfers between devices, halos(): east = lax.ppermute(lefts, 'lon', lon_down)  8.98 us
    ppermute x2, starting transfers between devices, halos(): north = lax.ppermute(bottom, 'lat', lat_up)  7.09 us
    all_to_all x1, starting transfers between devices, local(): lax.all_to_all(send, ('lat', 'lon'), split_axis=0, concat_axis=0, tiled=T...  7.08 us
    pallas_call x1, Pallas kernels, local(): pl.pallas_call(spread_kernel, out_shape=jax.ShapeDtypeStruct((levels, cha...  6.87 us
    all_to_all x1, waiting for transfers between devices, local(): lax.all_to_all(send, ('lat', 'lon'), split_axis=0, concat_axis=0, tiled=T...  5.3 us
    ppermute x2, starting transfers between devices, halos(): east = lax.ppermute(lefts, 'lon', lon_down)  4.51 us
  transfers between devices with their start and end apart: 10, of which 4 were waited for; matrix products, arithmetic and copies ran while one was open for 2% of the time, Pallas kernels for 55%

profile of v4, /device:TPU:1, one launch (start us, length us, event | category | flops | bytes accessed | tf_op | source)
XLA Modules:
  0.0 121.4 jit_solution(12538499063611213024)
XLA Ops:
  0.6 3.2 %pack.1 = (f32[32,40,128]{2,1,0:T(8,128)}, s32[1,512]{1,0:T(1,128)}) custom-call(s32[1]{0:T(128)} %bitcast.lane_ref, s32[1,512]{1,0:T(1,128)} %bitcast.11, s32[1,512]{1,0:T(1,128)} %bitcast.12, f32[4,512]{1,0:T(4,128)} %bitcast.10, f32[512,128]{1,0:T(8,128)} %observed_ref.3, s32[512,128]{1,0:T(8,128)} %accept_ref.1), custom_call_target="tpu_custom_call" | custom-call | flops 402653184 | bytes 1572864 | tf_op jit(solution)/shard_map/pack/pallas_call | solution.py:497
  3.9 7.1 %all-to-all-start = ((f32[32,40,128]{2,1,0:T(8,128)}), f32[32,40,128]{2,1,0:T(8,128)S(1)}, u32[]{:S(2)}, u32[]{:S(2)}) async-start(f32[32,40,128]{2,1,0:T(8,128)} %get-tuple-element.15), calls=%async_computation | async-start | bytes 1310720 | tf_op jit(solution)/shard_map/all_to_all | solution.py:513
  11.0 0.9 add_convert_fusion.2
  11.9 3.5 %collective-permute-start.4 = (s16[8,64,128]{2,1,0:T(8,128)(2,1)}, s16[8,64,128]{2,1,0:T(8,128)(2,1)S(1)}, u32[]{:S(2)}, u32[]{:S(2)}) collective-permute-start(s16[8,64,128]{2,1,0:T(8,128)(2,1)} %get-tuple-element.29), channel_id=1, source_target_pairs={{0,8},{8,16},{16,24},{1,9},{9,17},{17,25},{2,10},{10,18},{18,26},{... | collective-permute-start | bytes 393224 | tf_op jit(solution)/shard_map/ppermute | solution.py:471
  15.4 1.9 %collective-permute-start.5 = (s16[8,64,128]{2,1,0:T(8,128)(2,1)}, s16[8,64,128]{2,1,0:T(8,128)(2,1)S(1)}, u32[]{:S(2)}, u32[]{:S(2)}) collective-permute-start(s16[8,64,128]{2,1,0:T(8,128)(2,1)} %get-tuple-element.28), channel_id=1, source_target_pairs={{8,0},{16,8},{24,16},{9,1},{17,9},{25,17},{10,2},{18,10},{26,18},{... | collective-permute-start | bytes 393224 | tf_op jit(solution)/shard_map/ppermute | solution.py:470
  17.4 6.9 %spread.1.absorb_any = f32[128,128,128]{2,1,0:T(8,128)} custom-call(f32[128,128]{1,0:T(8,128)} %absorb_ref.1), custom_call_target="tpu_custom_call" | custom-call | flops 2097152 | bytes 8388608 | tf_op jit(solution)/shard_map/spread/pallas_call | solution.py:519
  24.2 5.3 %all-to-all-done.recv_ref = f32[32,40,128]{2,1,0:T(8,128)S(1)} async-done(((f32[32,40,128]{2,1,0:T(8,128)}), f32[32,40,128]{2,1,0:T(8,128)S(1)}, u32[]{:S(2)}, u32[]{:S(2)}) %all-to-all-start) | async-done | bytes 655392 | tf_op jit(solution)/shard_map/all_to_all | solution.py:513
  29.5 0.9 copy-done.6
  30.5 46.6 %column.1 = (f32[32,32,128]{2,1,0:T(8,128)}, f32[64,64,128]{2,1,0:T(8,128)}, s16[9,64,128]{2,1,0:T(8,128)(2,1)}, s16[9,64,128]{2,1,0:T(8,128)(2,1)}, s16[83,8,12...) custom-call(f32[32,40,128]{2,1,0:T(8,128)} %copy-done.6, bf16[64,64,128]{2,1,0:T(8,128)(2,1)} %background_ref.1, ...), custom_call_target="tpu_custom_call" | custom-call | flops 234881024 | bytes 6291456 | tf_op jit(solution)/shard_map/column/pallas_call | solution.py:532
  77.0 0.0 copy-start.2
  77.1 3.2 %all-to-all-start.1 = ((f32[32,32,128]{2,1,0:T(8,128)}), f32[32,32,128]{2,1,0:T(8,128)S(1)}, u32[]{:S(2)}, u32[]{:S(2)}) async-start(f32[32,32,128]{2,1,0:T(8,128)} %get-tuple-element.16), calls=%async_computation.1 | async-start | bytes 1048576 | tf_op jit(solution)/shard_map/all_to_all | solution.py:596
  80.3 0.2 add_convert_fusion
  80.5 0.0 collective-permute-done.5.south_ref
  80.5 3.6 %collective-permute-start = (s16[9,64,128]{2,1,0:T(8,128)(2,1)}, s16[9,64,128]{2,1,0:T(8,128)(2,1)S(1)}, u32[]{:S(2)}, u32[]{:S(2)}) collective-permute-start(s16[9,64,128]{2,1,0:T(8,128)(2,1)} %get-tuple-element.18), channel_id=1, source_target_pairs={{0,8},{8,16},{16,24},{1,9},{9,17},{17,25},{2,10},{10,18},{18,26},{... | collective-permute-start | bytes 442376 | tf_op jit(solution)/shard_map/ppermute | solution.py:471
  84.1 1.9 %collective-permute-start.1 = (s16[9,64,128]{2,1,0:T(8,128)(2,1)}, s16[9,64,128]{2,1,0:T(8,128)(2,1)S(1)}, u32[]{:S(2)}, u32[]{:S(2)}) collective-permute-start(s16[9,64,128]{2,1,0:T(8,128)(2,1)} %get-tuple-element.19), channel_id=1, source_target_pairs={{8,0},{16,8},{24,16},{9,1},{17,9},{25,17},{10,2},{18,10},{26,18},{... | collective-permute-start | bytes 442376 | tf_op jit(solution)/shard_map/ppermute | solution.py:470
  86.0 0.7 pad_add_fusion
  86.7 1.2 collective-permute-start.6
  87.9 0.1 collective-permute-done.north_ref
  88.0 4.1 %collective-permute-done.1.south_ref = s16[9,64,128]{2,1,0:T(8,128)(2,1)S(1)} collective-permute-done((s16[9,64,128]{2,1,0:T(8,128)(2,1)}, s16[9,64,128]{2,1,0:T(8,128)(2,1)S(1)}, u32[]{:S(2)}, u32[]{:S(2)}) %collective-permute-start.1) | collective-permute-done | bytes 147488 | tf_op jit(solution)/shard_map/ppermute | solution.py:470
  92.1 0.1 join.1
  92.2 0.6 collective-permute-start.2
  92.7 3.7 %collective-permute-start.3 = (s16[83,8,128]{2,1,0:T(8,128)(2,1)S(1)}, s16[83,8,128]{2,1,0:T(8,128)(2,1)}, u32[]{:S(2)}, u32[]{:S(2)}) collective-permute-start(s16[83,8,128]{2,1,0:T(8,128)(2,1)S(1)} %get-tuple-element.23), channel_id=1, source_target_pairs={{1,0},{2,1},{3,2},{4,3},{5,4},{6,5},{7,6},{0,7},{9,8},{10,9},{11,1... | collective-permute-start | bytes 509960 | tf_op jit(solution)/shard_map/ppermute | solution.py:474
  96.4 0.7 pad_add_fusion.1
  97.0 0.9 collective-permute-start.7
  97.9 0.1 add_convert_fusion.4.inside_ref
  98.0 0.0 collective-permute-done.6.west_hbm
  98.0 9.0 %collective-permute-done.7.east_hbm = s16[80,8,128]{2,1,0:T(8,128)(2,1)} collective-permute-done((s16[80,8,128]{2,1,0:T(8,128)(2,1)}, s16[80,8,128]{2,1,0:T(8,128)(2,1)}, u32[]{:S(2)}, u32[]{:S(2)}) %collective-permute-start.7) | collective-permute-done | bytes 163872 | tf_op jit(solution)/shard_map/ppermute | solution.py:474
  107.0 2.3 %edges.1 = (f32[80,10,8,128]{3,2,1,0:T(8,128)S(1)}, f32[80,10,8,128]{3,2,1,0:T(8,128)S(1)}) custom-call(f32[2]{0:T(128)S(1)} %add_convert_fusion.4.inside_ref, f32[64,64,128]{2,1,0:T(8,128)S(1)} %copy-done, s16[8,64,128]{2,1,0:T(8,128)(2,1)S(1)} %collective-permute-done.4.north_ref, s16[8,64,128]{2,1,0:T(8,128)(2,1)S(1)} %collective-permute-done.5.south_ref, ...), custom_call_target="tpu_custom_call" | custom-call | flops 3276800 | bytes 6291456 | tf_op jit(solution)/shard_map/edges/pallas_call | solution.py:582
  109.3 0.0 collective-permute-done.2.west_ref
  109.3 0.0 copy-start.4
  109.4 10.6 %relax.1 = f32[64,64,128]{2,1,0:T(8,128)} custom-call(f32[2]{0:T(128)S(1)} %add_convert_fusion.4.inside_ref, f32[64,64,128]{2,1,0:T(8,128)S(1)} %copy-done.1, s16[9,64,128]{2,1,0:T(8,128)(2,1)S(1)} %collective-permute-done.north_ref, s16[9,64,128]{2,1,0:T(8,128)(2,1)S(1)} %collective-permute-done.1.south_ref, ...), custom_call_target="tpu_custom_call" | custom-call | flops 65536000 | bytes 8388608 | tf_op jit(solution)/shard_map/relax/pallas_call | solution.py:610
  120.0 1.5 %depart.1 = f32[512,128]{1,0:T(8,128)} custom-call(s32[1,512]{1,0:T(1,128)S(1)} %copy-done.5, f32[1024,128]{1,0:T(8,128)S(1)} %bitcast.9, f32[512,128]{1,0:T(8,128)S(1)} %copy-done.4), custom_call_target="tpu_custom_call" | custom-call | flops 402653184 | bytes 1048576 | tf_op jit(solution)/shard_map/depart/pallas_call | solution.py:600
  (16 shorter events, 0.0 us)
Async XLA Ops:
  0.6 10.4 %copy-start = (f32[64,64,128]{2,1,0:T(8,128)S(1)}, f32[64,64,128]{2,1,0:T(8,128)}, u32[]{:S(2)}) copy-start(f32[64,64,128]{2,1,0:T(8,128)} %centre_ref.1) | copy-start | bytes 6291460
  3.9 25.6 %all-to-all-start = ((f32[32,40,128]{2,1,0:T(8,128)}), f32[32,40,128]{2,1,0:T(8,128)S(1)}, u32[]{:S(2)}, u32[]{:S(2)}) async-start(f32[32,40,128]{2,1,0:T(8,128)} %get-tuple-element.15), calls=%async_computation | async-start | bytes 1310720 | tf_op jit(solution)/shard_map/all_to_all | solution.py:513
  11.9 74.1 %collective-permute-start.4 = (s16[8,64,128]{2,1,0:T(8,128)(2,1)}, s16[8,64,128]{2,1,0:T(8,128)(2,1)S(1)}, u32[]{:S(2)}, u32[]{:S(2)}) collective-permute-start(s16[8,64,128]{2,1,0:T(8,128)(2,1)} %get-tuple-element.29), channel_id=1, source_target_pairs={{0,8},{8,16},{16,24},{1,9},{9,17},{17,25},{2,10},{10,18},{18,26},{... | collective-permute-start | bytes 393224 | tf_op jit(solution)/shard_map/ppermute | solution.py:471
  15.4 65.0 %collective-permute-start.5 = (s16[8,64,128]{2,1,0:T(8,128)(2,1)}, s16[8,64,128]{2,1,0:T(8,128)(2,1)S(1)}, u32[]{:S(2)}, u32[]{:S(2)}) collective-permute-start(s16[8,64,128]{2,1,0:T(8,128)(2,1)} %get-tuple-element.28), channel_id=1, source_target_pairs={{8,0},{16,8},{24,16},{9,1},{17,9},{25,17},{10,2},{18,10},{26,18},{... | collective-permute-start | bytes 393224 | tf_op jit(solution)/shard_map/ppermute | solution.py:470
  29.5 0.9 copy-start.6
  77.0 15.0 %copy-start.2 = (s16[83,8,128]{2,1,0:T(8,128)(2,1)S(1)}, s16[83,8,128]{2,1,0:T(8,128)(2,1)}, u32[]{:S(2)}) copy-start(s16[83,8,128]{2,1,0:T(8,128)(2,1)} %get-tuple-element.20._) | copy-start | bytes 509956
  77.1 15.0 %copy-start.3 = (s16[83,8,128]{2,1,0:T(8,128)(2,1)S(1)}, s16[83,8,128]{2,1,0:T(8,128)(2,1)}, u32[]{:S(2)}) copy-start(s16[83,8,128]{2,1,0:T(8,128)(2,1)} %get-tuple-element.21.__) | copy-start | bytes 509956
  77.1 42.9 %all-to-all-start.1 = ((f32[32,32,128]{2,1,0:T(8,128)}), f32[32,32,128]{2,1,0:T(8,128)S(1)}, u32[]{:S(2)}, u32[]{:S(2)}) async-start(f32[32,32,128]{2,1,0:T(8,128)} %get-tuple-element.16), calls=%async_computation.1 | async-start | bytes 1048576 | tf_op jit(solution)/shard_map/all_to_all | solution.py:596
  80.5 7.5 %collective-permute-start = (s16[9,64,128]{2,1,0:T(8,128)(2,1)}, s16[9,64,128]{2,1,0:T(8,128)(2,1)S(1)}, u32[]{:S(2)}, u32[]{:S(2)}) collective-permute-start(s16[9,64,128]{2,1,0:T(8,128)(2,1)} %get-tuple-element.18), channel_id=1, source_target_pairs={{0,8},{8,16},{16,24},{1,9},{9,17},{17,25},{2,10},{10,18},{18,26},{... | collective-permute-start | bytes 442376 | tf_op jit(solution)/shard_map/ppermute | solution.py:471
  84.1 8.0 %collective-permute-start.1 = (s16[9,64,128]{2,1,0:T(8,128)(2,1)}, s16[9,64,128]{2,1,0:T(8,128)(2,1)S(1)}, u32[]{:S(2)}, u32[]{:S(2)}) collective-permute-start(s16[9,64,128]{2,1,0:T(8,128)(2,1)} %get-tuple-element.19), channel_id=1, source_target_pairs={{8,0},{16,8},{24,16},{9,1},{17,9},{25,17},{10,2},{18,10},{26,18},{... | collective-permute-start | bytes 442376 | tf_op jit(solution)/shard_map/ppermute | solution.py:470
  86.7 11.3 %collective-permute-start.6 = (s16[80,8,128]{2,1,0:T(8,128)(2,1)}, s16[80,8,128]{2,1,0:T(8,128)(2,1)}, u32[]{:S(2)}, u32[]{:S(2)}) collective-permute-start(s16[80,8,128]{2,1,0:T(8,128)(2,1)} %pad_add_fusion), channel_id=1, source_target_pairs={{0,1},{1,2},{2,3},{3,4},{4,5},{5,6},{6,7},{7,0},{8,9},{9,10},{10,1... | collective-permute-start | bytes 491528 | tf_op jit(solution)/shard_map/ppermute | solution.py:473
  92.2 17.2 %collective-permute-start.2 = (s16[83,8,128]{2,1,0:T(8,128)(2,1)S(1)}, s16[83,8,128]{2,1,0:T(8,128)(2,1)}, u32[]{:S(2)}, u32[]{:S(2)}) collective-permute-start(s16[83,8,128]{2,1,0:T(8,128)(2,1)S(1)} %get-tuple-element.22), channel_id=1, source_target_pairs={{0,1},{1,2},{2,3},{3,4},{4,5},{5,6},{6,7},{7,0},{8,9},{9,10},{10,1... | collective-permute-start | bytes 509960 | tf_op jit(solution)/shard_map/ppermute | solution.py:473
  92.7 16.6 %collective-permute-start.3 = (s16[83,8,128]{2,1,0:T(8,128)(2,1)S(1)}, s16[83,8,128]{2,1,0:T(8,128)(2,1)}, u32[]{:S(2)}, u32[]{:S(2)}) collective-permute-start(s16[83,8,128]{2,1,0:T(8,128)(2,1)S(1)} %get-tuple-element.23), channel_id=1, source_target_pairs={{1,0},{2,1},{3,2},{4,3},{5,4},{6,5},{7,6},{0,7},{9,8},{10,9},{11,1... | collective-permute-start | bytes 509960 | tf_op jit(solution)/shard_map/ppermute | solution.py:474
  97.0 9.9 %collective-permute-start.7 = (s16[80,8,128]{2,1,0:T(8,128)(2,1)}, s16[80,8,128]{2,1,0:T(8,128)(2,1)}, u32[]{:S(2)}, u32[]{:S(2)}) collective-permute-start(s16[80,8,128]{2,1,0:T(8,128)(2,1)} %pad_add_fusion.1), channel_id=1, source_target_pairs={{1,0},{2,1},{3,2},{4,3},{5,4},{6,5},{7,6},{0,7},{9,8},{10,9},{11,1... | collective-permute-start | bytes 491528 | tf_op jit(solution)/shard_map/ppermute | solution.py:474
  97.9 11.4 %copy-start.1 = (f32[64,64,128]{2,1,0:T(8,128)S(1)}, f32[64,64,128]{2,1,0:T(8,128)}, u32[]{:S(2)}) copy-start(f32[64,64,128]{2,1,0:T(8,128)} %get-tuple-element.17.centre_ref) | copy-start | bytes 6291460
  109.3 10.7 %copy-start.4 = (f32[512,128]{1,0:T(8,128)S(1)}, f32[512,128]{1,0:T(8,128)}, u32[]{:S(2)}) copy-start(f32[512,128]{1,0:T(8,128)} %observed_ref.3) | copy-start | bytes 786436
  109.3 10.6 %copy-start.5 = (s32[1,512]{1,0:T(1,128)S(1)}, s32[1,512]{1,0:T(1,128)}, u32[]{:S(2)}) copy-start(s32[1,512]{1,0:T(1,128)} %get-tuple-element.14.slot_ref) | copy-start | bytes 6148

commit v5 on v4

--- a/solution.py
+++ b/solution.py
@@ -238,29 +238,41 @@
 
     lax.fori_loop(0, lanes // 8, scatter_last, 0)
 
-    field = (sums_ref[0] + sums_ref[1]) + (sums_ref[2] + sums_ref[3])
-    field = field.reshape(tile_rows, tile_cols, levels)
-    field_ref[...] = field
-
-    borders = (
-        (top_ref, 0, field[:halo]),
-        (bottom_ref, 0, field[tile_rows - halo :]),
-        (left_ref, halo + 1, field[:, :halo]),
-        (right_ref, halo + 1, field[:, tile_cols - halo :]),
+    def add_up(r, carry):
+        row = pl.ds(pl.multiple_of(r * tile_cols, tile_cols), tile_cols)
+        total = (sums_ref[0, row, :] + sums_ref[1, row, :]) + (
+            sums_ref[2, row, :] + sums_ref[3, row, :]
+        )
+        field_ref[r] = total
+        return jnp.maximum(carry, jnp.maximum(jnp.abs(total[:halo]), jnp.abs(total[-halo:])))
+
+    peak = lax.fori_loop(
+        0, tile_rows, add_up, jnp.full((halo, levels), 1e-30, jnp.float32), unroll=2
     )
-    peak = jnp.full((1, levels), 1e-30, jnp.float32)
-    for _, _, strip in borders:
-        peak = jnp.maximum(
-            peak, jnp.max(jnp.max(jnp.abs(strip), axis=0), axis=0, keepdims=True)
-        )
-    power = jnp.ceil(jnp.log2(peak))
+    for r in (*range(halo), *range(tile_rows - halo, tile_rows)):
+        for first in range(0, tile_cols, halo):
+            peak = jnp.maximum(peak, jnp.abs(field_ref[r, first : first + halo]))
+    power = jnp.ceil(jnp.log2(jnp.max(peak, axis=0, keepdims=True)))
     scale = jnp.exp2(15.0 - power)
-    for ref, first, strip in borders:
-        last = first + strip.shape[0]
-        whole = jnp.floor(strip * scale + 0.5)
-        whole = jnp.clip(whole, -32767.0, 32767.0)
-        ref[first:last] = whole.astype(jnp.int32).astype(jnp.int16)
-        ref[last] = jnp.broadcast_to(power, strip.shape[1:]).astype(jnp.int32).astype(jnp.int16)
+
+    def code(x):
+        whole = jnp.clip(jnp.floor(x * scale + 0.5), -32767.0, 32767.0)
+        return whole.astype(jnp.int32).astype(jnp.int16)
+
+    def code_sides(r, carry):
+        left_ref[halo + 1 + r] = code(field_ref[r, :halo])
+        right_ref[halo + 1 + r] = code(field_ref[r, tile_cols - halo :])
+        return carry
+
+    lax.fori_loop(0, tile_rows, code_sides, 0, unroll=4)
+    for r in range(halo):
+        top_ref[r] = code(field_ref[r])
+        bottom_ref[r] = code(field_ref[tile_rows - halo + r])
+    for ref, last in (
+        (top_ref, halo), (bottom_ref, halo),
+        (left_ref, halo + 1 + tile_rows), (right_ref, halo + 1 + tile_rows),
+    ):
+        ref[last] = jnp.broadcast_to(power, ref.shape[1:]).astype(jnp.int32).astype(jnp.int16)
 
 
 def decode_field(coded, power):
@@ -561,7 +573,7 @@
             pltpu.VMEM((levels * 8, lanes), f32),
             pltpu.VMEM((4, cells, levels), f32),
         ],
-        compiler_params=params(60),
+        compiler_params=params(50),
         cost_estimate=cost(
             14 * slots * levels * channels, 2 * slots * levels * channels, 12 * cells * levels
         ),

time: 122 us -> 122 us (level)
  local copies, waits for them, and re-layouts: 0.97 us -> 2.58 us
  Pallas kernels: 71.2 us -> 69.7 us
    unnamed x14 -> x18, local copies, waits for them, and re-layouts: 0.96 us -> 2.57 us
    pallas_call x1, Pallas kernels: 46.6 us -> 45.1 us  [local(): pl.pallas_call(functools.partial(column_kernel, capacity, halo), out_shap...]
  transfers between devices with their start and end apart: 10 -> 10, of which waited for: 4 -> 4; matrix products, arithmetic and copies ran while one was open for 2% -> 2% of each run, Pallas kernels for 55% -> 54%
where the time goes in v5:
time: 122 us; the launch traced here: 121 us
  Pallas kernels  69.7 us (57%)
  starting transfers between devices  27.3 us (22%)
  waiting for transfers between devices  18.5 us (15%)
  local copies, waits for them, and re-layouts  2.58 us (2%)
  other arithmetic  2.5 us (2%)
    pallas_call x1, Pallas kernels, local(): pl.pallas_call(functools.partial(column_kernel, capacity, halo), out_shap...  45.1 us
    pallas_call x1, Pallas kernels, local(): pl.pallas_call(functools.partial(relax_kernel, halo), out_shape=jax.Shape...  10.6 us
    ppermute x2, waiting for transfers between devices, halos(): east = lax.ppermute(lefts, 'lon', lon_down)  8.98 us
    ppermute x2, starting transfers between devices, halos(): north = lax.ppermute(bottom, 'lat', lat_up)  7.09 us
    all_to_all x1, starting transfers between devices, local(): lax.all_to_all(send, ('lat', 'lon'), split_axis=0, concat_axis=0, tiled=T...  7.08 us
    pallas_call x1, Pallas kernels, local(): pl.pallas_call(spread_kernel, out_shape=jax.ShapeDtypeStruct((levels, cha...  6.89 us
    all_to_all x1, waiting for transfers between devices, local(): lax.all_to_all(send, ('lat', 'lon'), split_axis=0, concat_axis=0, tiled=T...  5.28 us
    ppermute x2, starting transfers between devices, halos(): east = lax.ppermute(lefts, 'lon', lon_down)  4.51 us
  transfers between devices with their start and end apart: 10, of which 4 were waited for; matrix products, arithmetic and copies ran while one was open for 2% of the time, Pallas kernels for 54%

profile of v5, /device:TPU:1, one launch (start us, length us, event | category | flops | bytes accessed | tf_op | source)
XLA Modules:
  0.0 121.5 jit_solution(14462351620244601243)
XLA Ops:
  0.6 3.2 %pack.1 = (f32[32,40,128]{2,1,0:T(8,128)}, s32[1,512]{1,0:T(1,128)}) custom-call(s32[1]{0:T(128)} %bitcast.lane_ref, s32[1,512]{1,0:T(1,128)} %bitcast.13, s32[1,512]{1,0:T(1,128)} %bitcast.14, f32[4,512]{1,0:T(4,128)} %bitcast.12, f32[512,128]{1,0:T(8,128)} %observed_ref.3, s32[512,128]{1,0:T(8,128)} %accept_ref.1), custom_call_target="tpu_custom_call" | custom-call | flops 402653184 | bytes 1572864 | tf_op jit(solution)/shard_map/pack/pallas_call | solution.py:509
  3.9 7.1 %all-to-all-start = ((f32[32,40,128]{2,1,0:T(8,128)}), f32[32,40,128]{2,1,0:T(8,128)S(1)}, u32[]{:S(2)}, u32[]{:S(2)}) async-start(f32[32,40,128]{2,1,0:T(8,128)} %get-tuple-element.15), calls=%async_computation | async-start | bytes 1310720 | tf_op jit(solution)/shard_map/all_to_all | solution.py:525
  11.0 0.9 add_convert_fusion.2
  11.9 3.5 %collective-permute-start.4 = (s16[8,64,128]{2,1,0:T(8,128)(2,1)}, s16[8,64,128]{2,1,0:T(8,128)(2,1)S(1)}, u32[]{:S(2)}, u32[]{:S(2)}) collective-permute-start(s16[8,64,128]{2,1,0:T(8,128)(2,1)} %get-tuple-element.29), channel_id=1, source_target_pairs={{0,8},{8,16},{16,24},{1,9},{9,17},{17,25},{2,10},{10,18},{18,26},{... | collective-permute-start | bytes 393224 | tf_op jit(solution)/shard_map/ppermute | solution.py:483
  15.4 0.0 copy-start.6
  15.4 0.0 copy-start.7
  15.4 1.9 %collective-permute-start.5 = (s16[8,64,128]{2,1,0:T(8,128)(2,1)}, s16[8,64,128]{2,1,0:T(8,128)(2,1)S(1)}, u32[]{:S(2)}, u32[]{:S(2)}) collective-permute-start(s16[8,64,128]{2,1,0:T(8,128)(2,1)} %get-tuple-element.28), channel_id=1, source_target_pairs={{8,0},{16,8},{24,16},{9,1},{17,9},{25,17},{10,2},{18,10},{26,18},{... | collective-permute-start | bytes 393224 | tf_op jit(solution)/shard_map/ppermute | solution.py:482
  17.4 6.9 %spread.1.absorb_any = f32[128,128,128]{2,1,0:T(8,128)} custom-call(f32[128,128]{1,0:T(8,128)} %absorb_ref.1), custom_call_target="tpu_custom_call" | custom-call | flops 2097152 | bytes 8388608 | tf_op jit(solution)/shard_map/spread/pallas_call | solution.py:531
  24.3 5.3 %all-to-all-done.recv_ref = f32[32,40,128]{2,1,0:T(8,128)S(1)} async-done(((f32[32,40,128]{2,1,0:T(8,128)}), f32[32,40,128]{2,1,0:T(8,128)S(1)}, u32[]{:S(2)}, u32[]{:S(2)}) %all-to-all-start) | async-done | bytes 655392 | tf_op jit(solution)/shard_map/all_to_all | solution.py:525
  29.5 1.2 %copy-done.2 = bf16[64,64,128]{2,1,0:T(8,128)(2,1)S(1)} copy-done((bf16[64,64,128]{2,1,0:T(8,128)(2,1)S(1)}, bf16[64,64,128]{2,1,0:T(8,128)(2,1)}, u32[]{:S(2)}) %copy-start.2) | copy-done | bytes 1048600
  30.8 45.1 %column.1 = (f32[32,32,128]{2,1,0:T(8,128)}, f32[64,64,128]{2,1,0:T(8,128)}, s16[9,64,128]{2,1,0:T(8,128)(2,1)S(1)}, s16[9,64,128]{2,1,0:T(8,128)(2,1)S(1)}, s16...) custom-call(f32[32,40,128]{2,1,0:T(8,128)S(1)} %all-to-all-done.recv_ref, bf16[64,64,128]{2,1,0:T(8,128)(2,1)S(1)} %copy-done.2, ...), custom_call_target="tpu_custom_call" | custom-call | flops 234881024 | bytes 6291456 | tf_op jit(solution)/shard_map/column/pallas_call | solution.py:544
  75.9 0.7 copy-done.4
  76.6 0.7 copy-done.5
  77.2 3.1 %all-to-all-start.1 = ((f32[32,32,128]{2,1,0:T(8,128)}), f32[32,32,128]{2,1,0:T(8,128)S(1)}, u32[]{:S(2)}, u32[]{:S(2)}) async-start(f32[32,32,128]{2,1,0:T(8,128)} %get-tuple-element.16), calls=%async_computation.1 | async-start | bytes 1048576 | tf_op jit(solution)/shard_map/all_to_all | solution.py:608
  80.3 0.2 add_convert_fusion
  80.5 3.6 %collective-permute-start = (s16[9,64,128]{2,1,0:T(8,128)(2,1)}, s16[9,64,128]{2,1,0:T(8,128)(2,1)S(1)}, u32[]{:S(2)}, u32[]{:S(2)}) collective-permute-start(s16[9,64,128]{2,1,0:T(8,128)(2,1)} %copy-done.5), channel_id=1, source_target_pairs={{0,8},{8,16},{16,24},{1,9},{9,17},{17,25},{2,10},{10,18},{18,26},{... | collective-permute-start | bytes 442376 | tf_op jit(solution)/shard_map/ppermute | solution.py:483
  84.1 1.9 %collective-permute-start.1 = (s16[9,64,128]{2,1,0:T(8,128)(2,1)}, s16[9,64,128]{2,1,0:T(8,128)(2,1)S(1)}, u32[]{:S(2)}, u32[]{:S(2)}) collective-permute-start(s16[9,64,128]{2,1,0:T(8,128)(2,1)} %copy-done.4), channel_id=1, source_target_pairs={{8,0},{16,8},{24,16},{9,1},{17,9},{25,17},{10,2},{18,10},{26,18},{... | collective-permute-start | bytes 442376 | tf_op jit(solution)/shard_map/ppermute | solution.py:482
  86.0 0.7 pad_add_fusion
  86.7 1.2 collective-permute-start.6
  87.9 0.1 collective-permute-done.north_ref
  88.0 4.1 %collective-permute-done.1.south_ref = s16[9,64,128]{2,1,0:T(8,128)(2,1)S(1)} collective-permute-done((s16[9,64,128]{2,1,0:T(8,128)(2,1)}, s16[9,64,128]{2,1,0:T(8,128)(2,1)S(1)}, u32[]{:S(2)}, u32[]{:S(2)}) %collective-permute-start.1) | collective-permute-done | bytes 147488 | tf_op jit(solution)/shard_map/ppermute | solution.py:482
  92.1 0.1 join.1
  92.2 0.6 collective-permute-start.2
  92.7 3.7 %collective-permute-start.3 = (s16[83,8,128]{2,1,0:T(8,128)(2,1)S(1)}, s16[83,8,128]{2,1,0:T(8,128)(2,1)}, u32[]{:S(2)}, u32[]{:S(2)}) collective-permute-start(s16[83,8,128]{2,1,0:T(8,128)(2,1)S(1)} %get-tuple-element.23), channel_id=1, source_target_pairs={{1,0},{2,1},{3,2},{4,3},{5,4},{6,5},{7,6},{0,7},{9,8},{10,9},{11,1... | collective-permute-start | bytes 509960 | tf_op jit(solution)/shard_map/ppermute | solution.py:486
  96.4 0.7 pad_add_fusion.1
  97.1 0.9 collective-permute-start.7
  97.9 0.1 add_convert_fusion.4.inside_ref
  98.0 9.0 %collective-permute-done.7.east_hbm = s16[80,8,128]{2,1,0:T(8,128)(2,1)} collective-permute-done((s16[80,8,128]{2,1,0:T(8,128)(2,1)}, s16[80,8,128]{2,1,0:T(8,128)(2,1)}, u32[]{:S(2)}, u32[]{:S(2)}) %collective-permute-start.7) | collective-permute-done | bytes 163872 | tf_op jit(solution)/shard_map/ppermute | solution.py:486
  107.0 2.3 %edges.1 = (f32[80,10,8,128]{3,2,1,0:T(8,128)S(1)}, f32[80,10,8,128]{3,2,1,0:T(8,128)S(1)}) custom-call(f32[2]{0:T(128)S(1)} %add_convert_fusion.4.inside_ref, f32[64,64,128]{2,1,0:T(8,128)S(1)} %copy-done, s16[8,64,128]{2,1,0:T(8,128)(2,1)S(1)} %collective-permute-done.4.north_ref, s16[8,64,128]{2,1,0:T(8,128)(2,1)S(1)} %collective-permute-done.5.south_ref, ...), custom_call_target="tpu_custom_call" | custom-call | flops 3276800 | bytes 6291456 | tf_op jit(solution)/shard_map/edges/pallas_call | solution.py:594
  109.3 0.0 copy-start.3
  109.4 10.6 %relax.1 = f32[64,64,128]{2,1,0:T(8,128)} custom-call(f32[2]{0:T(128)S(1)} %add_convert_fusion.4.inside_ref, f32[64,64,128]{2,1,0:T(8,128)S(1)} %copy-done.1, s16[9,64,128]{2,1,0:T(8,128)(2,1)S(1)} %collective-permute-done.north_ref, s16[9,64,128]{2,1,0:T(8,128)(2,1)S(1)} %collective-permute-done.1.south_ref, ...), custom_call_target="tpu_custom_call" | custom-call | flops 65536000 | bytes 8388608 | tf_op jit(solution)/shard_map/relax/pallas_call | solution.py:622
  120.0 1.5 %depart.1 = f32[512,128]{1,0:T(8,128)} custom-call(s32[1,512]{1,0:T(1,128)S(1)} %copy-done.8, f32[1024,128]{1,0:T(8,128)S(1)} %bitcast.9, f32[512,128]{1,0:T(8,128)S(1)} %copy-done.3), custom_call_target="tpu_custom_call" | custom-call | flops 402653184 | bytes 1048576 | tf_op jit(solution)/shard_map/depart/pallas_call | solution.py:612
  (20 shorter events, 0.1 us)
Async XLA Ops:
  0.6 10.4 %copy-start = (f32[64,64,128]{2,1,0:T(8,128)S(1)}, f32[64,64,128]{2,1,0:T(8,128)}, u32[]{:S(2)}) copy-start(f32[64,64,128]{2,1,0:T(8,128)} %centre_ref.1) | copy-start | bytes 6291460
  3.9 25.6 %all-to-all-start = ((f32[32,40,128]{2,1,0:T(8,128)}), f32[32,40,128]{2,1,0:T(8,128)S(1)}, u32[]{:S(2)}, u32[]{:S(2)}) async-start(f32[32,40,128]{2,1,0:T(8,128)} %get-tuple-element.15), calls=%async_computation | async-start | bytes 1310720 | tf_op jit(solution)/shard_map/all_to_all | solution.py:525
  11.9 74.1 %collective-permute-start.4 = (s16[8,64,128]{2,1,0:T(8,128)(2,1)}, s16[8,64,128]{2,1,0:T(8,128)(2,1)S(1)}, u32[]{:S(2)}, u32[]{:S(2)}) collective-permute-start(s16[8,64,128]{2,1,0:T(8,128)(2,1)} %get-tuple-element.29), channel_id=1, source_target_pairs={{0,8},{8,16},{16,24},{1,9},{9,17},{17,25},{2,10},{10,18},{18,26},{... | collective-permute-start | bytes 393224 | tf_op jit(solution)/shard_map/ppermute | solution.py:483
  15.4 14.1 %copy-start.6 = (f32[128]{0:T(128)S(1)}, f32[128]{0:T(128)}, u32[]{:S(2)}) copy-start(f32[128]{0:T(128)} %param.18) | copy-start | bytes 1540
  15.4 14.1 %copy-start.7 = (f32[128]{0:T(128)S(1)}, f32[128]{0:T(128)}, u32[]{:S(2)}) copy-start(f32[128]{0:T(128)} %param.19) | copy-start | bytes 1540
  15.4 65.0 %collective-permute-start.5 = (s16[8,64,128]{2,1,0:T(8,128)(2,1)}, s16[8,64,128]{2,1,0:T(8,128)(2,1)S(1)}, u32[]{:S(2)}, u32[]{:S(2)}) collective-permute-start(s16[8,64,128]{2,1,0:T(8,128)(2,1)} %get-tuple-element.28), channel_id=1, source_target_pairs={{8,0},{16,8},{24,16},{9,1},{17,9},{25,17},{10,2},{18,10},{26,18},{... | collective-permute-start | bytes 393224 | tf_op jit(solution)/shard_map/ppermute | solution.py:482
  29.5 1.2 %copy-start.2 = (bf16[64,64,128]{2,1,0:T(8,128)(2,1)S(1)}, bf16[64,64,128]{2,1,0:T(8,128)(2,1)}, u32[]{:S(2)}) copy-start(bf16[64,64,128]{2,1,0:T(8,128)(2,1)} %background_ref.1) | copy-start | bytes 3145732
  75.9 0.7 copy-start.4
  76.6 0.7 copy-start.5
  77.2 42.8 %all-to-all-start.1 = ((f32[32,32,128]{2,1,0:T(8,128)}), f32[32,32,128]{2,1,0:T(8,128)S(1)}, u32[]{:S(2)}, u32[]{:S(2)}) async-start(f32[32,32,128]{2,1,0:T(8,128)} %get-tuple-element.16), calls=%async_computation.1 | async-start | bytes 1048576 | tf_op jit(solution)/shard_map/all_to_all | solution.py:608
  80.5 7.5 %collective-permute-start = (s16[9,64,128]{2,1,0:T(8,128)(2,1)}, s16[9,64,128]{2,1,0:T(8,128)(2,1)S(1)}, u32[]{:S(2)}, u32[]{:S(2)}) collective-permute-start(s16[9,64,128]{2,1,0:T(8,128)(2,1)} %copy-done.5), channel_id=1, source_target_pairs={{0,8},{8,16},{16,24},{1,9},{9,17},{17,25},{2,10},{10,18},{18,26},{... | collective-permute-start | bytes 442376 | tf_op jit(solution)/shard_map/ppermute | solution.py:483
  84.1 8.0 %collective-permute-start.1 = (s16[9,64,128]{2,1,0:T(8,128)(2,1)}, s16[9,64,128]{2,1,0:T(8,128)(2,1)S(1)}, u32[]{:S(2)}, u32[]{:S(2)}) collective-permute-start(s16[9,64,128]{2,1,0:T(8,128)(2,1)} %copy-done.4), channel_id=1, source_target_pairs={{8,0},{16,8},{24,16},{9,1},{17,9},{25,17},{10,2},{18,10},{26,18},{... | collective-permute-start | bytes 442376 | tf_op jit(solution)/shard_map/ppermute | solution.py:482
  86.7 11.3 %collective-permute-start.6 = (s16[80,8,128]{2,1,0:T(8,128)(2,1)}, s16[80,8,128]{2,1,0:T(8,128)(2,1)}, u32[]{:S(2)}, u32[]{:S(2)}) collective-permute-start(s16[80,8,128]{2,1,0:T(8,128)(2,1)} %pad_add_fusion), channel_id=1, source_target_pairs={{0,1},{1,2},{2,3},{3,4},{4,5},{5,6},{6,7},{7,0},{8,9},{9,10},{10,1... | collective-permute-start | bytes 491528 | tf_op jit(solution)/shard_map/ppermute | solution.py:485
  92.2 17.2 %collective-permute-start.2 = (s16[83,8,128]{2,1,0:T(8,128)(2,1)S(1)}, s16[83,8,128]{2,1,0:T(8,128)(2,1)}, u32[]{:S(2)}, u32[]{:S(2)}) collective-permute-start(s16[83,8,128]{2,1,0:T(8,128)(2,1)S(1)} %get-tuple-element.22), channel_id=1, source_target_pairs={{0,1},{1,2},{2,3},{3,4},{4,5},{5,6},{6,7},{7,0},{8,9},{9,10},{10,1... | collective-permute-start | bytes 509960 | tf_op jit(solution)/shard_map/ppermute | solution.py:485
  92.7 16.6 %collective-permute-start.3 = (s16[83,8,128]{2,1,0:T(8,128)(2,1)S(1)}, s16[83,8,128]{2,1,0:T(8,128)(2,1)}, u32[]{:S(2)}, u32[]{:S(2)}) collective-permute-start(s16[83,8,128]{2,1,0:T(8,128)(2,1)S(1)} %get-tuple-element.23), channel_id=1, source_target_pairs={{1,0},{2,1},{3,2},{4,3},{5,4},{6,5},{7,6},{0,7},{9,8},{10,9},{11,1... | collective-permute-start | bytes 509960 | tf_op jit(solution)/shard_map/ppermute | solution.py:486
  97.1 9.9 %collective-permute-start.7 = (s16[80,8,128]{2,1,0:T(8,128)(2,1)}, s16[80,8,128]{2,1,0:T(8,128)(2,1)}, u32[]{:S(2)}, u32[]{:S(2)}) collective-permute-start(s16[80,8,128]{2,1,0:T(8,128)(2,1)} %pad_add_fusion.1), channel_id=1, source_target_pairs={{1,0},{2,1},{3,2},{4,3},{5,4},{6,5},{7,6},{0,7},{9,8},{10,9},{11,1... | collective-permute-start | bytes 491528 | tf_op jit(solution)/shard_map/ppermute | solution.py:486
  97.9 11.4 %copy-start.1 = (f32[64,64,128]{2,1,0:T(8,128)S(1)}, f32[64,64,128]{2,1,0:T(8,128)}, u32[]{:S(2)}) copy-start(f32[64,64,128]{2,1,0:T(8,128)} %get-tuple-element.17.centre_ref) | copy-start | bytes 6291460
  109.3 10.7 %copy-start.3 = (f32[512,128]{1,0:T(8,128)S(1)}, f32[512,128]{1,0:T(8,128)}, u32[]{:S(2)}) copy-start(f32[512,128]{1,0:T(8,128)} %observed_ref.3) | copy-start | bytes 786436
  109.4 10.6 %copy-start.8 = (s32[1,512]{1,0:T(1,128)S(1)}, s32[1,512]{1,0:T(1,128)}, u32[]{:S(2)}) copy-start(s32[1,512]{1,0:T(1,128)} %get-tuple-element.14.slot_ref) | copy-start | bytes 6148

commit v6 on v5

--- a/solution.py
+++ b/solution.py
@@ -101,9 +101,9 @@
 
 
 def column_kernel(
-    capacity, halo, recv_ref, background_ref, absorb_any, sensitivity_ref, inverse_ref,
+    capacity, halo, recv_ref, background_hbm, absorb_any, sensitivity_ref, inverse_ref,
     evolved_ref, field_ref, top_ref, bottom_ref, left_ref, right_ref,
-    base_ref, slot_base_ref, sem, absorb_sem, cells_ref, absorb_b, slope_b, inverse_b, taken_ref, terms_ref, profile_ref,
+    base_ref, slot_base_ref, sem, absorb_sem, background_ref, background_sem, cells_ref, absorb_b, slope_b, inverse_b, taken_ref, terms_ref, profile_ref,
     rise_ref, obs_ref, evo_ref, main_ref, side_ref, push_ref, sums_ref
 ):
     dev_count = recv_ref.shape[0]
@@ -116,6 +116,8 @@
     per_loop = UNROLL * wide * lanes // (levels * channels)
     corners = (0, 1, tile_cols, tile_cols + 1)
 
+    background_copy = pltpu.make_async_copy(background_hbm, background_ref, background_sem)
+    background_copy.start()
     rows = recv_ref[:, capacity, :].reshape(blocks, group, lanes)
     slot_base_ref[...] = jnp.sum(rows, axis=1).astype(jnp.int32)
     copy = pltpu.make_async_copy(slot_base_ref, base_ref, sem)
@@ -130,12 +132,13 @@
     for c in range(channels // wide):
         absorb_copy(c).start()
 
-    cells_ref[...] = background_ref[...].reshape(cells, levels).astype(jnp.float32)
     slope_b[...] = jnp.broadcast_to(sensitivity_ref[...] * LOG2E, (lanes, channels)).T
     inverse_b[...] = jnp.broadcast_to(inverse_ref[...], (lanes, channels)).T
 
     sums_ref[...] = jnp.zeros_like(sums_ref)
     terms_ref[...] = jnp.zeros_like(terms_ref)
+    background_copy.wait()
+    cells_ref[...] = background_ref[...].reshape(cells, levels).astype(jnp.float32)
     copy.wait()
 
     def gather(f, at):
@@ -551,13 +554,15 @@
             jax.ShapeDtypeStruct((tile_rows + 2 * halo + 3, halo, levels), jnp.int16),
             jax.ShapeDtypeStruct((tile_rows + 2 * halo + 3, halo, levels), jnp.int16),
         ),
-        in_specs=[vmem()] * 2 + [hbm()] + [vmem()] * 2,
+        in_specs=[vmem()] + [hbm()] * 2 + [vmem()] * 2,
         out_specs=(vmem(),) * 6,
         scratch_shapes=[
             pltpu.SMEM((slots // lanes, lanes), jnp.int32),
         pltpu.VMEM((slots // lanes, lanes), jnp.int32),
             pltpu.SemaphoreType.DMA,
             pltpu.SemaphoreType.DMA((channels // wide,)),
+            pltpu.VMEM((tile_rows, tile_cols, levels), background.dtype),
+            pltpu.SemaphoreType.DMA,
             pltpu.VMEM((cells, levels), f32),
             pltpu.VMEM((levels, channels, lanes), f32),
             pltpu.VMEM((channels, lanes), f32),
@@ -573,7 +578,7 @@
             pltpu.VMEM((levels * 8, lanes), f32),
             pltpu.VMEM((4, cells, levels), f32),
         ],
-        compiler_params=params(50),
+        compiler_params=params(52),
         cost_estimate=cost(
             14 * slots * levels * channels, 2 * slots * levels * channels, 12 * cells * levels
         ),

time: 122 us -> 123 us (level)
  Pallas kernels: 69.7 us -> 71.9 us
    pallas_call x1, Pallas kernels: 45.1 us -> 47.3 us  [local(): pl.pallas_call(functools.partial(column_kernel, capacity, halo), out_shap...]
    unnamed x18 -> x16, local copies, waits for them, and re-layouts: 2.57 us -> 1.34 us
  transfers between devices with their start and end apart: 10 -> 10, of which waited for: 4 -> 4; matrix products, arithmetic and copies ran while one was open for 2% -> 2% of each run, Pallas kernels for 54% -> 55%
where the time goes in v6:
time: 123 us; the launch traced here: 122 us
  Pallas kernels  71.9 us (58%)
  starting transfers between devices  27.3 us (22%)
  waiting for transfers between devices  18.5 us (15%)
  other arithmetic  2.48 us (2%)
  local copies, waits for them, and re-layouts  1.36 us (1%)
    pallas_call x1, Pallas kernels, local(): pl.pallas_call(functools.partial(column_kernel, capacity, halo), out_shap...  47.3 us
    pallas_call x1, Pallas kernels, local(): pl.pallas_call(functools.partial(relax_kernel, halo), out_shape=jax.Shape...  10.6 us
    ppermute x2, waiting for transfers between devices, halos(): east = lax.ppermute(lefts, 'lon', lon_down)  8.99 us
    ppermute x2, starting transfers between devices, halos(): north = lax.ppermute(bottom, 'lat', lat_up)  7.09 us
    all_to_all x1, starting transfers between devices, local(): lax.all_to_all(send, ('lat', 'lon'), split_axis=0, concat_axis=0, tiled=T...  7.08 us
    pallas_call x1, Pallas kernels, local(): pl.pallas_call(spread_kernel, out_shape=jax.ShapeDtypeStruct((levels, cha...  6.86 us
    all_to_all x1, waiting for transfers between devices, local(): lax.all_to_all(send, ('lat', 'lon'), split_axis=0, concat_axis=0, tiled=T...  5.31 us
    ppermute x2, starting transfers between devices, halos(): east = lax.ppermute(lefts, 'lon', lon_down)  4.51 us
  transfers between devices with their start and end apart: 10, of which 4 were waited for; matrix products, arithmetic and copies ran while one was open for 2% of the time, Pallas kernels for 55%

profile of v6, /device:TPU:1, one launch (start us, length us, event | category | flops | bytes accessed | tf_op | source)
XLA Modules:
  0.0 122.4 jit_solution(12031286564706709702)
XLA Ops:
  0.6 3.2 %pack.1 = (f32[32,40,128]{2,1,0:T(8,128)}, s32[1,512]{1,0:T(1,128)}) custom-call(s32[1]{0:T(128)} %bitcast.lane_ref, s32[1,512]{1,0:T(1,128)} %bitcast.13, s32[1,512]{1,0:T(1,128)} %bitcast.14, f32[4,512]{1,0:T(4,128)} %bitcast.12, f32[512,128]{1,0:T(8,128)} %observed_ref.3, s32[512,128]{1,0:T(8,128)} %accept_ref.1), custom_call_target="tpu_custom_call" | custom-call | flops 402653184 | bytes 1572864 | tf_op jit(solution)/shard_map/pack/pallas_call | solution.py:512
  3.9 7.1 %all-to-all-start = ((f32[32,40,128]{2,1,0:T(8,128)}), f32[32,40,128]{2,1,0:T(8,128)S(1)}, u32[]{:S(2)}, u32[]{:S(2)}) async-start(f32[32,40,128]{2,1,0:T(8,128)} %get-tuple-element.15), calls=%async_computation | async-start | bytes 1310720 | tf_op jit(solution)/shard_map/all_to_all | solution.py:528
  11.0 0.9 add_convert_fusion.2
  11.9 3.5 %collective-permute-start.4 = (s16[8,64,128]{2,1,0:T(8,128)(2,1)}, s16[8,64,128]{2,1,0:T(8,128)(2,1)S(1)}, u32[]{:S(2)}, u32[]{:S(2)}) collective-permute-start(s16[8,64,128]{2,1,0:T(8,128)(2,1)} %get-tuple-element.29), channel_id=1, source_target_pairs={{0,8},{8,16},{16,24},{1,9},{9,17},{17,25},{2,10},{10,18},{18,26},{... | collective-permute-start | bytes 393224 | tf_op jit(solution)/shard_map/ppermute | solution.py:486
  15.4 0.0 copy-start.5
  15.4 0.0 copy-start.6
  15.4 1.9 %collective-permute-start.5 = (s16[8,64,128]{2,1,0:T(8,128)(2,1)}, s16[8,64,128]{2,1,0:T(8,128)(2,1)S(1)}, u32[]{:S(2)}, u32[]{:S(2)}) collective-permute-start(s16[8,64,128]{2,1,0:T(8,128)(2,1)} %get-tuple-element.28), channel_id=1, source_target_pairs={{8,0},{16,8},{24,16},{9,1},{17,9},{25,17},{10,2},{18,10},{26,18},{... | collective-permute-start | bytes 393224 | tf_op jit(solution)/shard_map/ppermute | solution.py:485
  17.4 6.9 %spread.1.absorb_any = f32[128,128,128]{2,1,0:T(8,128)} custom-call(f32[128,128]{1,0:T(8,128)} %absorb_ref.1), custom_call_target="tpu_custom_call" | custom-call | flops 2097152 | bytes 8388608 | tf_op jit(solution)/shard_map/spread/pallas_call | solution.py:534
  24.2 5.3 %all-to-all-done.recv_ref = f32[32,40,128]{2,1,0:T(8,128)S(1)} async-done(((f32[32,40,128]{2,1,0:T(8,128)}), f32[32,40,128]{2,1,0:T(8,128)S(1)}, u32[]{:S(2)}, u32[]{:S(2)}) %all-to-all-start) | async-done | bytes 655392 | tf_op jit(solution)/shard_map/all_to_all | solution.py:528
  29.5 47.3 %column.1 = (f32[32,32,128]{2,1,0:T(8,128)}, f32[64,64,128]{2,1,0:T(8,128)}, s16[9,64,128]{2,1,0:T(8,128)(2,1)S(1)}, s16[9,64,128]{2,1,0:T(8,128)(2,1)S(1)}, s16...) custom-call(f32[32,40,128]{2,1,0:T(8,128)S(1)} %all-to-all-done.recv_ref, ...), custom_call_target="tpu_custom_call" | custom-call | flops 234881024 | bytes 6291456 | tf_op jit(solution)/shard_map/column/pallas_call | solution.py:547
  76.8 0.7 copy-done.3
  77.5 0.7 copy-done.4
  78.2 3.1 %all-to-all-start.1 = ((f32[32,32,128]{2,1,0:T(8,128)}), f32[32,32,128]{2,1,0:T(8,128)S(1)}, u32[]{:S(2)}, u32[]{:S(2)}) async-start(f32[32,32,128]{2,1,0:T(8,128)} %get-tuple-element.16), calls=%async_computation.1 | async-start | bytes 1048576 | tf_op jit(solution)/shard_map/all_to_all | solution.py:613
  81.2 0.2 add_convert_fusion
  81.4 0.0 collective-permute-done.5.south_ref
  81.4 3.6 %collective-permute-start = (s16[9,64,128]{2,1,0:T(8,128)(2,1)}, s16[9,64,128]{2,1,0:T(8,128)(2,1)S(1)}, u32[]{:S(2)}, u32[]{:S(2)}) collective-permute-start(s16[9,64,128]{2,1,0:T(8,128)(2,1)} %copy-done.4), channel_id=1, source_target_pairs={{0,8},{8,16},{16,24},{1,9},{9,17},{17,25},{2,10},{10,18},{18,26},{... | collective-permute-start | bytes 442376 | tf_op jit(solution)/shard_map/ppermute | solution.py:486
  85.0 1.9 %collective-permute-start.1 = (s16[9,64,128]{2,1,0:T(8,128)(2,1)}, s16[9,64,128]{2,1,0:T(8,128)(2,1)S(1)}, u32[]{:S(2)}, u32[]{:S(2)}) collective-permute-start(s16[9,64,128]{2,1,0:T(8,128)(2,1)} %copy-done.3), channel_id=1, source_target_pairs={{8,0},{16,8},{24,16},{9,1},{17,9},{25,17},{10,2},{18,10},{26,18},{... | collective-permute-start | bytes 442376 | tf_op jit(solution)/shard_map/ppermute | solution.py:485
  87.0 0.7 pad_add_fusion
  87.6 1.2 collective-permute-start.6
  88.8 0.1 collective-permute-done.north_ref
  88.9 4.1 %collective-permute-done.1.south_ref = s16[9,64,128]{2,1,0:T(8,128)(2,1)S(1)} collective-permute-done((s16[9,64,128]{2,1,0:T(8,128)(2,1)}, s16[9,64,128]{2,1,0:T(8,128)(2,1)S(1)}, u32[]{:S(2)}, u32[]{:S(2)}) %collective-permute-start.1) | collective-permute-done | bytes 147488 | tf_op jit(solution)/shard_map/ppermute | solution.py:485
  93.0 0.1 join.1
  93.1 0.6 collective-permute-start.2
  93.6 3.7 %collective-permute-start.3 = (s16[83,8,128]{2,1,0:T(8,128)(2,1)S(1)}, s16[83,8,128]{2,1,0:T(8,128)(2,1)}, u32[]{:S(2)}, u32[]{:S(2)}) collective-permute-start(s16[83,8,128]{2,1,0:T(8,128)(2,1)S(1)} %get-tuple-element.23), channel_id=1, source_target_pairs={{1,0},{2,1},{3,2},{4,3},{5,4},{6,5},{7,6},{0,7},{9,8},{10,9},{11,1... | collective-permute-start | bytes 509960 | tf_op jit(solution)/shard_map/ppermute | solution.py:489
  97.3 0.7 pad_add_fusion.1
  98.0 0.9 collective-permute-start.7
  98.8 0.1 add_convert_fusion.4.inside_ref
  98.9 9.0 %collective-permute-done.7.east_hbm = s16[80,8,128]{2,1,0:T(8,128)(2,1)} collective-permute-done((s16[80,8,128]{2,1,0:T(8,128)(2,1)}, s16[80,8,128]{2,1,0:T(8,128)(2,1)}, u32[]{:S(2)}, u32[]{:S(2)}) %collective-permute-start.7) | collective-permute-done | bytes 163872 | tf_op jit(solution)/shard_map/ppermute | solution.py:489
  107.9 2.3 %edges.1 = (f32[80,10,8,128]{3,2,1,0:T(8,128)S(1)}, f32[80,10,8,128]{3,2,1,0:T(8,128)S(1)}) custom-call(f32[2]{0:T(128)S(1)} %add_convert_fusion.4.inside_ref, f32[64,64,128]{2,1,0:T(8,128)S(1)} %copy-done, s16[8,64,128]{2,1,0:T(8,128)(2,1)S(1)} %collective-permute-done.4.north_ref, s16[8,64,128]{2,1,0:T(8,128)(2,1)S(1)} %collective-permute-done.5.south_ref, ...), custom_call_target="tpu_custom_call" | custom-call | flops 3276800 | bytes 6291456 | tf_op jit(solution)/shard_map/edges/pallas_call | solution.py:599
  110.3 0.0 copy-start.2
  110.3 10.6 %relax.1 = f32[64,64,128]{2,1,0:T(8,128)} custom-call(f32[2]{0:T(128)S(1)} %add_convert_fusion.4.inside_ref, f32[64,64,128]{2,1,0:T(8,128)S(1)} %copy-done.1, s16[9,64,128]{2,1,0:T(8,128)(2,1)S(1)} %collective-permute-done.north_ref, s16[9,64,128]{2,1,0:T(8,128)(2,1)S(1)} %collective-permute-done.1.south_ref, ...), custom_call_target="tpu_custom_call" | custom-call | flops 65536000 | bytes 8388608 | tf_op jit(solution)/shard_map/relax/pallas_call | solution.py:627
  120.9 1.5 %depart.1 = f32[512,128]{1,0:T(8,128)} custom-call(s32[1,512]{1,0:T(1,128)S(1)} %copy-done.7, f32[1024,128]{1,0:T(8,128)S(1)} %bitcast.9, f32[512,128]{1,0:T(8,128)S(1)} %copy-done.2), custom_call_target="tpu_custom_call" | custom-call | flops 402653184 | bytes 1048576 | tf_op jit(solution)/shard_map/depart/pallas_call | solution.py:617
  (18 shorter events, 0.1 us)
Async XLA Ops:
  0.6 10.4 %copy-start = (f32[64,64,128]{2,1,0:T(8,128)S(1)}, f32[64,64,128]{2,1,0:T(8,128)}, u32[]{:S(2)}) copy-start(f32[64,64,128]{2,1,0:T(8,128)} %centre_ref.1) | copy-start | bytes 6291460
  3.9 25.6 %all-to-all-start = ((f32[32,40,128]{2,1,0:T(8,128)}), f32[32,40,128]{2,1,0:T(8,128)S(1)}, u32[]{:S(2)}, u32[]{:S(2)}) async-start(f32[32,40,128]{2,1,0:T(8,128)} %get-tuple-element.15), calls=%async_computation | async-start | bytes 1310720 | tf_op jit(solution)/shard_map/all_to_all | solution.py:528
  11.9 75.1 %collective-permute-start.4 = (s16[8,64,128]{2,1,0:T(8,128)(2,1)}, s16[8,64,128]{2,1,0:T(8,128)(2,1)S(1)}, u32[]{:S(2)}, u32[]{:S(2)}) collective-permute-start(s16[8,64,128]{2,1,0:T(8,128)(2,1)} %get-tuple-element.29), channel_id=1, source_target_pairs={{0,8},{8,16},{16,24},{1,9},{9,17},{17,25},{2,10},{10,18},{18,26},{... | collective-permute-start | bytes 393224 | tf_op jit(solution)/shard_map/ppermute | solution.py:486
  15.4 14.1 %copy-start.5 = (f32[128]{0:T(128)S(1)}, f32[128]{0:T(128)}, u32[]{:S(2)}) copy-start(f32[128]{0:T(128)} %param.18) | copy-start | bytes 1540
  15.4 14.1 %copy-start.6 = (f32[128]{0:T(128)S(1)}, f32[128]{0:T(128)}, u32[]{:S(2)}) copy-start(f32[128]{0:T(128)} %param.19) | copy-start | bytes 1540
  15.4 66.0 %collective-permute-start.5 = (s16[8,64,128]{2,1,0:T(8,128)(2,1)}, s16[8,64,128]{2,1,0:T(8,128)(2,1)S(1)}, u32[]{:S(2)}, u32[]{:S(2)}) collective-permute-start(s16[8,64,128]{2,1,0:T(8,128)(2,1)} %get-tuple-element.28), channel_id=1, source_target_pairs={{8,0},{16,8},{24,16},{9,1},{17,9},{25,17},{10,2},{18,10},{26,18},{... | collective-permute-start | bytes 393224 | tf_op jit(solution)/shard_map/ppermute | solution.py:485
  76.8 0.7 copy-start.3
  77.5 0.7 copy-start.4
  78.2 42.8 %all-to-all-start.1 = ((f32[32,32,128]{2,1,0:T(8,128)}), f32[32,32,128]{2,1,0:T(8,128)S(1)}, u32[]{:S(2)}, u32[]{:S(2)}) async-start(f32[32,32,128]{2,1,0:T(8,128)} %get-tuple-element.16), calls=%async_computation.1 | async-start | bytes 1048576 | tf_op jit(solution)/shard_map/all_to_all | solution.py:613
  81.4 7.5 %collective-permute-start = (s16[9,64,128]{2,1,0:T(8,128)(2,1)}, s16[9,64,128]{2,1,0:T(8,128)(2,1)S(1)}, u32[]{:S(2)}, u32[]{:S(2)}) collective-permute-start(s16[9,64,128]{2,1,0:T(8,128)(2,1)} %copy-done.4), channel_id=1, source_target_pairs={{0,8},{8,16},{16,24},{1,9},{9,17},{17,25},{2,10},{10,18},{18,26},{... | collective-permute-start | bytes 442376 | tf_op jit(solution)/shard_map/ppermute | solution.py:486
  85.0 8.0 %collective-permute-start.1 = (s16[9,64,128]{2,1,0:T(8,128)(2,1)}, s16[9,64,128]{2,1,0:T(8,128)(2,1)S(1)}, u32[]{:S(2)}, u32[]{:S(2)}) collective-permute-start(s16[9,64,128]{2,1,0:T(8,128)(2,1)} %copy-done.3), channel_id=1, source_target_pairs={{8,0},{16,8},{24,16},{9,1},{17,9},{25,17},{10,2},{18,10},{26,18},{... | collective-permute-start | bytes 442376 | tf_op jit(solution)/shard_map/ppermute | solution.py:485
  87.6 11.3 %collective-permute-start.6 = (s16[80,8,128]{2,1,0:T(8,128)(2,1)}, s16[80,8,128]{2,1,0:T(8,128)(2,1)}, u32[]{:S(2)}, u32[]{:S(2)}) collective-permute-start(s16[80,8,128]{2,1,0:T(8,128)(2,1)} %pad_add_fusion), channel_id=1, source_target_pairs={{0,1},{1,2},{2,3},{3,4},{4,5},{5,6},{6,7},{7,0},{8,9},{9,10},{10,1... | collective-permute-start | bytes 491528 | tf_op jit(solution)/shard_map/ppermute | solution.py:488
  93.1 17.2 %collective-permute-start.2 = (s16[83,8,128]{2,1,0:T(8,128)(2,1)S(1)}, s16[83,8,128]{2,1,0:T(8,128)(2,1)}, u32[]{:S(2)}, u32[]{:S(2)}) collective-permute-start(s16[83,8,128]{2,1,0:T(8,128)(2,1)S(1)} %get-tuple-element.22), channel_id=1, source_target_pairs={{0,1},{1,2},{2,3},{3,4},{4,5},{5,6},{6,7},{7,0},{8,9},{9,10},{10,1... | collective-permute-start | bytes 509960 | tf_op jit(solution)/shard_map/ppermute | solution.py:488
  93.6 16.6 %collective-permute-start.3 = (s16[83,8,128]{2,1,0:T(8,128)(2,1)S(1)}, s16[83,8,128]{2,1,0:T(8,128)(2,1)}, u32[]{:S(2)}, u32[]{:S(2)}) collective-permute-start(s16[83,8,128]{2,1,0:T(8,128)(2,1)S(1)} %get-tuple-element.23), channel_id=1, source_target_pairs={{1,0},{2,1},{3,2},{4,3},{5,4},{6,5},{7,6},{0,7},{9,8},{10,9},{11,1... | collective-permute-start | bytes 509960 | tf_op jit(solution)/shard_map/ppermute | solution.py:489
  98.0 9.9 %collective-permute-start.7 = (s16[80,8,128]{2,1,0:T(8,128)(2,1)}, s16[80,8,128]{2,1,0:T(8,128)(2,1)}, u32[]{:S(2)}, u32[]{:S(2)}) collective-permute-start(s16[80,8,128]{2,1,0:T(8,128)(2,1)} %pad_add_fusion.1), channel_id=1, source_target_pairs={{1,0},{2,1},{3,2},{4,3},{5,4},{6,5},{7,6},{0,7},{9,8},{10,9},{11,1... | collective-permute-start | bytes 491528 | tf_op jit(solution)/shard_map/ppermute | solution.py:489
  98.8 11.4 %copy-start.1 = (f32[64,64,128]{2,1,0:T(8,128)S(1)}, f32[64,64,128]{2,1,0:T(8,128)}, u32[]{:S(2)}) copy-start(f32[64,64,128]{2,1,0:T(8,128)} %get-tuple-element.17.centre_ref) | copy-start | bytes 6291460
  110.3 10.7 %copy-start.2 = (f32[512,128]{1,0:T(8,128)S(1)}, f32[512,128]{1,0:T(8,128)}, u32[]{:S(2)}) copy-start(f32[512,128]{1,0:T(8,128)} %observed_ref.3) | copy-start | bytes 786436
  110.3 10.6 %copy-start.7 = (s32[1,512]{1,0:T(1,128)S(1)}, s32[1,512]{1,0:T(1,128)}, u32[]{:S(2)}) copy-start(s32[1,512]{1,0:T(1,128)} %get-tuple-element.14.slot_ref) | copy-start | bytes 6148
